TPU v7x, 256 devices: a whole 4x4x8 slice. The times are simulated.
256 devices in a mesh: qb: 32 (over y, z), kb: 8 (over x, core).
Axes of the slice: x: 4, y: 4, z: 8, core: 2. Of those that a mesh axis runs over, the one named last changes fastest.
Arguments:
- queries: bfloat16 [32, 8, 128, 128], P('qb', 'kb'), may hold values from -64 to 64
- keys: bfloat16 [8, 32, 128, 128], P('kb', 'qb'), may hold values from -6 to 6
- positions: int32 [32768], replicated, may hold values from 0 to 65534, as said below
- tile_mask: int32 [128, 128], P('qb', 'kb'), may hold values from 0 to 1, as said below
- w_query: bfloat16 [1, 128, 128], replicated, may hold values from -0.5 to 0.5
- w_key: bfloat16 [1, 128, 128], replicated, may hold values from -0.5 to 0.5
Outputs:
- row_loss: float32 [32, 8, 128], P('qb', 'kb')
- grad_query: float32 [1, 128, 128], replicated
- grad_key: float32 [1, 128, 128], replicated
Inputs may be any that keep to these rules, and one draw needn't show every extreme that they name: `positions`: strictly increasing along the sequence, first 0, last 65534. `tile_mask`: 1 on the diagonal, 0 above it.
All inputs are finite; a program needn't handle non-finite values.
Results may differ from a plain program's by a relative error of at most 0.022.
The roundings to bfloat16 on the way count: a program that leaves them out, or rounds other values in their place, can miss the bound.
Values may be sent and summed in bfloat16 or wider, within the bound.
No kernel may reach another device: no remote copies, remote signals or barrier semaphores. Data moves between devices by JAX's collectives and lax.ppermute only.
A program may use at most 64 MiB of HBM per device.

v0:
```python
import jax
import jax.numpy as jnp
from jax import lax
from jax.sharding import Mesh
from jax.sharding import PartitionSpec as P

KB = ("kb_0", "kb_1")
QB = ("qb_0", "qb_1")


NEGATIVE = -1e30


def copy_for_each(array, axis):
    copies = jnp.broadcast_to(array, (lax.axis_size(axis), *array.shape))
    return lax.all_to_all(copies, axis, split_axis=0, concat_axis=0, tiled=True)


def joined_along(parts, dim):
    dims = list(parts.shape[1:])
    dims[dim] *= parts.shape[0]
    return jnp.moveaxis(parts, 0, dim).reshape(dims)


def gather_directly(array, axis, dim):
    parts = copy_for_each(array, axis)
    return joined_along(parts, dim)


def all_in_one(array, axis):
    leaves = jax.tree.leaves(array)
    sequence = sorted(range(len(leaves)), key=lambda k: -leaves[k].size)
    width = (1, *leaves[sequence[0]].shape)[-1]
    lines = [
        jnp.pad(leaves[k].reshape(-1), (0, -leaves[k].size % width)).reshape(-1, width)
        for k in sequence
    ]
    both, at, found = (copy_for_each(jnp.concatenate(lines), axis), 0, {})
    for k, line in zip(sequence, lines):
        share = both[:, at : at + len(line)].reshape(len(both), -1)
        found[k] = share[:, : leaves[k].size].reshape(-1, *leaves[k].shape)
        at += len(line)
    numbers = iter(range(len(leaves)))
    return jax.tree.map(lambda _: found[next(numbers)], array)


def joined_by_halves(pieces, combine):
    while len(jax.tree.leaves(pieces)[0]) > 1:
        pieces = jax.vmap(combine)(
            *(jax.tree.map(lambda part: part[side::2], pieces) for side in (0, 1))
        )
    return jax.tree.map(lambda part: part[0], pieces)


def combined_all(array, axis, combine):
    pieces = all_in_one(array, axis)
    return joined_by_halves(pieces, combine)


def filled_up(lines, count):
    spare = -lines.shape[0] % count
    if not spare:
        return lines
    return jnp.concatenate([lines, jnp.zeros((spare, *lines.shape[1:]), lines.dtype)])


def gathered_by_axis(array, axes, dim):
    far, near = axes
    parts = copy_for_each(copy_for_each(array, far), near)
    return joined_along(parts.swapaxes(0, 1).reshape(-1, *array.shape), dim)


def in_blocks(array, dim, count):
    before, after = (array.shape[:dim], array.shape[dim + 1 :])
    return jnp.moveaxis(array.reshape(*before, count, -1, *after), dim, 0)


def sum_at_owner(array, axis, dim):
    parts = in_blocks(array, dim, lax.axis_size(axis))
    arrived = lax.all_to_all(parts, axis, split_axis=0, concat_axis=0, tiled=True)
    return arrived.sum(axis=0)


def sum_by_axis(array, axes, dim):
    far, near = axes
    parts = in_blocks(array, dim, lax.axis_size(far))
    nearer = sum_at_owner(parts, near, dim + 1)
    arrived = lax.all_to_all(nearer, far, split_axis=0, concat_axis=0, tiled=True)
    return arrived.sum(axis=0)


def nested_sum(array, axes):
    padded = filled_up(array, lax.axis_size(axes[0]) * lax.axis_size(axes[1]))
    whole = gathered_by_axis(sum_by_axis(padded, axes, 0), axes, 0)
    return lax.slice_in_dim(whole, 0, len(array)).reshape(array.shape)


def in_one(arrays, axis):
    flat, at, finished = (jnp.concatenate([a.reshape(-1) for a in arrays]), 0, [])
    total = nested_sum(flat, axis)
    for a in arrays:
        finished.append(total[at : at + a.size].reshape(a.shape))
        at += a.size
    return tuple(finished)


def rotate(inputs, positions, heads):
    row_count = inputs.shape[0]
    head_width = inputs.shape[1] // heads
    half_width = head_width // 2
    frequency = jnp.exp(
        jnp.arange(half_width, dtype=jnp.float32)
        * (-2.0 * jnp.log(jnp.float32(10000.0)) / head_width)
    )
    angles = positions.astype(jnp.float32)[:, None, None] * frequency[None, None, :]
    cosine = jnp.cos(angles)
    sine_vals = jnp.sin(angles)
    shaped = inputs.astype(jnp.float32).reshape(row_count, heads, 2, half_width)
    lower_half = shaped[:, :, 0]
    upper_half = shaped[:, :, 1]
    turned = jnp.stack(
        [
            lower_half * cosine - upper_half * sine_vals,
            upper_half * cosine + lower_half * sine_vals,
        ],
        axis=2,
    )
    return turned.reshape(row_count, heads * head_width).astype(jnp.bfloat16)


def feature_map(inputs, weight, heads):
    row_count = inputs.shape[0]
    head_width = weight.shape[1]
    mapped = jnp.einsum(
        "rhd,hde->rhe",
        inputs.reshape(row_count, heads, head_width),
        weight,
        preferred_element_type=jnp.float32,
    )
    return (jax.nn.softmax(mapped, axis=-1), jax.nn.softmax(-mapped, axis=-1))


def map_grad(inputs, upper_map, lower_map, dfeature, heads):
    half_width = upper_map.shape[-1]
    dfeat_up = dfeature[..., :half_width]
    dfeat_down = dfeature[..., half_width:]
    dmapped = upper_map * (
        dfeat_up - jnp.sum(upper_map * dfeat_up, -1, keepdims=True)
    ) - lower_map * (dfeat_down - jnp.sum(lower_map * dfeat_down, -1, keepdims=True))
    shaped = inputs.astype(jnp.float32).reshape(inputs.shape[0], heads, half_width)
    return jnp.einsum("rhd,rhe->hde", shaped, dmapped, precision=lax.Precision.HIGHEST)


def combine(earlier, later):
    row_top = jnp.maximum(earlier[0], later[0])
    left_factor = jnp.exp(earlier[0] - row_top)
    right_factor = jnp.exp(later[0] - row_top)
    return (
        row_top,
        earlier[1] * left_factor + later[1] * right_factor,
        earlier[2] * left_factor + later[2] * right_factor,
        earlier[3] + later[3],
    )


def local(queries, keys, positions, tile_mask, w_query, w_key):
    heads = w_query.shape[0]
    head_width = w_query.shape[1]
    piece_rows = queries.shape[2]
    kb_count = lax.axis_size(KB)
    qb_count = lax.axis_size(QB)
    qb_index = lax.axis_index(QB)
    kb_index = lax.axis_index(KB)
    query_tile = piece_rows * kb_count
    key_tile = piece_rows * qb_count
    seq_total = query_tile * qb_count
    query_start = (qb_index * kb_count + kb_index) * piece_rows
    key_start = (kb_index * qb_count + qb_index) * piece_rows
    own_query = rotate(
        queries.reshape(piece_rows, -1),
        lax.dynamic_slice_in_dim(positions, query_start, piece_rows),
        heads,
    )
    own_key = rotate(
        keys.reshape(piece_rows, -1),
        lax.dynamic_slice_in_dim(positions, key_start, piece_rows),
        heads,
    )
    query_rows = gather_directly(own_query[None], KB, 0).reshape(query_tile, -1)
    key_rows = gather_directly(own_key[None], QB, 0).reshape(key_tile, -1)
    mask_rows = tile_mask.shape[0]
    query_pos = lax.dynamic_slice_in_dim(positions, qb_index * query_tile, query_tile)
    key_pos = lax.dynamic_slice_in_dim(positions, kb_index * key_tile, key_tile)
    query_up, query_down = feature_map(query_rows, w_query, heads)
    key_up, key_down = feature_map(key_rows, w_key, heads)
    query_features_mapped = jnp.concatenate([query_up, query_down], -1).astype(jnp.bfloat16)
    key_features_mapped = jnp.concatenate([key_up, key_down], -1).astype(jnp.bfloat16)
    feat_width = query_features_mapped.shape[2]
    query_heads = query_rows.reshape(query_tile, heads, head_width)
    key_heads = key_rows.reshape(key_tile, heads, head_width)
    inv_root = 1.0 / jnp.sqrt(jnp.float32(head_width))
    mask_block = query_tile // mask_rows
    sub_total = key_tile // query_tile
    sub_indices = jnp.arange(sub_total, dtype=jnp.int32)

    def sub_mask(sub_index):
        return lax.dynamic_slice_in_dim(tile_mask, sub_index * mask_rows, mask_rows, 1)

    def sub_tile(sub_index):
        sub_start = sub_index * query_tile
        key_part = lax.dynamic_slice_in_dim(key_heads, sub_start, query_tile, 0)
        feature_slice = lax.dynamic_slice_in_dim(key_features_mapped, sub_start, query_tile, 0)
        pos_part = lax.dynamic_slice_in_dim(key_pos, sub_start, query_tile, 0)
        block_ok = jnp.broadcast_to(
            sub_mask(sub_index)[:, None, :, None] > 0,
            (mask_rows, mask_block, mask_rows, mask_block),
        ).reshape(query_tile, query_tile)
        allowed = (block_ok & (pos_part[None, :] <= query_pos[:, None]))[None]
        scores = (
            jnp.einsum("qhd,khd->hqk", query_heads, key_part, preferred_element_type=jnp.float32)
            * inv_root
        )
        student_probs = jnp.einsum(
            "buz,wuz->ubw", query_features_mapped, feature_slice, preferred_element_type=jnp.float32
        )
        return (allowed, scores, student_probs, feature_slice)

    stat_shape = (heads, query_tile)
    empty_stats = (
        jnp.full(stat_shape, NEGATIVE, jnp.float32),
        jnp.zeros(stat_shape, jnp.float32),
        jnp.zeros(stat_shape, jnp.float32),
        jnp.zeros(stat_shape, jnp.float32),
    )

    def tile_stats(sub_index):
        allowed, scores, student_probs, feature_slice = sub_tile(sub_index)
        row_top = jnp.max(jnp.where(allowed, scores, NEGATIVE), axis=2)
        weights = jnp.where(allowed, jnp.exp(scores - row_top[:, :, None]), 0.0)
        log_student = jnp.where(allowed, jnp.log(student_probs), 0.0)
        return (
            row_top,
            jnp.sum(weights, 2),
            jnp.sum(weights * log_student, 2),
            jnp.sum(jnp.where(allowed, student_probs, 0.0), 2),
        )

    def first_pass(running, sub_index):
        partial_value = tile_stats(sub_index)
        return (combine(running, partial_value), None)

    local_stats, unused = lax.scan(first_pass, empty_stats, sub_indices)
    row_top, row_total, log_sum, row_norm = combined_all(local_stats, KB, combine)
    row_loss = jnp.sum(jnp.log(row_norm) - log_sum / row_total, 0)
    own_loss = lax.dynamic_slice_in_dim(row_loss, kb_index * piece_rows, piece_rows).reshape(
        1, 1, piece_rows
    )
    zero_grads = (
        jnp.zeros((query_tile, heads, feat_width), jnp.float32),
        jnp.zeros((query_tile, heads, feat_width), jnp.float32),
    )

    def tile_grads(sub_index):
        allowed, scores, student_probs, feature_slice = sub_tile(sub_index)
        prob = (
            jnp.where(allowed, jnp.exp(scores - row_top[:, :, None]), 0.0) / row_total[:, :, None]
        )
        pairwise_gradient = (
            jnp.where(allowed, 1.0 / row_norm[:, :, None] - prob / student_probs, 0.0) / seq_total
        ).astype(jnp.bfloat16)
        query_gradient = jnp.einsum(
            "wes,swm->ewm", pairwise_gradient, feature_slice, preferred_element_type=jnp.float32
        )
        key_gradient = jnp.einsum(
            "lrx,rlv->xlv",
            pairwise_gradient,
            query_features_mapped,
            preferred_element_type=jnp.float32,
        )
        return (query_gradient, key_gradient)

    def second_pass(running, sub_index):
        query_gradient, key_gradient = tile_grads(sub_index)
        return (running + query_gradient, key_gradient)

    dquery_all, dkey_parts = lax.scan(second_pass, zero_grads[0], sub_indices)
    dkey_all = dkey_parts.reshape(key_tile, heads, feat_width)
    grad_query = map_grad(query_rows, query_up, query_down, dquery_all, heads)
    grad_key = map_grad(key_rows, key_up, key_down, dkey_all, heads)
    grad_query, grad_key = in_one((grad_query, grad_key), (("qb_0", "qb_1"), ("kb_0", "kb_1")))
    return (own_loss, grad_query, grad_key)


def solution(mesh):
    finer = Mesh(mesh.devices.reshape(4, 8, 4, 2), ("qb_0", "qb_1", "kb_0", "kb_1"))
    placed = (P(QB, KB, None, None), P(KB, QB, None, None), P(), P(QB, KB), P(), P())
    return jax.shard_map(
        local, mesh=finer, in_specs=placed, out_specs=(P(QB, KB, None), P(), P()), check_vma=False
    )
```

profile of v0, /device:TPU:1, one launch (start us, length us, event | category | flops | bytes accessed | tf_op | source)
XLA Modules:
  0.0 247.6 jit_solution(15625879538836151602)
XLA Ops:
  4.5 6.6 %all-to-all-start.1 = ((bf16[8,1,128,128]{3,2,1,0:T(8,128)(2,1)}), bf16[8,1,128,128]{3,2,1,0:T(8,128)(2,1)S(1)}, u32[]{:S(2)}, u32[]{:S(2)}) async-start(bf16[8,1,128,128]{3,2,1,0:T(8,128)(2,1)} %broadcast_in_dim.54), calls=%async_computation.1 | async-start | bytes 524288 | tf_op jit(solution)/shard_map/all_to_all | solution.py:16
  11.1 6.4 %all-to-all-done.1 = bf16[8,1,128,128]{3,2,1,0:T(8,128)(2,1)S(1)} async-done(((bf16[8,1,128,128]{3,2,1,0:T(8,128)(2,1)}), bf16[8,1,128,128]{3,2,1,0:T(8,128)(2,1)S(1)}, u32[]{:S(2)}, u32[]{:S(2)}) %all-to-all-start.1) | async-done | bytes 262176 | tf_op jit(solution)/shard_map/all_to_all | solution.py:16
  18.8 10.5 %all-to-all-start = ((bf16[32,1,128,128]{3,2,1,0:T(8,128)(2,1)}), bf16[32,1,128,128]{3,2,1,0:T(8,128)(2,1)}, u32[]{:S(2)}, u32[]{:S(2)}) async-start(bf16[32,1,128,128]{3,2,1,0:T(8,128)(2,1)} %broadcast_in_dim.45), calls=%async_computation | async-start | bytes 2097152 | tf_op jit(solution)/shard_map/all_to_all | solution.py:16
  33.8 20.6 %all-to-all-done = bf16[32,1,128,128]{3,2,1,0:T(8,128)(2,1)} async-done(((bf16[32,1,128,128]{3,2,1,0:T(8,128)(2,1)}), bf16[32,1,128,128]{3,2,1,0:T(8,128)(2,1)}, u32[]{:S(2)}, u32[]{:S(2)}) %all-to-all-start) | async-done | bytes 1048608 | tf_op jit(solution)/shard_map/all_to_all | solution.py:16
  60.8 37.2 %while.30 = (s32[]{:T(128)}, f32[1,1024]{1,0:T(1,128)S(1)}, f32[1,1024]{1,0:T(1,128)S(1)}, f32[1,1024]{1,0:T(1,128)S(1)}, f32[1,1024]{1,0:T(1,128)S(1)}, /*index...) while((s32[]{:T(128)}, f32[1,1024]{1,0:T(1,128)S(1)}, ...), condition=%wide.region_13.14_spmd.clone, body=%wide.region_8.13_spmd.clone.sunk | while | flops 822096896 | bytes 15319448 | solution.py:252
  66.2 3.9 %fusion.137 = (f32[1024]{0:T(1024)S(1)}, f32[1024]{0:T(1024)S(1)}, f32[1024]{0:T(1024)S(1)}) fusion(f32[1024,1024]{1,0:T(8,128)S(1)} %get-tuple-element.613, f32[1024]{0:T(1024)S(1)} %get-tuple-element.614, pred[1024,1024]{0,1:T(8,128)(4,1)S(1)} %bitcast.342, s32[1024]{0:T(1024)} %get-tuple-element.682, s32[1024]{0:T(1024)S(1)} %dynamic_slice.146, ...), kind=kOutput, calls=%fused_computation.4.clone.1 | convolution fusion | flops 548402176 | bytes 6316036 | tf_op jit(solution)/shard_map/while/body/eval_jaxpr/buz,wuz->ubw/dot_general | solution.py:223
  75.5 3.9 %fusion.137 = (f32[1024]{0:T(1024)S(1)}, f32[1024]{0:T(1024)S(1)}, f32[1024]{0:T(1024)S(1)}) fusion(f32[1024,1024]{1,0:T(8,128)S(1)} %get-tuple-element.613, f32[1024]{0:T(1024)S(1)} %get-tuple-element.614, pred[1024,1024]{0,1:T(8,128)(4,1)S(1)} %bitcast.342, s32[1024]{0:T(1024)} %get-tuple-element.682, s32[1024]{0:T(1024)S(1)} %dynamic_slice.146, ...), kind=kOutput, calls=%fused_computation.4.clone.1 | convolution fusion | flops 548402176 | bytes 6316036 | tf_op jit(solution)/shard_map/while/body/eval_jaxpr/buz,wuz->ubw/dot_general | solution.py:223
  84.8 3.9 %fusion.137 = (f32[1024]{0:T(1024)S(1)}, f32[1024]{0:T(1024)S(1)}, f32[1024]{0:T(1024)S(1)}) fusion(f32[1024,1024]{1,0:T(8,128)S(1)} %get-tuple-element.613, f32[1024]{0:T(1024)S(1)} %get-tuple-element.614, pred[1024,1024]{0,1:T(8,128)(4,1)S(1)} %bitcast.342, s32[1024]{0:T(1024)} %get-tuple-element.682, s32[1024]{0:T(1024)S(1)} %dynamic_slice.146, ...), kind=kOutput, calls=%fused_computation.4.clone.1 | convolution fusion | flops 548402176 | bytes 6316036 | tf_op jit(solution)/shard_map/while/body/eval_jaxpr/buz,wuz->ubw/dot_general | solution.py:223
  94.1 3.9 %fusion.137 = (f32[1024]{0:T(1024)S(1)}, f32[1024]{0:T(1024)S(1)}, f32[1024]{0:T(1024)S(1)}) fusion(f32[1024,1024]{1,0:T(8,128)S(1)} %get-tuple-element.613, f32[1024]{0:T(1024)S(1)} %get-tuple-element.614, pred[1024,1024]{0,1:T(8,128)(4,1)S(1)} %bitcast.342, s32[1024]{0:T(1024)} %get-tuple-element.682, s32[1024]{0:T(1024)S(1)} %dynamic_slice.146, ...), kind=kOutput, calls=%fused_computation.4.clone.1 | convolution fusion | flops 548402176 | bytes 6316036 | tf_op jit(solution)/shard_map/while/body/eval_jaxpr/buz,wuz->ubw/dot_general | solution.py:223
  98.8 7.8 %all-to-all-start.2 = ((f32[8,4,1024]{2,1,0:T(4,128)}), f32[8,4,1024]{2,1,0:T(4,128)S(1)}, u32[]{:S(2)}, u32[]{:S(2)}) async-start(f32[8,4,1024]{2,1,0:T(4,128)} %broadcast_in_dim.55), calls=%async_computation.2 | async-start | bytes 262144 | tf_op jit(solution)/shard_map/all_to_all | solution.py:16
  114.0 68.7 %while.31 = (s32[]{:T(128)}, f32[1024,1,256]{0,2,1:T(8,128)S(1)}, f32[4,1024,1,256]{3,1,2,0:T(8,128)}, s32[4]{0:T(128)}, bf16[4096,1,256]{2,0,1:T(8,128)(2,1)}, ...) while((s32[]{:T(128)}, f32[1024,1,256]{0,2,1:T(8,128)S(1)}, ...), condition=%wide.region_15.16_spmd.clone, body=%wide.region_14.15_spmd.clone.sunk | while | flops 1891107840 | bytes 24678824 | solution.py:286
  116.0 3.6 %fusion.148 = f32[1024,1024]{1,0:T(8,128)} fusion(bf16[1024,1,128]{2,0,1:T(8,128)(2,1)S(1)} %get-tuple-element.743, bf16[4096,1,128]{2,0,1:T(8,128)(2,1)} %get-tuple-element.742, s32[]{:T(128)S(6)} %select_n.113), kind=kOutput, calls=%fused_computation.52.clone.1 | convolution fusion | flops 268435456 | bytes 4718596 | tf_op jit(solution)/shard_map/while/body/eval_jaxpr/qhd,khd->hqk/dot_general | solution.py:220
  121.5 5.0 %fusion.149 = bf16[1024,1024]{0,1:T(8,128)(2,1)S(1)} fusion(f32[1024,1024]{1,0:T(8,128)} %fusion.148, pred[1024,1024]{0,1:T(8,128)(4,1)S(1)} %bitcast.343, f32[1024]{0:T(1024)S(1)} %bitcast.361, f32[1024]{0:T(1024)} %bitcast.337, f32[1024]{0:T(1024)S(1)} %bitcast.358, s32[1024]{0:T(1024)} %get-tuple-element.740, s32[1024]{0:T(1024)S(1)} %dynamic_slice.152, ...), kind=kOutput, calls=%fused_computation.41.clone.1 | convolution fusion | flops 548405248 | bytes 8409092 | tf_op jit(solution)/shard_map/while/body/eval_jaxpr/buz,wuz->ubw/dot_general | solution.py:223
  128.4 2.8 %fusion.151 = f32[4,1024,1,256]{3,1,2,0:T(8,128)} fusion(f32[4,1024,1,256]{3,1,2,0:T(8,128)} %get-tuple-element.715, s32[]{:T(128)S(6)} %copy.102, bf16[1024,1024]{0,1:T(8,128)(2,1)S(1)} %fusion.149, bf16[1024,1,256]{2,0,1:T(8,128)(2,1)} %get-tuple-element.746), kind=kOutput, calls=%fused_computation.43.clone.1 | convolution fusion | flops 536870912 | bytes 3670020 | tf_op jit(solution)/shard_map/while/body/eval_jaxpr/lrx,rlv->xlv/dot_general | solution.py:274
  133.2 3.6 %fusion.148 = f32[1024,1024]{1,0:T(8,128)} fusion(bf16[1024,1,128]{2,0,1:T(8,128)(2,1)S(1)} %get-tuple-element.743, bf16[4096,1,128]{2,0,1:T(8,128)(2,1)} %get-tuple-element.742, s32[]{:T(128)S(6)} %select_n.113), kind=kOutput, calls=%fused_computation.52.clone.1 | convolution fusion | flops 268435456 | bytes 4718596 | tf_op jit(solution)/shard_map/while/body/eval_jaxpr/qhd,khd->hqk/dot_general | solution.py:220
  138.7 5.0 %fusion.149 = bf16[1024,1024]{0,1:T(8,128)(2,1)S(1)} fusion(f32[1024,1024]{1,0:T(8,128)} %fusion.148, pred[1024,1024]{0,1:T(8,128)(4,1)S(1)} %bitcast.343, f32[1024]{0:T(1024)S(1)} %bitcast.361, f32[1024]{0:T(1024)} %bitcast.337, f32[1024]{0:T(1024)S(1)} %bitcast.358, s32[1024]{0:T(1024)} %get-tuple-element.740, s32[1024]{0:T(1024)S(1)} %dynamic_slice.152, ...), kind=kOutput, calls=%fused_computation.41.clone.1 | convolution fusion | flops 548405248 | bytes 8409092 | tf_op jit(solution)/shard_map/while/body/eval_jaxpr/buz,wuz->ubw/dot_general | solution.py:223
  145.6 2.8 %fusion.151 = f32[4,1024,1,256]{3,1,2,0:T(8,128)} fusion(f32[4,1024,1,256]{3,1,2,0:T(8,128)} %get-tuple-element.715, s32[]{:T(128)S(6)} %copy.102, bf16[1024,1024]{0,1:T(8,128)(2,1)S(1)} %fusion.149, bf16[1024,1,256]{2,0,1:T(8,128)(2,1)} %get-tuple-element.746), kind=kOutput, calls=%fused_computation.43.clone.1 | convolution fusion | flops 536870912 | bytes 3670020 | tf_op jit(solution)/shard_map/while/body/eval_jaxpr/lrx,rlv->xlv/dot_general | solution.py:274
  150.4 3.6 %fusion.148 = f32[1024,1024]{1,0:T(8,128)} fusion(bf16[1024,1,128]{2,0,1:T(8,128)(2,1)S(1)} %get-tuple-element.743, bf16[4096,1,128]{2,0,1:T(8,128)(2,1)} %get-tuple-element.742, s32[]{:T(128)S(6)} %select_n.113), kind=kOutput, calls=%fused_computation.52.clone.1 | convolution fusion | flops 268435456 | bytes 4718596 | tf_op jit(solution)/shard_map/while/body/eval_jaxpr/qhd,khd->hqk/dot_general | solution.py:220
  155.9 5.0 %fusion.149 = bf16[1024,1024]{0,1:T(8,128)(2,1)S(1)} fusion(f32[1024,1024]{1,0:T(8,128)} %fusion.148, pred[1024,1024]{0,1:T(8,128)(4,1)S(1)} %bitcast.343, f32[1024]{0:T(1024)S(1)} %bitcast.361, f32[1024]{0:T(1024)} %bitcast.337, f32[1024]{0:T(1024)S(1)} %bitcast.358, s32[1024]{0:T(1024)} %get-tuple-element.740, s32[1024]{0:T(1024)S(1)} %dynamic_slice.152, ...), kind=kOutput, calls=%fused_computation.41.clone.1 | convolution fusion | flops 548405248 | bytes 8409092 | tf_op jit(solution)/shard_map/while/body/eval_jaxpr/buz,wuz->ubw/dot_general | solution.py:223
  162.8 2.7 %fusion.151 = f32[4,1024,1,256]{3,1,2,0:T(8,128)} fusion(f32[4,1024,1,256]{3,1,2,0:T(8,128)} %get-tuple-element.715, s32[]{:T(128)S(6)} %copy.102, bf16[1024,1024]{0,1:T(8,128)(2,1)S(1)} %fusion.149, bf16[1024,1,256]{2,0,1:T(8,128)(2,1)} %get-tuple-element.746), kind=kOutput, calls=%fused_computation.43.clone.1 | convolution fusion | flops 536870912 | bytes 3670020 | tf_op jit(solution)/shard_map/while/body/eval_jaxpr/lrx,rlv->xlv/dot_general | solution.py:274
  167.5 3.6 %fusion.148 = f32[1024,1024]{1,0:T(8,128)} fusion(bf16[1024,1,128]{2,0,1:T(8,128)(2,1)S(1)} %get-tuple-element.743, bf16[4096,1,128]{2,0,1:T(8,128)(2,1)} %get-tuple-element.742, s32[]{:T(128)S(6)} %select_n.113), kind=kOutput, calls=%fused_computation.52.clone.1 | convolution fusion | flops 268435456 | bytes 4718596 | tf_op jit(solution)/shard_map/while/body/eval_jaxpr/qhd,khd->hqk/dot_general | solution.py:220
  173.1 5.0 %fusion.149 = bf16[1024,1024]{0,1:T(8,128)(2,1)S(1)} fusion(f32[1024,1024]{1,0:T(8,128)} %fusion.148, pred[1024,1024]{0,1:T(8,128)(4,1)S(1)} %bitcast.343, f32[1024]{0:T(1024)S(1)} %bitcast.361, f32[1024]{0:T(1024)} %bitcast.337, f32[1024]{0:T(1024)S(1)} %bitcast.358, s32[1024]{0:T(1024)} %get-tuple-element.740, s32[1024]{0:T(1024)S(1)} %dynamic_slice.152, ...), kind=kOutput, calls=%fused_computation.41.clone.1 | convolution fusion | flops 548405248 | bytes 8409092 | tf_op jit(solution)/shard_map/while/body/eval_jaxpr/buz,wuz->ubw/dot_general | solution.py:223
  179.9 2.7 %fusion.151 = f32[4,1024,1,256]{3,1,2,0:T(8,128)} fusion(f32[4,1024,1,256]{3,1,2,0:T(8,128)} %get-tuple-element.715, s32[]{:T(128)S(6)} %copy.102, bf16[1024,1024]{0,1:T(8,128)(2,1)S(1)} %fusion.149, bf16[1024,1,256]{2,0,1:T(8,128)(2,1)} %get-tuple-element.746), kind=kOutput, calls=%fused_computation.43.clone.1 | convolution fusion | flops 536870912 | bytes 3670020 | tf_op jit(solution)/shard_map/while/body/eval_jaxpr/lrx,rlv->xlv/dot_general | solution.py:274
  182.7 3.8 %fusion.111 = (f32[4096,1,128]{2,0,1:T(8,128)}, f32[4096,1,128]{2,0,1:T(8,128)S(1)}) fusion(f32[4096,1,256]{2,0,1:T(8,128)} %bitcast.347), kind=kLoop, calls=%fused_computation.180 | loop fusion | bytes 8388608 | tf_op jit(solution)/shard_map/slice | solution.py:145
  188.3 3.1 %copy.73 = f32[4096,1,128]{0,2,1:T(8,128)} copy(f32[4096,1,128]{2,0,1:T(8,128)} %get-tuple-element.426) | data formatting | bytes 4194304
  192.7 3.3 %fusion.49 = (f32[4096]{0:T(1024)S(1)}, f32[4096]{0:T(1024)S(1)}) fusion(f32[4096,1,128]{0,2,1:T(8,128)} %copy.73, f32[4096]{0:T(1024)S(1)} %get-tuple-element.352, f32[4096]{0:T(1024)S(1)} %get-tuple-element.448, f32[4096,128]{0,1:T(8,128)S(1)} %copy-done.2, f32[4096,1,128]{0,2,1:T(8,128)} %copy.74, f32[4096]{0:T(1024)S(1)} %get-tuple-element.353, ...), kind=kLoop, calls=%fused_computation.75 | loop fusion | flops 4710400 | bytes 6389760 | tf_op jit(solution)/shard_map/reduce_sum | solution.py:148
  199.4 8.5 %all_to_all.43 = f32[8,32,128]{2,1,0:T(8,128)S(1)} all-to-all(f32[8,32,128]{2,1,0:T(8,128)S(1)} %copy.66), channel_id=1, replica_groups=mesh['qb_0'=4,'qb_1'=8,'kb_0'=4,'kb_1'=2] {'kb_0','kb_1'}, dimensions={0} | all-to-all | bytes 262144 | tf_op jit(solution)/shard_map/all_to_all | solution.py:80
  207.9 13.2 %all_to_all.44 = f32[32,1,128]{2,1,0:T(1,128)S(1)} all-to-all(f32[32,1,128]{2,1,0:T(1,128)S(1)} %bitcast.360), channel_id=1, replica_groups=mesh['qb_0'=4,'qb_1'=8,'kb_0'=4,'kb_1'=2] {'qb_0','qb_1'}, dimensions={0} | all-to-all | bytes 32768 | tf_op jit(solution)/shard_map/all_to_all | solution.py:88
  221.8 3.8 %all-to-all-start.5 = ((f32[32,1,128]{2,1,0:T(1,128)}), f32[32,1,128]{2,1,0:T(1,128)S(1)}, u32[]{:S(2)}, u32[]{:S(2)}) async-start(f32[32,1,128]{2,1,0:T(1,128)} %broadcast_in_dim.58), calls=%async_computation.5 | async-start | bytes 32768 | tf_op jit(solution)/shard_map/all_to_all | solution.py:16
  225.6 8.6 %all-to-all-done.5 = f32[32,1,128]{2,1,0:T(1,128)S(1)} async-done(((f32[32,1,128]{2,1,0:T(1,128)}), f32[32,1,128]{2,1,0:T(1,128)S(1)}, u32[]{:S(2)}, u32[]{:S(2)}) %all-to-all-start.5) | async-done | bytes 16416 | tf_op jit(solution)/shard_map/all_to_all | solution.py:16
  234.8 6.7 %all-to-all-start.6 = ((f32[8,32,128]{2,1,0:T(8,128)}), f32[8,32,128]{2,1,0:T(8,128)S(1)}, u32[]{:S(2)}, u32[]{:S(2)}) async-start(f32[8,32,128]{2,1,0:T(8,128)} %broadcast_in_dim.59), calls=%async_computation.6 | async-start | bytes 262144 | tf_op jit(solution)/shard_map/all_to_all | solution.py:16
  242.8 4.1 %all-to-all-done.6 = f32[8,32,128]{2,1,0:T(8,128)S(1)} async-done(((f32[8,32,128]{2,1,0:T(8,128)}), f32[8,32,128]{2,1,0:T(8,128)S(1)}, u32[]{:S(2)}, u32[]{:S(2)}) %all-to-all-start.6) | async-done | bytes 131104 | tf_op jit(solution)/shard_map/all_to_all | solution.py:16
  (151 shorter events, 67.3 us)
Async XLA Ops:
  0.6 53.8 %copy-start = (bf16[1,128,128]{2,1,0:T(8,128)(2,1)S(1)}, bf16[1,128,128]{2,1,0:T(8,128)(2,1)}, u32[]{:S(2)}) copy-start(bf16[1,128,128]{2,1,0:T(8,128)(2,1)} %param.15) | copy-start | bytes 98308
  3.6 25.7 %copy-start.11 = (s32[4,16]{1,0:T(4,128)S(1)}, s32[4,16]{1,0:T(4,128)}, u32[]{:S(2)}) copy-start(s32[4,16]{1,0:T(4,128)} %param.13) | copy-start | bytes 772
  3.6 27.8 %copy-start.9 = (bf16[1,128,128]{2,1,0:T(8,128)(2,1)S(1)}, bf16[1,128,128]{2,1,0:T(8,128)(2,1)}, u32[]{:S(2)}) copy-start(bf16[1,128,128]{2,1,0:T(8,128)(2,1)} %param.14) | copy-start | bytes 98308
  4.5 13.1 %all-to-all-start.1 = ((bf16[8,1,128,128]{3,2,1,0:T(8,128)(2,1)}), bf16[8,1,128,128]{3,2,1,0:T(8,128)(2,1)S(1)}, u32[]{:S(2)}, u32[]{:S(2)}) async-start(bf16[8,1,128,128]{3,2,1,0:T(8,128)(2,1)} %broadcast_in_dim.54), calls=%async_computation.1 | async-start | bytes 524288 | tf_op jit(solution)/shard_map/all_to_all | solution.py:16
  18.8 35.7 %all-to-all-start = ((bf16[32,1,128,128]{3,2,1,0:T(8,128)(2,1)}), bf16[32,1,128,128]{3,2,1,0:T(8,128)(2,1)}, u32[]{:S(2)}, u32[]{:S(2)}) async-start(bf16[32,1,128,128]{3,2,1,0:T(8,128)(2,1)} %broadcast_in_dim.45), calls=%async_computation | async-start | bytes 2097152 | tf_op jit(solution)/shard_map/all_to_all | solution.py:16
  31.7 0.8 copy-start.3
  56.1 1.4 copy-start.1
  98.8 13.1 %all-to-all-start.2 = ((f32[8,4,1024]{2,1,0:T(4,128)}), f32[8,4,1024]{2,1,0:T(4,128)S(1)}, u32[]{:S(2)}, u32[]{:S(2)}) async-start(f32[8,4,1024]{2,1,0:T(4,128)} %broadcast_in_dim.55), calls=%async_computation.2 | async-start | bytes 262144 | tf_op jit(solution)/shard_map/all_to_all | solution.py:16
  188.3 4.4 %copy-start.2 = (f32[4096,128]{0,1:T(8,128)S(1)}, f32[4096,128]{0,1:T(8,128)}, u32[]{:S(2)}) copy-start(f32[4096,128]{0,1:T(8,128)} %copy-done.1) | copy-start | bytes 6291460
  192.7 3.4 %copy-start.5 = (f32[4096,1,128]{0,2,1:T(8,128)S(1)}, f32[4096,1,128]{0,2,1:T(8,128)}, u32[]{:S(2)}) copy-start(f32[4096,1,128]{0,2,1:T(8,128)} %copy.74) | copy-start | bytes 6291460
  192.7 3.5 %copy-start.6 = (f32[4096,1,128]{0,2,1:T(8,128)S(1)}, f32[4096,1,128]{0,2,1:T(8,128)}, u32[]{:S(2)}) copy-start(f32[4096,1,128]{0,2,1:T(8,128)} %copy.73) | copy-start | bytes 6291460
  192.7 3.7 %copy-start.7 = (bf16[4096,128]{0,1:T(8,128)(2,1)S(1)}, bf16[4096,128]{0,1:T(8,128)(2,1)}, u32[]{:S(2)}) copy-start(bf16[4096,128]{0,1:T(8,128)(2,1)} %copy.63) | copy-start | bytes 3145732
  196.5 2.2 copy-start.4
  196.5 2.2 copy-start.8
  198.7 42.9 %copy-start.10 = (f32[2,1,1024]{2,1,0:T(1,128)S(1)}, f32[2,1,1024]{2,1,0:T(1,128)}, u32[]{:S(2)}) copy-start(f32[2,1,1024]{2,1,0:T(1,128)} %get-tuple-element.414) | copy-start | bytes 24580
  221.8 12.4 %all-to-all-start.5 = ((f32[32,1,128]{2,1,0:T(1,128)}), f32[32,1,128]{2,1,0:T(1,128)S(1)}, u32[]{:S(2)}, u32[]{:S(2)}) async-start(f32[32,1,128]{2,1,0:T(1,128)} %broadcast_in_dim.58), calls=%async_computation.5 | async-start | bytes 32768 | tf_op jit(solution)/shard_map/all_to_all | solution.py:16
  234.8 12.0 %all-to-all-start.6 = ((f32[8,32,128]{2,1,0:T(8,128)}), f32[8,32,128]{2,1,0:T(8,128)S(1)}, u32[]{:S(2)}, u32[]{:S(2)}) async-start(f32[8,32,128]{2,1,0:T(8,128)} %broadcast_in_dim.59), calls=%async_computation.6 | async-start | bytes 262144 | tf_op jit(solution)/shard_map/all_to_all | solution.py:16
where the time goes:
time: 249 us; the launch traced here: 248 us
  matrix products  82.3 us (33%)
  local copies, waits for them, and re-layouts  43.1 us (17%)
  waiting for transfers between devices  41.8 us (17%)
  starting transfers between devices  35.5 us (14%)
  blocking collectives  21.6 us (9%)
  loops' own time  11.2 us (4%)
  other arithmetic  11 us (4%)
    all_to_all x5, waiting for transfers between devices, copy_for_each(): return lax.all_to_all(copies, axis, split_axis=0, concat_axis=0, tiled=True)  41.8 us
    all_to_all x5, starting transfers between devices, copy_for_each(): return lax.all_to_all(copies, axis, split_axis=0, concat_axis=0, tiled=True)  35.5 us
    dot_general x8, matrix products, sub_tile(): jnp.einsum('buz,wuz->ubw', query_features_mapped, feature_slice, preferre...  35.5 us
    dot_general x8, matrix products, sub_tile(): jnp.einsum('qhd,khd->hqk', query_heads, key_part, preferred_element_type=...  23.4 us
    all_to_all x1, blocking collectives, sum_by_axis(): lax.all_to_all(nearer, far, split_axis=0, concat_axis=0, tiled=True)  13.2 us
    unnamed x31, local copies, waits for them, and re-layouts  11.7 us
    dot_general x4, matrix products, tile_grads(): jnp.einsum('lrx,rlv->xlv', pairwise_gradient, query_features_mapped, pref...  11 us
    all_to_all x1, blocking collectives, sum_at_owner(): lax.all_to_all(parts, axis, split_axis=0, concat_axis=0, tiled=True)  8.48 us
  transfers between devices with their start and end apart: 5, of which 5 were waited for; matrix products, arithmetic and copies ran while one was open for 3% of the time, Pallas kernels for 0%

commit v1 on v0

v1 whole, which is shorter than its diff:
```python
import functools

import jax
import jax.numpy as jnp
from jax import lax
from jax.experimental import pallas as pl
from jax.experimental.pallas import tpu as pltpu
from jax.sharding import Mesh
from jax.sharding import PartitionSpec as P

LOW = -1e30
LOG2E = 1.4426950408889634
LN2 = 0.6931471805599453
TILE = 256
HEAD = 128
FEAT = 256
SLOTS = 40


def rotate(inputs, positions):
    half_width = inputs.shape[1] // 2
    frequency = jnp.exp(
        jnp.arange(half_width, dtype=jnp.float32)
        * (-2.0 * jnp.log(jnp.float32(10000.0)) / inputs.shape[1])
    )
    angles = positions.astype(jnp.float32)[:, None] * frequency[None, :]
    cosine = jnp.cos(angles)
    sine = jnp.sin(angles)
    values = inputs.astype(jnp.float32)
    lower, upper = values[:, :half_width], values[:, half_width:]
    return jnp.concatenate(
        [lower * cosine - upper * sine, upper * cosine + lower * sine], axis=1
    ).astype(jnp.bfloat16)


def send_copies(array, axes):
    copies = jnp.broadcast_to(array, (lax.axis_size(axes), *array.shape))
    return lax.all_to_all(copies, axes, split_axis=0, concat_axis=0, tiled=True)


def nn(a, b):
    return lax.dot_general(a, b, (((1,), (0,)), ((), ())), preferred_element_type=jnp.float32)


def nt(a, b):
    return lax.dot_general(a, b, (((1,), (1,)), ((), ())), preferred_element_type=jnp.float32)


def rows_of(q_ref, stripe):
    return jnp.concatenate([q_ref[2 * stripe, :HEAD], q_ref[2 * stripe + 1, :HEAD]], axis=0)


def features(weight_t, rows):
    mapped = nt(weight_t, rows)
    up = jnp.exp(mapped - jnp.max(mapped, 0, keepdims=True))
    down = jnp.exp(jnp.min(mapped, 0, keepdims=True) - mapped)
    up = up * (1.0 / jnp.sum(up, 0, keepdims=True))
    down = down * (1.0 / jnp.sum(down, 0, keepdims=True))
    return jnp.concatenate([up, down], axis=0)


def turned(a):
    return jnp.transpose(a.astype(jnp.float32)).astype(jnp.bfloat16)


def slot_of(band, stripe, sub):
    return (band * 4 - (band * (band - 1)) // 2 + stripe - band) * 4 + sub


def not_after():
    shape = (TILE, TILE)
    return lax.broadcasted_iota(jnp.int32, shape, 0) <= lax.broadcasted_iota(jnp.int32, shape, 1)


def for_tiles(where, mask, chunk, sub, body):
    x, y, z, c = where[0], where[1], where[2], where[3]
    band = (x - chunk + 4) % 4
    key_tile = band * 32 + c * 16 + y * 4 + sub

    def step(stripe, carry):
        row_tile = stripe * 32 + z * 4 + x
        live = mask[chunk * 16 + stripe * 4 + sub] > 0
        slot = slot_of(band, stripe, sub)

        @pl.when(live & (key_tile < row_tile))
        def _():
            body(stripe, slot, False)

        @pl.when(live & (key_tile == row_tile))
        def _():
            body(stripe, slot, True)

        return carry

    lax.fori_loop(0, 4, step, 0)


def first_kernel(
    where, mask, q_ref, k0, k1, k2, k3, wq_ref, wk_ref,
    stats_ref, top_ref, r_ref, kfeat_ref, qfeat_ref,
    q_turned, qf_low, run, kf_ref,
):
    scale = LOG2E * HEAD**-0.5
    wq_t = turned(wq_ref[...])
    wk_t = turned(wk_ref[...])
    for stripe in range(4):
        rows = rows_of(q_ref, stripe)
        q_turned[stripe] = turned(rows)
        feat = features(wq_t, rows)
        qfeat_ref[stripe] = feat
        qf_low[stripe] = feat.astype(jnp.bfloat16)
    run[0] = jnp.full((4, 8, TILE), LOW, jnp.float32)
    run[1] = jnp.zeros((4, 8, TILE), jnp.float32)
    run[2] = jnp.zeros((4, 8, TILE), jnp.float32)
    run[3] = jnp.zeros((4, 8, TILE), jnp.float32)

    def chunk_tiles(chunk, k_ref):
        def key_step(sub, carry):
            keys = k_ref[pl.ds(pl.multiple_of(sub * TILE, TILE), TILE), :]
            feat = features(wk_t, keys)
            kfeat_ref[chunk * 4 + sub] = feat
            kf_ref[...] = jnp.transpose(feat).astype(jnp.bfloat16)

            def body(stripe, slot, corner):
                raw = nn(keys, q_turned[stripe])
                student = nn(kf_ref[...], qf_low[stripe])
                if corner:
                    ok = not_after()
                    raw = jnp.where(ok, raw, LOW)
                    counted = jnp.where(ok, student, 0.0)
                    student = jnp.where(ok, student, 1.0)
                else:
                    counted = student
                fold = lambda a: a.reshape(TILE // 8, 8, TILE)
                top = jnp.max(jnp.max(fold(raw), 0), 0, keepdims=True) * scale
                t = raw * scale - top
                weight = jnp.exp2(t)
                log_student = jnp.log2(student)
                r_ref[slot] = jnp.exp2(t - log_student)
                total = jnp.sum(fold(weight), 0)
                logs = jnp.sum(fold(weight * log_student), 0)
                norm = jnp.sum(fold(counted), 0)
                top = jnp.broadcast_to(top, (8, TILE))
                top_ref[slot] = top
                old = run[0, stripe]
                new = jnp.maximum(old, top)
                left = jnp.exp2(old - new)
                right = jnp.exp2(top - new)
                run[0, stripe] = new
                run[1, stripe] = run[1, stripe] * left + total * right
                run[2, stripe] = run[2, stripe] * left + logs * right
                run[3, stripe] = run[3, stripe] + norm

            for_tiles(where, mask, chunk, sub, body)
            return carry

        lax.fori_loop(0, 4, key_step, 0)

    for chunk, k_ref in enumerate((k0, k1, k2, k3)):
        chunk_tiles(chunk, k_ref)
    for stripe in range(4):
        lines = [run[0, stripe][:1]] + [
            jnp.sum(run[n, stripe], 0, keepdims=True) for n in (1, 2, 3)
        ]
        for n, line in enumerate(lines):
            for copy in range(8):
                stats_ref[copy, pl.ds(n * 4 + stripe, 1), :] = line


def split3(a):
    high = a.astype(jnp.bfloat16)
    rest = a - high.astype(jnp.float32)
    middle = rest.astype(jnp.bfloat16)
    low = (rest - middle.astype(jnp.float32)).astype(jnp.bfloat16)
    return jnp.concatenate([high, middle, low], axis=0)


def weight_grad(feat, dfeat, rows):
    up, down = feat[:HEAD], feat[HEAD:]
    d1, d2 = dfeat[:HEAD], dfeat[HEAD:]
    dmapped = up * (d1 - jnp.sum(up * d1, 0, keepdims=True)) - down * (
        d2 - jnp.sum(down * d2, 0, keepdims=True)
    )
    parts = nn(split3(dmapped), rows)
    return (parts[2 * HEAD :] + parts[HEAD : 2 * HEAD]) + parts[:HEAD]


def second_kernel(
    where, mask, st_ref, q_ref, k0, k1, k2, k3, top_ref, r_ref, kfeat_ref, qfeat_ref,
    loss_ref, grad_ref,
    lines, losses, qf_low, dq_ref, dk_ref, gq_ref, gk_ref,
):
    top = st_ref[0, 0:4]
    for n in range(1, 8):
        top = jnp.maximum(top, st_ref[n, 0:4])
    total = jnp.zeros_like(top)
    logs = jnp.zeros_like(top)
    norm = jnp.zeros_like(top)
    for n in range(8):
        factor = jnp.exp2(st_ref[n, 0:4] - top)
        total = total + st_ref[n, 4:8] * factor
        logs = logs + st_ref[n, 8:12] * factor
        norm = norm + st_ref[n, 12:16]
    loss = jnp.log(norm) - (logs / total) * LN2
    for stripe in range(4):
        for half in range(2):
            losses[half, stripe] = jnp.broadcast_to(
                loss[stripe : stripe + 1, half * 128 : half * 128 + 128], (8, 128)
            )
    loss_ref[...] = losses[where[3], where[1]][:1]
    base = (1.0 / norm) * (1.0 / 32768.0)
    shift = top + jnp.log2(total) + 15.0
    for stripe in range(4):
        lines[0, stripe] = jnp.broadcast_to(base[stripe : stripe + 1], (8, TILE))
        lines[1, stripe] = jnp.broadcast_to(shift[stripe : stripe + 1], (8, TILE))
        qf_low[stripe] = qfeat_ref[stripe].astype(jnp.bfloat16)
    dq_ref[...] = jnp.zeros_like(dq_ref)
    gk_ref[...] = jnp.zeros_like(gk_ref)

    def chunk_tiles(chunk, k_ref):
        def key_step(sub, carry):
            feat = kfeat_ref[chunk * 4 + sub]
            kf_t = feat.astype(jnp.bfloat16)
            dk_ref[...] = jnp.zeros_like(dk_ref)

            def body(stripe, slot, corner):
                factor = jnp.exp2(top_ref[slot] - lines[1, stripe])
                r = r_ref[slot].reshape(TILE // 8, 8, TILE)
                grad = (lines[0, stripe][None] - r * factor[None]).reshape(TILE, TILE)
                if corner:
                    grad = jnp.where(not_after(), grad, 0.0)
                grad = grad.astype(jnp.bfloat16)
                dq_ref[stripe] += nn(kf_t, grad)
                dk_ref[...] += nt(qf_low[stripe], grad)

            for_tiles(where, mask, chunk, sub, body)
            keys = k_ref[pl.ds(pl.multiple_of(sub * TILE, TILE), TILE), :]
            gk_ref[...] += weight_grad(feat, dk_ref[...], keys)
            return carry

        lax.fori_loop(0, 4, key_step, 0)

    for chunk, k_ref in enumerate((k0, k1, k2, k3)):
        chunk_tiles(chunk, k_ref)
    gq = jnp.zeros((HEAD, HEAD), jnp.float32)
    for stripe in range(4):
        gq = gq + weight_grad(qfeat_ref[stripe], dq_ref[stripe], rows_of(q_ref, stripe))
    grad_ref[0] = jnp.transpose(gq)
    grad_ref[1] = jnp.transpose(gk_ref[...])


def f32(*shape):
    return jax.ShapeDtypeStruct(shape, jnp.float32)


def local(queries, keys, positions, tile_mask, w_query, w_key):
    x, y, z, c = (lax.axis_index(name) for name in ("x", "y", "z", "c"))
    piece = queries.shape[2]
    query_start = ((y * 8 + z) * 8 + x * 2 + c) * piece
    key_start = ((x * 2 + c) * 32 + y * 8 + z) * piece
    own_query = rotate(
        queries.reshape(piece, HEAD), lax.dynamic_slice_in_dim(positions, query_start, piece)
    )
    own_key = rotate(
        keys.reshape(piece, HEAD), lax.dynamic_slice_in_dim(positions, key_start, piece)
    )
    marks = jnp.pad(tile_mask.reshape(1, 64).astype(jnp.bfloat16), ((0, 15), (0, 64)))
    q_all = send_copies(jnp.concatenate([own_query, marks], 0), ("y", "c"))
    k_near = send_copies(own_key, "z").reshape(1024, HEAD)
    marks = jnp.pad(q_all[:, piece], ((0, 8), (0, 0)))
    load = jnp.concatenate([k_near, marks], 0)
    chunks = [load] + [
        lax.ppermute(load, "x", [(i, (i + step) % 4) for i in range(4)]) for step in (1, 2, 3)
    ]
    own = jnp.stack([chunk[1024:1032, :64] for chunk in chunks]).reshape(4, 4, 2, 4, 4, 4)
    own = lax.dynamic_slice(own, (0, 0, c, x, y, 0), (4, 4, 1, 1, 1, 4))
    mask = own.reshape(64).astype(jnp.int32)
    where = jnp.stack([x, y, z, c]).astype(jnp.int32)
    vmem = pl.BlockSpec(memory_space=pltpu.VMEM)
    smem = pl.BlockSpec(memory_space=pltpu.SMEM)
    stats, tops, r, kfeat, qfeat = pl.pallas_call(
        first_kernel,
        out_shape=(
            f32(8, 16, TILE),
            f32(SLOTS, 8, TILE),
            f32(SLOTS, TILE, TILE),
            f32(16, FEAT, TILE),
            f32(4, FEAT, TILE),
        ),
        in_specs=[smem, smem] + [vmem] * 7,
        out_specs=(vmem,) * 5,
        scratch_shapes=[
            pltpu.VMEM((4, HEAD, TILE), jnp.bfloat16),
            pltpu.VMEM((4, FEAT, TILE), jnp.bfloat16),
            pltpu.VMEM((4, 4, 8, TILE), jnp.float32),
            pltpu.VMEM((TILE, FEAT), jnp.bfloat16),
        ],
        name="first",
    )(where, mask, q_all, *chunks, w_query[0], w_key[0])
    stats = lax.all_to_all(stats, ("y", "c"), split_axis=0, concat_axis=0, tiled=True)
    loss, grads = pl.pallas_call(
        second_kernel,
        out_shape=(f32(1, piece), f32(2, HEAD, HEAD)),
        in_specs=[smem, smem] + [vmem] * 10,
        out_specs=(vmem,) * 2,
        scratch_shapes=[
            pltpu.VMEM((2, 4, 8, TILE), jnp.float32),
            pltpu.VMEM((2, 4, 8, 128), jnp.float32),
            pltpu.VMEM((4, FEAT, TILE), jnp.bfloat16),
            pltpu.VMEM((4, FEAT, TILE), jnp.float32),
            pltpu.VMEM((FEAT, TILE), jnp.float32),
            pltpu.VMEM((HEAD, HEAD), jnp.float32),
            pltpu.VMEM((HEAD, HEAD), jnp.float32),
        ],
        name="second",
    )(where, mask, stats, q_all, *chunks, tops, r, kfeat, qfeat)
    wide = ("y", "x", "c")
    part = lax.all_to_all(
        grads.reshape(32, 8, HEAD), wide, split_axis=0, concat_axis=0, tiled=True
    ).sum(0)
    part = send_copies(part, "z").sum(0)
    whole = send_copies(part, wide).reshape(2, 1, HEAD, HEAD)
    return loss.reshape(1, 1, piece), whole[0], whole[1]


def solution(mesh):
    finer = Mesh(mesh.devices.reshape(4, 8, 4, 2), ("y", "z", "x", "c"))
    qb, kb = ("y", "z"), ("x", "c")
    placed = (P(qb, kb, None, None), P(kb, qb, None, None), P(), P(qb, kb), P(), P())
    return jax.shard_map(
        local, mesh=finer, in_specs=placed, out_specs=(P(qb, kb, None), P(), P()), check_vma=False
    )
```

time: 249 us -> 148 us (0.59)
  matrix products: 82.3 us -> 0 us
  local copies, waits for them, and re-layouts: 43.1 us -> 5.39 us
  Pallas kernels: 0 us -> 35.6 us
  blocking collectives: 21.6 us -> 55.2 us
  starting transfers between devices: 35.5 us -> 17.8 us
  waiting for transfers between devices: 41.8 us -> 29.5 us
  loops' own time: 11.2 us -> 0 us
  other arithmetic: 11 us -> 2.58 us
    dot_general x28 -> x0, matrix products: 82.3 us -> none  [the longest x8 35.5 us: sub_tile(): jnp.einsum('buz,wuz->ubw', query_features_mapped, feature_slice, preferre...]
    pallas_call x0 -> x2, Pallas kernels: none -> 35.6 us  [the longest x1 18.8 us: local(): pl.pallas_call(first_kernel, out_shape=(f32(8, 16, TILE), f32(SLOTS, 8, T...]
    all_to_all x2 -> x4, blocking collectives: 21.6 us -> 55.2 us  [the longest x2 24 us: send_copies(): return lax.all_to_all(copies, axes, split_axis=0, concat_axis=0, tiled=True)]
    all_to_all x5 -> x2, waiting for transfers between devices: 41.8 us -> 16.8 us  [send_copies(): return lax.all_to_all(copies, axes, split_axis=0, concat_axis=0, tiled=True)]
    all_to_all x5 -> x2, starting transfers between devices: 35.5 us -> 14.1 us  [send_copies(): return lax.all_to_all(copies, axes, split_axis=0, concat_axis=0, tiled=True)]
    ppermute x0 -> x3, waiting for transfers between devices: none -> 12.7 us  [local(): lax.ppermute(load, 'x', [(i, (i + step) % 4) for i in range(4)])]
    another operation x2 -> x0, loops' own time: 11.2 us -> none  [the longest x1 5.75 us: local(): dquery_all, dkey_parts = lax.scan(second_pass, zero_grads[0], sub_indices)]
    unnamed x31 -> x13, local copies, waits for them, and re-layouts: 11.7 us -> 1.76 us
  transfers between devices with their start and end apart: 5 -> 5, of which waited for: 5 -> 5; matrix products, arithmetic and copies ran while one was open for 3% -> 1% of each run, Pallas kernels for 0% -> 0%
where the time goes in v1:
time: 148 us; the launch traced here: 147 us
  blocking collectives  55.2 us (37%)
  Pallas kernels  35.6 us (24%)
  waiting for transfers between devices  29.5 us (20%)
  starting transfers between devices  17.8 us (12%)
  local copies, waits for them, and re-layouts  5.39 us (4%)
  other arithmetic  2.58 us (2%)
    all_to_all x2, blocking collectives, send_copies(): return lax.all_to_all(copies, axes, split_axis=0, concat_axis=0, tiled=True)  24 us
    pallas_call x1, Pallas kernels, local(): pl.pallas_call(first_kernel, out_shape=(f32(8, 16, TILE), f32(SLOTS, 8, T...  18.8 us
    all_to_all x1, blocking collectives, local(): lax.all_to_all(grads.reshape(32, 8, HEAD), wide, split_axis=0, concat_axi...  18.6 us
    all_to_all x2, waiting for transfers between devices, send_copies(): return lax.all_to_all(copies, axes, split_axis=0, concat_axis=0, tiled=True)  16.8 us
    pallas_call x1, Pallas kernels, local(): pl.pallas_call(second_kernel, out_shape=(f32(1, piece), f32(2, HEAD, HEAD...  16.7 us
    all_to_all x2, starting transfers between devices, send_copies(): return lax.all_to_all(copies, axes, split_axis=0, concat_axis=0, tiled=True)  14.1 us
    ppermute x3, waiting for transfers between devices, local(): lax.ppermute(load, 'x', [(i, (i + step) % 4) for i in range(4)])  12.7 us
    all_to_all x1, blocking collectives, local(): lax.all_to_all(stats, ('y', 'c'), split_axis=0, concat_axis=0, tiled=True)  12.6 us
  transfers between devices with their start and end apart: 5, of which 5 were waited for; matrix products, arithmetic and copies ran while one was open for 1% of the time, Pallas kernels for 0%

profile of v1, /device:TPU:1, one launch (start us, length us, event | category | flops | bytes accessed | tf_op | source)
XLA Modules:
  0.0 146.8 jit_solution(17981916772375125809)
XLA Ops:
  0.7 0.7 convert_element_type.46
  1.4 0.1 convert_element_type.56
  1.4 0.9 copy.25
  2.3 0.9 copy.29
  3.2 0.8 dynamic-slice_convert_fusion
  4.0 0.3 fusion.13
  4.4 0.1 copy.27
  4.5 0.8 broadcast_in_dim.16
  5.2 6.6 %all-to-all-start = ((bf16[8,144,128]{2,1,0:T(8,128)(2,1)}), bf16[8,144,128]{2,1,0:T(8,128)(2,1)S(1)}, u32[]{:S(2)}, u32[]{:S(2)}) async-start(bf16[8,144,128]{2,1,0:T(8,128)(2,1)} %broadcast_in_dim.16), calls=%async_computation | async-start | bytes 589824 | tf_op jit(solution)/shard_map/all_to_all | solution.py:38
  11.8 0.1 copy.30
  11.9 6.7 %all-to-all-done.q_ref = bf16[8,144,128]{2,1,0:T(8,128)(2,1)S(1)} async-done(((bf16[8,144,128]{2,1,0:T(8,128)(2,1)}), bf16[8,144,128]{2,1,0:T(8,128)(2,1)S(1)}, u32[]{:S(2)}, u32[]{:S(2)}) %all-to-all-start) | async-done | bytes 294944 | tf_op jit(solution)/shard_map/all_to_all | solution.py:38
  18.6 0.8 broadcast_in_dim.17
  19.4 7.5 %all-to-all-start.1 = ((bf16[8,128,128]{2,1,0:T(8,128)(2,1)}), bf16[8,128,128]{2,1,0:T(8,128)(2,1)S(1)}, u32[]{:S(2)}, u32[]{:S(2)}) async-start(bf16[8,128,128]{2,1,0:T(8,128)(2,1)} %broadcast_in_dim.17), calls=%async_computation.1 | async-start | bytes 524288 | tf_op jit(solution)/shard_map/all_to_all | solution.py:38
  27.0 10.1 %all-to-all-done.1 = bf16[8,128,128]{2,1,0:T(8,128)(2,1)S(1)} async-done(((bf16[8,128,128]{2,1,0:T(8,128)(2,1)}), bf16[8,128,128]{2,1,0:T(8,128)(2,1)S(1)}, u32[]{:S(2)}, u32[]{:S(2)}) %all-to-all-start.1) | async-done | bytes 262176 | tf_op jit(solution)/shard_map/all_to_all | solution.py:38
  37.2 2.6 %collective-permute-start.2 = (bf16[1040,128]{1,0:T(8,128)(2,1)S(1)}, bf16[1040,128]{1,0:T(8,128)(2,1)S(1)}, u32[]{:S(2)}, u32[]{:S(2)}) collective-permute-start(bf16[1040,128]{1,0:T(8,128)(2,1)S(1)} %fusion.1.k0), channel_id=1, source_target_pairs={{0,6},{2,0},{4,2},{6,4},{1,7},{3,1},{5,3},{7,5},{8,14},{10,8},{12,... | collective-permute-start | bytes 798728 | tf_op jit(solution)/shard_map/ppermute | solution.py:273
  39.7 0.5 collective-permute-start.1
  40.3 0.6 collective-permute-start
  40.9 0.7 pad_add_fusion.where
  41.6 3.8 %collective-permute-done.2.k3 = bf16[1040,128]{1,0:T(8,128)(2,1)S(1)} collective-permute-done((bf16[1040,128]{1,0:T(8,128)(2,1)S(1)}, bf16[1040,128]{1,0:T(8,128)(2,1)S(1)}, u32[]{:S(2)}, u32[]{:S(2)}) %collective-permute-start.2) | collective-permute-done | bytes 266272 | tf_op jit(solution)/shard_map/ppermute | solution.py:273
  45.5 0.1 stack.38
  45.6 1.0 collective-permute-done.1.k2
  46.6 0.1 stack.37
  46.7 7.8 %collective-permute-done.k1 = bf16[1040,128]{1,0:T(8,128)(2,1)S(1)} collective-permute-done((bf16[1040,128]{1,0:T(8,128)(2,1)S(1)}, bf16[1040,128]{1,0:T(8,128)(2,1)S(1)}, u32[]{:S(2)}, u32[]{:S(2)}) %collective-permute-start) | collective-permute-done | bytes 266272 | tf_op jit(solution)/shard_map/ppermute | solution.py:273
  54.6 0.1 stack.36
  54.7 0.6 reshape.64.mask
  55.3 18.8 %first.1 = (f32[8,16,256]{2,1,0:T(8,128)}, f32[40,8,256]{2,1,0:T(8,128)}, f32[40,256,256]{2,1,0:T(8,128)}, f32[16,256,256]{2,1,0:T(8,128)}, f32[4,256,256]{2,1,0:T(8,128)}) custom-call(s32[4]{0:T(128)} %pad_add_fusion.where, s32[64]{0:T(128)} %reshape.64.mask, bf16[8,144,128]{2,1,0:T(8,128)(2,1)} %copy-done, bf16[1040,128]{1,0:T(8,128)(2,1)} %copy-done.1, ...), custom_call_target="tpu_custom_call" | custom-call | tf_op jit(solution)/shard_map/first/pallas_call | solution.py:281
  74.2 12.6 %all_to_all.30.st_ref = f32[8,16,256]{2,1,0:T(8,128)} all-to-all(f32[8,16,256]{2,1,0:T(8,128)} %get-tuple-element.10), channel_id=1, replica_groups=mesh['y'=4,'z'=8,'x'=4,'c'=2] {'y','c'}, dimensions={0} | all-to-all | bytes 262144 | tf_op jit(solution)/shard_map/all_to_all | solution.py:300
  86.7 16.7 %second.1 = (f32[1,128]{1,0:T(1,128)}, f32[2,128,128]{2,1,0:T(8,128)}) custom-call(s32[4]{0:T(128)} %pad_add_fusion.where, s32[64]{0:T(128)} %reshape.64.mask, f32[8,16,256]{2,1,0:T(8,128)} %all_to_all.30.st_ref, bf16[8,144,128]{2,1,0:T(8,128)(2,1)} %copy-done, bf16[1040,128]{1,0:T(8,128)(2,1)} %copy-done.1, bf16[1040,128]{1,0:T(8,128)(2,1)} %copy-done.4, ...), custom_call_target="tpu_custom_call" | custom-call | tf_op jit(solution)/shard_map/second/pallas_call | solution.py:301
  103.5 18.6 %all_to_all.31 = f32[32,8,128]{2,1,0:T(8,128)S(1)} all-to-all(f32[32,8,128]{2,1,0:T(8,128)} %bitcast.26), channel_id=1, replica_groups=mesh['y'=4,'z'=8,'x'=4,'c'=2] {'y','x','c'}, dimensions={0} | all-to-all | bytes 262144 | tf_op jit(solution)/shard_map/all_to_all | solution.py:318
  122.1 11.4 %all_to_all.32 = f32[8,8,128]{2,1,0:T(8,128)S(1)} all-to-all(f32[8,8,128]{2,1,0:T(8,128)S(1)} %broadcast_in_dim.18), channel_id=1, replica_groups=mesh['y'=4,'z'=8,'x'=4,'c'=2] {'z'}, dimensions={0} | all-to-all | bytes 65536 | tf_op jit(solution)/shard_map/all_to_all | solution.py:38
  133.6 12.6 %all_to_all.33 = f32[32,8,128]{2,1,0:T(8,128)S(1)} all-to-all(f32[32,8,128]{2,1,0:T(8,128)S(1)} %broadcast_in_dim.19), channel_id=1, replica_groups=mesh['y'=4,'z'=8,'x'=4,'c'=2] {'y','x','c'}, dimensions={0} | all-to-all | bytes 262144 | tf_op jit(solution)/shard_map/all_to_all | solution.py:38
  146.2 0.7 slice_bitcast_fusion
  (30 shorter events, 0.4 us)
Async XLA Ops:
  5.2 13.4 %all-to-all-start = ((bf16[8,144,128]{2,1,0:T(8,128)(2,1)}), bf16[8,144,128]{2,1,0:T(8,128)(2,1)S(1)}, u32[]{:S(2)}, u32[]{:S(2)}) async-start(bf16[8,144,128]{2,1,0:T(8,128)(2,1)} %broadcast_in_dim.16), calls=%async_computation | async-start | bytes 589824 | tf_op jit(solution)/shard_map/all_to_all | solution.py:38
  18.6 36.7 %copy-start = (bf16[8,144,128]{2,1,0:T(8,128)(2,1)}, bf16[8,144,128]{2,1,0:T(8,128)(2,1)S(1)}, u32[]{:S(2)}) copy-start(bf16[8,144,128]{2,1,0:T(8,128)(2,1)S(1)} %all-to-all-done.q_ref) | copy-start | bytes 884740
  19.4 17.7 %all-to-all-start.1 = ((bf16[8,128,128]{2,1,0:T(8,128)(2,1)}), bf16[8,128,128]{2,1,0:T(8,128)(2,1)S(1)}, u32[]{:S(2)}, u32[]{:S(2)}) async-start(bf16[8,128,128]{2,1,0:T(8,128)(2,1)} %broadcast_in_dim.17), calls=%async_computation.1 | async-start | bytes 524288 | tf_op jit(solution)/shard_map/all_to_all | solution.py:38
  37.2 18.2 %copy-start.1 = (bf16[1040,128]{1,0:T(8,128)(2,1)}, bf16[1040,128]{1,0:T(8,128)(2,1)S(1)}, u32[]{:S(2)}) copy-start(bf16[1040,128]{1,0:T(8,128)(2,1)S(1)} %fusion.1.k0) | copy-start | bytes 798724
  37.2 8.3 %collective-permute-start.2 = (bf16[1040,128]{1,0:T(8,128)(2,1)S(1)}, bf16[1040,128]{1,0:T(8,128)(2,1)S(1)}, u32[]{:S(2)}, u32[]{:S(2)}) collective-permute-start(bf16[1040,128]{1,0:T(8,128)(2,1)S(1)} %fusion.1.k0), channel_id=1, source_target_pairs={{0,6},{2,0},{4,2},{6,4},{1,7},{3,1},{5,3},{7,5},{8,14},{10,8},{12,... | collective-permute-start | bytes 798728 | tf_op jit(solution)/shard_map/ppermute | solution.py:273
  39.7 6.9 %collective-permute-start.1 = (bf16[1040,128]{1,0:T(8,128)(2,1)S(1)}, bf16[1040,128]{1,0:T(8,128)(2,1)S(1)}, u32[]{:S(2)}, u32[]{:S(2)}) collective-permute-start(bf16[1040,128]{1,0:T(8,128)(2,1)S(1)} %fusion.1.k0), channel_id=1, source_target_pairs={{0,4},{2,6},{4,0},{6,2},{1,5},{3,7},{5,1},{7,3},{8,12},{10,14},{12... | collective-permute-start | bytes 798728 | tf_op jit(solution)/shard_map/ppermute | solution.py:273
  40.3 14.3 %collective-permute-start = (bf16[1040,128]{1,0:T(8,128)(2,1)S(1)}, bf16[1040,128]{1,0:T(8,128)(2,1)S(1)}, u32[]{:S(2)}, u32[]{:S(2)}) collective-permute-start(bf16[1040,128]{1,0:T(8,128)(2,1)S(1)} %fusion.1.k0), channel_id=1, source_target_pairs={{0,2},{2,4},{4,6},{6,0},{1,3},{3,5},{5,7},{7,1},{8,10},{10,12},{12... | collective-permute-start | bytes 798728 | tf_op jit(solution)/shard_map/ppermute | solution.py:273
  45.5 9.9 %copy-start.2 = (bf16[1040,128]{1,0:T(8,128)(2,1)}, bf16[1040,128]{1,0:T(8,128)(2,1)S(1)}, u32[]{:S(2)}) copy-start(bf16[1040,128]{1,0:T(8,128)(2,1)S(1)} %collective-permute-done.2.k3) | copy-start | bytes 798724
  46.6 8.7 %copy-start.3 = (bf16[1040,128]{1,0:T(8,128)(2,1)}, bf16[1040,128]{1,0:T(8,128)(2,1)S(1)}, u32[]{:S(2)}) copy-start(bf16[1040,128]{1,0:T(8,128)(2,1)S(1)} %collective-permute-done.1.k2) | copy-start | bytes 798724
  54.6 0.8 copy-start.4

commit v2 on v1

v2 whole, which is shorter than its diff:
```python
import functools

import jax
import jax.numpy as jnp
from jax import lax
from jax.experimental import pallas as pl
from jax.experimental.pallas import tpu as pltpu
from jax.sharding import Mesh
from jax.sharding import PartitionSpec as P

LOW = -1e30
LOG2E = 1.4426950408889634
LN2 = 0.6931471805599453
TILE = 256
HEAD = 128
FEAT = 256
PIECE = 128
SUB = 64
MARKS = 32
CHUNKS = (0, 1, 3, 2)


def nn(a, b):
    return lax.dot_general(a, b, (((1,), (0,)), ((), ())), preferred_element_type=jnp.float32)


def nt(a, b):
    return lax.dot_general(a, b, (((1,), (1,)), ((), ())), preferred_element_type=jnp.float32)


def fold(a):
    return a.reshape(a.shape[0] // 8, 8, a.shape[1])


def place():
    return tuple(lax.axis_index(name) for name in ("x", "y", "z", "c"))


def rotate_kernel(
    pos_hbm, q_hbm, k_hbm, mask_hbm, wq_hbm, wk_hbm,
    q_out, k_out, wq_out, wk_out,
    lines_ref, values_ref, mask_ref, sems,
):
    x, y, z, c = place()
    pieces = ((y * 8 + z) * 8 + x * 2 + c, (x * 2 + c) * 32 + y * 8 + z)
    copies = [
        pltpu.make_async_copy(pos_hbm.at[pieces[0] // 8], lines_ref.at[0], sems.at[0]),
        pltpu.make_async_copy(pos_hbm.at[pieces[1] // 8], lines_ref.at[1], sems.at[1]),
        pltpu.make_async_copy(q_hbm, values_ref.at[0], sems.at[2]),
        pltpu.make_async_copy(k_hbm, values_ref.at[1], sems.at[3]),
        pltpu.make_async_copy(mask_hbm, mask_ref, sems.at[4]),
        pltpu.make_async_copy(wq_hbm, wq_out, sems.at[5]),
        pltpu.make_async_copy(wk_hbm, wk_out, sems.at[6]),
    ]
    for copy in copies:
        copy.start()
    row = lax.broadcasted_iota(jnp.int32, (8, PIECE), 0)
    base = jnp.ones((8, PIECE), jnp.float32)
    for n in range(1, 8):
        base = jnp.where(row == n, jnp.float32(10000.0 ** (-n / 64)), base)
    frequency = jnp.concatenate(
        [base * jnp.float32(10000.0 ** (-8 * n / 64)) for n in range(8)], 0
    )
    for copy in copies:
        copy.wait()

    def turn(n):
        line = jnp.sum(jnp.where(row == pieces[n] % 8, lines_ref[n], 0), 0, keepdims=True)
        angles = line.astype(jnp.float32) * frequency
        both = jnp.transpose(jnp.concatenate([jnp.cos(angles), jnp.sin(angles)], 0))
        other = pltpu.roll(both, 64, 1)
        low = lax.broadcasted_iota(jnp.int32, (PIECE, HEAD), 1) < 64
        values = values_ref[n].astype(jnp.float32)
        return (
            values * jnp.where(low, both, other)
            + pltpu.roll(values, 64, 1) * jnp.where(low, -other, both)
        ).astype(jnp.bfloat16)

    own_q = turn(0)
    own_k = turn(1)
    marks = mask_ref[...].astype(jnp.float32)
    marks = jnp.concatenate([marks, jnp.zeros((4, 112), jnp.float32)], 1)
    marks = jnp.concatenate([marks, jnp.zeros((12, HEAD), jnp.float32)], 0).astype(jnp.bfloat16)
    q_out[:PIECE] = own_q
    q_out[PIECE:] = marks
    for n in range(8):
        k_out[n] = own_k


def features(weight_t, rows):
    mapped = nt(weight_t, rows)
    up = jnp.exp(mapped - jnp.max(mapped, 0, keepdims=True))
    down = jnp.exp(jnp.min(mapped, 0, keepdims=True) - mapped)
    up = up * (1.0 / jnp.sum(up, 0, keepdims=True))
    down = down * (1.0 / jnp.sum(down, 0, keepdims=True))
    return jnp.concatenate([up, down], axis=0)


def turned(a):
    return jnp.transpose(a.astype(jnp.float32)).astype(jnp.bfloat16)


def not_after(start, count):
    shape = (count, TILE)
    keys = lax.broadcasted_iota(jnp.int32, shape, 0) + start
    return keys <= lax.broadcasted_iota(jnp.int32, shape, 1)


def fetch_marks(k_refs, staged, marks, sems):
    for n, k_ref in enumerate(k_refs):
        staged[n] = k_ref[4 * TILE :, :].astype(jnp.float32).astype(jnp.int32)
        pltpu.make_async_copy(staged.at[n], marks.at[n], sems.at[n]).start()


def wait_marks(k_refs, staged, marks, sems):
    for n in range(len(k_refs)):
        pltpu.make_async_copy(staged.at[n], marks.at[n], sems.at[n]).wait()


def for_tiles(marks, n, chunk, sub, body):
    x, y, z, c = place()
    key_tile = ((x + 4 - chunk) % 4) * 32 + c * 16 + y * 4 + sub

    def step(stripe, carry):
        row_tile = stripe * 32 + z * 4 + x
        back = (y + 4 - stripe) % 4
        live = marks[n, (back ^ (back // 2)) * 8 + x, y * 4 + sub] > 0

        @pl.when(live & (key_tile < row_tile))
        def _():
            body(stripe, False)

        @pl.when(live & (key_tile == row_tile))
        def _():
            body(stripe, True)

        return carry

    lax.fori_loop(0, 4, step, 0)


def first_kernel(chunks, *refs):
    count = len(chunks)
    opens, closes = 0 in chunks, 2 in chunks
    refs = list(refs)
    take = lambda number: [refs.pop(0) for _ in range(number)]
    k_refs = take(count)
    (wk_ref,) = take(1)
    if opens:
        wq_ref, *q_refs = take(5)
        run, q_turned, qf_low, qfeat_ref, rows_ref = take(5)
    else:
        old_run, q_turned, qf_low = take(3)
        (run,) = take(1)
    top_refs, u_refs, kfeat_refs = take(count), take(count), take(count)
    if closes:
        (stats_ref,) = take(1)
    raw_ref, kf_ref, staged, marks, sems = refs
    scale = LOG2E * HEAD**-0.5
    fetch_marks(k_refs, staged, marks, sems)
    wk_t = turned(wk_ref[...])
    if opens:
        wq_t = turned(wq_ref[...])

        x, y, z, c = place()
        for n, q_ref in enumerate(q_refs):
            stripe = (y + 4 - CHUNKS[n]) % 4
            rows_ref[stripe, c] = q_ref[0, :PIECE]
            rows_ref[stripe, 1 - c] = q_ref[1, :PIECE]
        for stripe in range(4):
            rows = rows_ref[stripe].reshape(TILE, HEAD)
            q_turned[stripe] = turned(rows)
            feat = features(wq_t, rows)
            qfeat_ref[stripe] = feat
            qf_low[stripe] = feat.astype(jnp.bfloat16)
        run[0] = jnp.full((4, 8, TILE), LOW, jnp.float32)
        for n in (1, 2, 3):
            run[n] = jnp.zeros((4, 8, TILE), jnp.float32)
    else:
        run[...] = old_run[...]
    wait_marks(k_refs, staged, marks, sems)

    for n, chunk in enumerate(chunks):
        k_ref, top_ref, u_ref, kfeat_ref = k_refs[n], top_refs[n], u_refs[n], kfeat_refs[n]

        def key_step(sub, carry):
            keys = k_ref[pl.ds(pl.multiple_of(sub * TILE, TILE), TILE), :]
            feat = features(wk_t, keys)
            kfeat_ref[sub] = feat
            kf_ref[...] = jnp.transpose(feat.astype(jnp.bfloat16))

            def body(stripe, corner):
                slot = sub * 4 + stripe
                raw = nn(keys, q_turned[stripe])
                if corner:
                    raw = jnp.where(not_after(0, TILE), raw, LOW)
                raw_ref[...] = raw
                top = jnp.max(jnp.max(fold(raw), 0), 0, keepdims=True) * scale
                top = jnp.broadcast_to(top, (8, TILE))
                total = jnp.zeros((8, TILE), jnp.float32)
                logs, norm = total, total
                for start in range(0, TILE, SUB):
                    part = pl.ds(start, SUB)
                    student = nn(kf_ref[part, :], qf_low[stripe])
                    if corner:
                        ok = not_after(start, SUB)
                        norm = norm + jnp.sum(fold(jnp.where(ok, student, 0.0)), 0)
                        student = jnp.where(ok, student, 1.0)
                    else:
                        norm = norm + jnp.sum(fold(student), 0)
                    t = fold(raw_ref[part, :]) * scale - top[None]
                    weight = jnp.exp2(t)
                    log_student = jnp.log2(fold(student))
                    u_ref[slot, part, :] = (t - log_student).reshape(SUB, TILE)
                    total = total + jnp.sum(weight, 0)
                    logs = logs + jnp.sum(weight * log_student, 0)
                top_ref[slot] = top
                old = run[0, stripe]
                new = jnp.maximum(old, top)
                left = jnp.exp2(old - new)
                right = jnp.exp2(top - new)
                run[0, stripe] = new
                run[1, stripe] = run[1, stripe] * left + total * right
                run[2, stripe] = run[2, stripe] * left + logs * right
                run[3, stripe] = run[3, stripe] + norm

            for_tiles(marks, n, chunk, sub, body)
            return carry

        lax.fori_loop(0, 4, key_step, 0)

    if closes:
        lines = [run[0, stripe][:1] for stripe in range(4)] + [
            jnp.sum(run[n, stripe], 0, keepdims=True) for n in (1, 2, 3) for stripe in range(4)
        ]
        lines = jnp.concatenate(lines, 0)
        for copy in range(8):
            stats_ref[copy] = lines


def split2(a):
    high = a.astype(jnp.bfloat16)
    low = (a - high.astype(jnp.float32)).astype(jnp.bfloat16)
    return jnp.concatenate([high, low], axis=0)


def weight_grad(feat, dfeat, rows):
    up, down = feat[:HEAD], feat[HEAD:]
    d1, d2 = dfeat[:HEAD], dfeat[HEAD:]
    dmapped = up * (d1 - jnp.sum(up * d1, 0, keepdims=True)) - down * (
        d2 - jnp.sum(down * d2, 0, keepdims=True)
    )
    parts = nn(split2(dmapped), rows)
    return parts[HEAD:] + parts[:HEAD]


def second_kernel(
    st_ref, q_ref, qfeat_ref, qf_low, *refs
):
    refs = list(refs)
    k_refs, top_refs, u_refs, kfeat_refs = (
        [refs.pop(0) for _ in range(4)] for _ in range(4)
    )
    loss_ref, grad_ref, lines, losses, kf_t, g_ref, dq_ref, dk_ref, gk_ref, staged, marks, sems = refs
    x, y, z, c = place()
    fetch_marks(k_refs, staged, marks, sems)
    top = st_ref[0, 0:4]
    for n in range(1, 8):
        top = jnp.maximum(top, st_ref[n, 0:4])
    total = jnp.zeros_like(top)
    logs = jnp.zeros_like(top)
    norm = jnp.zeros_like(top)
    for n in range(8):
        factor = jnp.exp2(st_ref[n, 0:4] - top)
        total = total + st_ref[n, 4:8] * factor
        logs = logs + st_ref[n, 8:12] * factor
        norm = norm + st_ref[n, 12:16]
    loss = jnp.log(norm) - (logs / total) * LN2
    for stripe in range(4):
        for half in range(2):
            losses[half, stripe] = jnp.broadcast_to(
                loss[stripe : stripe + 1, half * 128 : half * 128 + 128], (8, 128)
            )
    loss_ref[...] = losses[c, y][:1]
    base = (1.0 / norm) * (1.0 / 32768.0)
    shift = top + jnp.log2(total) + 15.0
    for stripe in range(4):
        lines[0, stripe] = jnp.broadcast_to(base[stripe : stripe + 1], (8, TILE))
        lines[1, stripe] = jnp.broadcast_to(shift[stripe : stripe + 1], (8, TILE))
    dq_ref[...] = jnp.zeros_like(dq_ref)
    gk_ref[...] = jnp.zeros_like(gk_ref)
    wait_marks(k_refs, staged, marks, sems)

    for n, chunk in enumerate(CHUNKS):
        k_ref, top_ref, u_ref, kfeat_ref = k_refs[n], top_refs[n], u_refs[n], kfeat_refs[n]

        def key_step(sub, carry):
            kf_t[...] = kfeat_ref[sub].astype(jnp.bfloat16)
            dk_ref[...] = jnp.zeros_like(dk_ref)

            def body(stripe, corner):
                slot = sub * 4 + stripe
                less = lines[1, stripe] - top_ref[slot]
                level = lines[0, stripe]
                for start in range(0, TILE, SUB):
                    part = pl.ds(start, SUB)
                    grad = level[None] - jnp.exp2(fold(u_ref[slot, part, :]) - less[None])
                    grad = grad.reshape(SUB, TILE)
                    if corner:
                        grad = jnp.where(not_after(start, SUB), grad, 0.0)
                    g_ref[part, :] = grad.astype(jnp.bfloat16)
                dq_ref[stripe] += nn(kf_t[...], g_ref[...])
                dk_ref[...] += nt(qf_low[stripe], g_ref[...])

            for_tiles(marks, n, chunk, sub, body)
            keys = k_ref[pl.ds(pl.multiple_of(sub * TILE, TILE), TILE), :]
            gk_ref[...] += weight_grad(kfeat_ref[sub], dk_ref[...], keys)
            return carry

        lax.fori_loop(0, 4, key_step, 0)

    gq = jnp.zeros((HEAD, HEAD), jnp.float32)
    for stripe in range(4):
        gq = gq + weight_grad(qfeat_ref[stripe], dq_ref[stripe], q_ref[stripe].reshape(TILE, HEAD))
    grad_ref[0] = jnp.transpose(gq)
    grad_ref[1] = jnp.transpose(gk_ref[...])


def f32(*shape):
    return jax.ShapeDtypeStruct(shape, jnp.float32)


def b16(*shape):
    return jax.ShapeDtypeStruct(shape, jnp.bfloat16)


def call(kernel, name, outs, scratch, work, *args):
    vmem = pl.BlockSpec(memory_space=pltpu.VMEM)
    return pl.pallas_call(
        kernel,
        out_shape=outs,
        in_specs=[vmem] * len(args),
        out_specs=(vmem,) * len(outs),
        scratch_shapes=scratch,
        compiler_params=pltpu.CompilerParams(vmem_limit_bytes=12 << 20),
        cost_estimate=pl.CostEstimate(
            flops=int(work * 1e8), bytes_accessed=int(work * 1e5), transcendentals=int(work * 1e5)
        ),
        name=name,
    )(*args)


def marks_scratch(count):
    return [
        pltpu.VMEM((count, MARKS, HEAD), jnp.int32),
        pltpu.SMEM((count, MARKS, HEAD), jnp.int32),
        pltpu.SemaphoreType.DMA((count,)),
    ]


def first_call(chunks, loads, w_key, opening, carried):
    count = len(chunks)
    outs = [f32(4, 4, 8, TILE)]
    if opening:
        outs += [b16(4, HEAD, TILE), b16(4, FEAT, TILE), f32(4, FEAT, TILE), b16(4, 2, PIECE, HEAD)]
    outs += [f32(16, 8, TILE)] * count + [f32(16, TILE, TILE)] * count
    outs += [f32(4, FEAT, TILE)] * count
    if 2 in chunks:
        outs += [f32(8, 16, TILE)]
    scratch = [
        pltpu.VMEM((TILE, TILE), jnp.float32),
        pltpu.VMEM((TILE, FEAT), jnp.bfloat16),
    ] + marks_scratch(count)
    return call(
        functools.partial(first_kernel, chunks),
        "first%d" % chunks[0],
        tuple(outs),
        scratch,
        20 * count,
        *loads,
        w_key,
        *(opening or carried),
    )


def exchanged(copies, axes):
    return lax.all_to_all(copies, axes, split_axis=0, concat_axis=0, tiled=True)


def local(queries, keys, positions, tile_mask, w_query, w_key):
    hbm = pl.BlockSpec(memory_space=pltpu.HBM)
    vmem = pl.BlockSpec(memory_space=pltpu.VMEM)
    q_own, k_copies, w_query, w_key = pl.pallas_call(
        rotate_kernel,
        out_shape=(
            b16(PIECE + 16, HEAD), b16(8, PIECE, HEAD), b16(HEAD, HEAD), b16(HEAD, HEAD)
        ),
        in_specs=[hbm] * 6,
        out_specs=(vmem,) * 4,
        scratch_shapes=[
            pltpu.VMEM((2, 8, PIECE), jnp.int32),
            pltpu.VMEM((2, PIECE, HEAD), jnp.bfloat16),
            pltpu.VMEM((4, 16), jnp.int32),
            pltpu.SemaphoreType.DMA((7,)),
        ],
        compiler_params=pltpu.CompilerParams(vmem_limit_bytes=60 << 20),
        name="rotate",
    )(
        positions.reshape(32, 8, PIECE),
        queries.reshape(PIECE, HEAD),
        keys.reshape(PIECE, HEAD),
        tile_mask,
        w_query[0],
        w_key[0],
    )
    k_near = exchanged(k_copies, "z")
    other = lax.ppermute(q_own, "c", [(0, 1), (1, 0)])
    pair = jnp.stack([q_own, other])
    pairs = [pair] + [
        lax.ppermute(pair, "y", [(i, (i + step) % 4) for i in range(4)]) for step in (1, 3, 2)
    ]
    marks = jnp.stack([near[:, PIECE : PIECE + 4] for near in pairs]).reshape(MARKS, HEAD)
    load = jnp.concatenate([k_near.reshape(4 * TILE, HEAD), marks], 0)
    loads = {0: load}
    for step in (1, 3, 2):
        loads[step] = lax.ppermute(load, "x", [(i, (i + step) % 4) for i in range(4)])
    run, q_turned, qf_low, qfeat, q_rows, *rest = first_call(
        (0,), [load], w_key, (w_query, *pairs), ()
    )
    tops, us, kfeats = ([item] for item in rest)
    for chunks in ((1, 3), (2,)):
        run, *rest = first_call(
            chunks, [loads[n] for n in chunks], w_key, (), (run, q_turned, qf_low)
        )
        count = len(chunks)
        tops += rest[:count]
        us += rest[count : 2 * count]
        kfeats += rest[2 * count : 3 * count]
    stats = exchanged(rest[-1], ("y", "c"))
    loss, grads = call(
        second_kernel,
        "second",
        (f32(1, PIECE), f32(2, HEAD, HEAD)),
        [
            pltpu.VMEM((2, 4, 8, TILE), jnp.float32),
            pltpu.VMEM((2, 4, 8, 128), jnp.float32),
            pltpu.VMEM((FEAT, TILE), jnp.bfloat16),
            pltpu.VMEM((TILE, TILE), jnp.bfloat16),
            pltpu.VMEM((4, FEAT, TILE), jnp.float32),
            pltpu.VMEM((FEAT, TILE), jnp.float32),
            pltpu.VMEM((HEAD, HEAD), jnp.float32),
        ]
        + marks_scratch(4),
        100,
        stats,
        q_rows,
        qfeat,
        qf_low,
        *[loads[n] for n in CHUNKS],
        *tops,
        *us,
        *kfeats,
    )
    wide = ("y", "x", "c")
    part = exchanged(grads.reshape(32, 8, HEAD), wide).sum(0)
    part = exchanged(jnp.broadcast_to(part, (8, 8, HEAD)), "z").sum(0)
    whole = exchanged(jnp.broadcast_to(part, (32, 8, HEAD)), wide).reshape(2, 1, HEAD, HEAD)
    return loss.reshape(1, 1, PIECE), whole[0], whole[1]


def solution(mesh):
    finer = Mesh(mesh.devices.reshape(4, 8, 4, 2), ("y", "z", "x", "c"))
    qb, kb = ("y", "z"), ("x", "c")
    placed = (P(qb, kb, None, None), P(kb, qb, None, None), P(), P(qb, kb), P(), P())
    return jax.shard_map(
        local, mesh=finer, in_specs=placed, out_specs=(P(qb, kb, None), P(), P()), check_vma=False
    )
```

time: 148 us -> 119 us (0.80)
  waiting for transfers between devices: 29.5 us -> 6.79 us
  Pallas kernels: 35.6 us -> 31.7 us
  local copies, waits for them, and re-layouts: 5.39 us -> 2.21 us
  blocking collectives: 55.2 us -> 57.5 us
    all_to_all x2 -> x1, waiting for transfers between devices: 16.8 us -> 3.4 us  [exchanged(): return lax.all_to_all(copies, axes, split_axis=0, concat_axis=0, tiled=True)]
    ppermute x3, waiting for transfers between devices: 12.7 us -> 0.32 us  [local(): lax.ppermute(load, 'x', [(i, (i + step) % 4) for i in range(4)])]
    ppermute x0 -> x4, starting transfers between devices: none -> 7.67 us  [the longest x3 4.38 us: local(): lax.ppermute(pair, 'y', [(i, (i + step) % 4) for i in range(4)])]
    all_to_all x2 -> x1, starting transfers between devices: 14.1 us -> 6.48 us  [exchanged(): return lax.all_to_all(copies, axes, split_axis=0, concat_axis=0, tiled=True)]
    pallas_call x2 -> x5, Pallas kernels: 35.6 us -> 31.7 us  [the longest x4 29.7 us: call(): pl.pallas_call(kernel, out_shape=outs, in_specs=[vmem] * len(args), out_s...]
    ppermute x0 -> x4, waiting for transfers between devices: none -> 3.07 us  [the longest x3 3.07 us: local(): lax.ppermute(pair, 'y', [(i, (i + step) % 4) for i in range(4)])]
    all_to_all x4, blocking collectives: 55.2 us -> 57.5 us  [exchanged(): return lax.all_to_all(copies, axes, split_axis=0, concat_axis=0, tiled=True)]
    broadcast_in_dim x4 -> x2, local copies, waits for them, and re-layouts: 1.6 us -> 0.02 us  [the longest x1 0.01 us: local(): jnp.broadcast_to(part, (32, 8, HEAD))]
  transfers between devices with their start and end apart: 5 -> 8, of which waited for: 5 -> 4; matrix products, arithmetic and copies ran while one was open for 1% -> 1% of each run, Pallas kernels for 0% -> 10%
where the time goes in v2:
time: 119 us
  blocking collectives  57.5 us (48%)
  Pallas kernels  31.7 us (27%)
  starting transfers between devices  18.4 us (15%)
  waiting for transfers between devices  6.79 us (6%)
  local copies, waits for them, and re-layouts  2.21 us (2%)
  other arithmetic  1.54 us (1%)
    all_to_all x4, blocking collectives, exchanged(): return lax.all_to_all(copies, axes, split_axis=0, concat_axis=0, tiled=True)  57.5 us
    pallas_call x4, Pallas kernels, call(): pl.pallas_call(kernel, out_shape=outs, in_specs=[vmem] * len(args), out_s...  29.7 us
    all_to_all x1, starting transfers between devices, exchanged(): return lax.all_to_all(copies, axes, split_axis=0, concat_axis=0, tiled=True)  6.48 us
    ppermute x3, starting transfers between devices, local(): lax.ppermute(pair, 'y', [(i, (i + step) % 4) for i in range(4)])  4.38 us
    ppermute x3, starting transfers between devices, local(): lax.ppermute(load, 'x', [(i, (i + step) % 4) for i in range(4)])  4.29 us
    all_to_all x1, waiting for transfers between devices, exchanged(): return lax.all_to_all(copies, axes, split_axis=0, concat_axis=0, tiled=True)  3.4 us
    ppermute x1, starting transfers between devices, local(): other = lax.ppermute(q_own, 'c', [(0, 1), (1, 0)])  3.29 us
    ppermute x3, waiting for transfers between devices, local(): lax.ppermute(pair, 'y', [(i, (i + step) % 4) for i in range(4)])  3.07 us
  transfers between devices with their start and end apart: 8, of which 4 were waited for; matrix products, arithmetic and copies ran while one was open for 1% of the time, Pallas kernels for 10%

profile of v2, /device:TPU:1, one launch (start us, length us, event | category | flops | bytes accessed | tf_op | source)
XLA Modules:
  0.0 119.0 jit_solution(16763654607014706884)
XLA Ops:
  0.6 2.1 %rotate.1 = (bf16[144,128]{1,0:T(8,128)(2,1)}, bf16[8,128,128]{2,1,0:T(8,128)(2,1)}, bf16[128,128]{1,0:T(8,128)(2,1)}, bf16[128,128]{1,0:T(8,128)(2,1)}) custom-call(s32[32,8,128]{2,1,0:T(8,128)} %bitcast.29, bf16[128,128]{1,0:T(8,128)(2,1)} %bitcast.31, bf16[128,128]{1,0:T(8,128)(2,1)} %bitcast.32, s32[4,16]{1,0:T(4,128)} %mask_hbm.1, ...), custom_call_target="tpu_custom_call" | custom-call | tf_op jit(solution)/shard_map/rotate/pallas_call | solution.py:393
  2.7 3.3 %collective-permute-start = (bf16[144,128]{1,0:T(8,128)(2,1)}, bf16[144,128]{1,0:T(8,128)(2,1)S(1)}, u32[]{:S(2)}, u32[]{:S(2)}) collective-permute-start(bf16[144,128]{1,0:T(8,128)(2,1)} %get-tuple-element.29), channel_id=1, source_target_pairs={{0,1},{1,0},{2,3},{3,2},{4,5},{5,4},{6,7},{7,6},{8,9},{9,8},{10,11... | collective-permute-start | bytes 110600 | tf_op jit(solution)/shard_map/ppermute | solution.py:417
  6.0 6.5 %all-to-all-start = ((bf16[8,128,128]{2,1,0:T(8,128)(2,1)}), bf16[8,128,128]{2,1,0:T(8,128)(2,1)S(1)}, u32[]{:S(2)}, u32[]{:S(2)}) async-start(bf16[8,128,128]{2,1,0:T(8,128)(2,1)} %get-tuple-element.28), calls=%async_computation | async-start | bytes 524288 | tf_op jit(solution)/shard_map/all_to_all | solution.py:387
  12.5 0.0 copy-start.1
  12.5 0.0 collective-permute-done
  12.5 0.8 pad_maximum_fusion.1.refs_3_
  13.3 2.9 %collective-permute-start.3 = (bf16[2,144,128]{2,1,0:T(8,128)(2,1)S(1)}, bf16[2,144,128]{2,1,0:T(8,128)(2,1)S(1)}, u32[]{:S(2)}, u32[]{:S(2)}) collective-permute-start(bf16[2,144,128]{2,1,0:T(8,128)(2,1)S(1)} %pad_maximum_fusion.1.refs_3_), channel_id=1, source_target_pairs={{0,128},{64,192},{128,0},{192,64},{1,129},{65,193},{129,1},{193,65... | collective-permute-start | bytes 221192 | tf_op jit(solution)/shard_map/ppermute | solution.py:420
  16.2 0.8 collective-permute-start.2
  16.9 0.7 collective-permute-start.1
  17.6 0.7 fusion.1
  18.3 0.0 collective-permute-done.3.refs_6_
  18.3 2.1 %collective-permute-done.2.refs_5_ = bf16[2,144,128]{2,1,0:T(8,128)(2,1)S(1)} collective-permute-done((bf16[2,144,128]{2,1,0:T(8,128)(2,1)S(1)}, bf16[2,144,128]{2,1,0:T(8,128)(2,1)S(1)}, u32[]{:S(2)}, u32[]{:S(2)}) %collective-permute-start.2) | collective-permute-done | bytes 73760 | tf_op jit(solution)/shard_map/ppermute | solution.py:420
  20.4 1.0 collective-permute-done.1.refs_4_
  21.4 3.4 %all-to-all-done = bf16[8,128,128]{2,1,0:T(8,128)(2,1)S(1)} async-done(((bf16[8,128,128]{2,1,0:T(8,128)(2,1)}), bf16[8,128,128]{2,1,0:T(8,128)(2,1)S(1)}, u32[]{:S(2)}, u32[]{:S(2)}) %all-to-all-start) | async-done | bytes 262176 | tf_op jit(solution)/shard_map/all_to_all | solution.py:387
  24.9 2.6 %collective-permute-start.6 = (bf16[1056,128]{1,0:T(8,128)(2,1)S(1)}, bf16[1056,128]{1,0:T(8,128)(2,1)S(1)}, u32[]{:S(2)}, u32[]{:S(2)}) collective-permute-start(bf16[1056,128]{1,0:T(8,128)(2,1)S(1)} %pad_maximum_fusion.refs_0_), channel_id=1, source_target_pairs={{0,6},{2,0},{4,2},{6,4},{1,7},{3,1},{5,3},{7,5},{8,14},{10,8},{12,... | collective-permute-start | bytes 811016 | tf_op jit(solution)/shard_map/ppermute | solution.py:426
  27.4 0.0 collective-permute-start.5
  27.4 1.7 %collective-permute-start.4 = (bf16[1056,128]{1,0:T(8,128)(2,1)S(1)}, bf16[1056,128]{1,0:T(8,128)(2,1)S(1)}, u32[]{:S(2)}, u32[]{:S(2)}) collective-permute-start(bf16[1056,128]{1,0:T(8,128)(2,1)S(1)} %pad_maximum_fusion.refs_0_), channel_id=1, source_target_pairs={{0,4},{2,6},{4,0},{6,2},{1,5},{3,7},{5,1},{7,3},{8,12},{10,14},{12... | collective-permute-start | bytes 811016 | tf_op jit(solution)/shard_map/ppermute | solution.py:426
  29.1 0.8 copy-done
  29.9 0.8 copy-done.2
  30.7 5.9 %first0.1 = (f32[4,4,8,256]{3,2,1,0:T(8,128)S(1)}, bf16[4,128,256]{2,1,0:T(8,128)(2,1)S(1)}, bf16[4,256,256]{2,1,0:T(8,128)(2,1)S(1)}, f32[4,256,256]{2,1,0:T(8,...) custom-call(bf16[1056,128]{1,0:T(8,128)(2,1)S(1)} %pad_maximum_fusio, ...), custom_call_target="tpu_custom_call" | custom-call | flops 2000000000 | bytes 2000000 | tf_op jit(solution)/shard_map/first0/pallas_call | solution.py:339
  36.5 0.0 collective-permute-done.6.refs_1_.refs_2_
  36.5 0.3 collective-permute-done.5.refs_0_.refs_1_
  36.9 0.0 copy-done.1
  36.9 6.2 %first1.1 = (f32[4,4,8,256]{3,2,1,0:T(8,128)S(1)}, f32[16,8,256]{2,1,0:T(8,128)S(1)}, f32[16,8,256]{2,1,0:T(8,128)S(1)}, f32[16,256,256]{2,1,0:T(8,128)S(1)}, f3...) custom-call(bf16[1056,128]{1,0:T(8,128)(2,1)S(1)} %collective-permute-done.5.refs_0_.refs_1_, ...), custom_call_target="tpu_custom_call" | custom-call | flops 4000000000 | bytes 4000000 | tf_op jit(solution)/shard_map/first1/pallas_call | solution.py:339
  43.1 0.0 collective-permute-done.4.refs_0_.refs_3_
  43.1 4.5 %first2.1 = (f32[4,4,8,256]{3,2,1,0:T(8,128)}, f32[16,8,256]{2,1,0:T(8,128)S(1)}, f32[16,256,256]{2,1,0:T(8,128)S(1)}, f32[4,256,256]{2,1,0:T(8,128)S(1)}, f32[8,16,256]{2,1,0:T(8,128)S(1)}) custom-call(bf16[1056,128]{1,0:T(8,128)(2,1)S(1)} %collective-permute-done.4.refs_0_.refs_3_, bf16[128,128]{1,0:T(8,128)(2,1)S(1)} %copy-done.1, ...), custom_call_target="tpu_custom_call" | custom-call | flops 2000000000 | bytes 2000000 | tf_op jit(solution)/shard_map/first2/pallas_call | solution.py:339
  47.6 15.8 %all_to_all.25.st_ref = f32[8,16,256]{2,1,0:T(8,128)S(1)} all-to-all(f32[8,16,256]{2,1,0:T(8,128)S(1)} %get-tuple-element.36), channel_id=1, replica_groups=mesh['y'=4,'z'=8,'x'=4,'c'=2] {'y','c'}, dimensions={0} | all-to-all | bytes 262144 | tf_op jit(solution)/shard_map/all_to_all | solution.py:387
  63.3 13.1 %second.1 = (f32[1,128]{1,0:T(1,128)}, f32[2,128,128]{2,1,0:T(8,128)S(1)}) custom-call(f32[8,16,256]{2,1,0:T(8,128)S(1)} %all_to_all.25.st_ref, bf16[4,2,128,128]{3,2,1,0:T(8,128)(2,1)S(1)} %get-tuple-element.37.q_ref, f32[4,256,256]{2,1,0:T(8,128)S(1)} %get-tuple-element.38.qfeat_ref, bf16[4,256,256]{2,1,0:T(8,128)(2,1)S(1)} %get-tuple-element.34.refs_5_.refs_4_.qf_low, ...), custom_call_target="tpu_custom_call" | custom-call | flops 10000000000 | bytes 10000000 | tf_op jit(solution)/shard_map/second/pallas_call | solution.py:339
  76.5 18.2 %all_to_all.26 = f32[32,8,128]{2,1,0:T(8,128)S(1)} all-to-all(f32[32,8,128]{2,1,0:T(8,128)S(1)} %bitcast.23), channel_id=1, replica_groups=mesh['y'=4,'z'=8,'x'=4,'c'=2] {'y','x','c'}, dimensions={0} | all-to-all | bytes 262144 | tf_op jit(solution)/shard_map/all_to_all | solution.py:387
  94.7 11.0 %all_to_all.27 = f32[8,8,128]{2,1,0:T(8,128)S(1)} all-to-all(f32[8,8,128]{2,1,0:T(8,128)S(1)} %broadcast_in_dim.6), channel_id=1, replica_groups=mesh['y'=4,'z'=8,'x'=4,'c'=2] {'z'}, dimensions={0} | all-to-all | bytes 65536 | tf_op jit(solution)/shard_map/all_to_all | solution.py:387
  105.7 12.6 %all_to_all.28 = f32[32,8,128]{2,1,0:T(8,128)S(1)} all-to-all(f32[32,8,128]{2,1,0:T(8,128)S(1)} %broadcast_in_dim.7), channel_id=1, replica_groups=mesh['y'=4,'z'=8,'x'=4,'c'=2] {'y','x','c'}, dimensions={0} | all-to-all | bytes 262144 | tf_op jit(solution)/shard_map/all_to_all | solution.py:387
  118.3 0.7 slice_bitcast_fusion
  (11 shorter events, 0.1 us)
Async XLA Ops:
  2.7 9.8 %collective-permute-start = (bf16[144,128]{1,0:T(8,128)(2,1)}, bf16[144,128]{1,0:T(8,128)(2,1)S(1)}, u32[]{:S(2)}, u32[]{:S(2)}) collective-permute-start(bf16[144,128]{1,0:T(8,128)(2,1)} %get-tuple-element.29), channel_id=1, source_target_pairs={{0,1},{1,0},{2,3},{3,2},{4,5},{5,4},{6,7},{7,6},{8,9},{9,8},{10,11... | collective-permute-start | bytes 110600 | tf_op jit(solution)/shard_map/ppermute | solution.py:417
  6.0 18.8 %all-to-all-start = ((bf16[8,128,128]{2,1,0:T(8,128)(2,1)}), bf16[8,128,128]{2,1,0:T(8,128)(2,1)S(1)}, u32[]{:S(2)}, u32[]{:S(2)}) async-start(bf16[8,128,128]{2,1,0:T(8,128)(2,1)} %get-tuple-element.28), calls=%async_computation | async-start | bytes 524288 | tf_op jit(solution)/shard_map/all_to_all | solution.py:387
  12.5 24.4 %copy-start.1 = (bf16[128,128]{1,0:T(8,128)(2,1)S(1)}, bf16[128,128]{1,0:T(8,128)(2,1)}, u32[]{:S(2)}) copy-start(bf16[128,128]{1,0:T(8,128)(2,1)} %get-tuple-element.30.refs_1_.refs_2_) | copy-start | bytes 98308
  13.3 5.1 %collective-permute-start.3 = (bf16[2,144,128]{2,1,0:T(8,128)(2,1)S(1)}, bf16[2,144,128]{2,1,0:T(8,128)(2,1)S(1)}, u32[]{:S(2)}, u32[]{:S(2)}) collective-permute-start(bf16[2,144,128]{2,1,0:T(8,128)(2,1)S(1)} %pad_maximum_fusion.1.refs_3_), channel_id=1, source_target_pairs={{0,128},{64,192},{128,0},{192,64},{1,129},{65,193},{129,1},{193,65... | collective-permute-start | bytes 221192 | tf_op jit(solution)/shard_map/ppermute | solution.py:420
  16.2 4.3 %collective-permute-start.2 = (bf16[2,144,128]{2,1,0:T(8,128)(2,1)S(1)}, bf16[2,144,128]{2,1,0:T(8,128)(2,1)S(1)}, u32[]{:S(2)}, u32[]{:S(2)}) collective-permute-start(bf16[2,144,128]{2,1,0:T(8,128)(2,1)S(1)} %pad_maximum_fusion.1.refs_3_), channel_id=1, source_target_pairs={{0,192},{64,0},{128,64},{192,128},{1,193},{65,1},{129,65},{193,129... | collective-permute-start | bytes 221192 | tf_op jit(solution)/shard_map/ppermute | solution.py:420
  16.9 4.5 %collective-permute-start.1 = (bf16[2,144,128]{2,1,0:T(8,128)(2,1)S(1)}, bf16[2,144,128]{2,1,0:T(8,128)(2,1)S(1)}, u32[]{:S(2)}, u32[]{:S(2)}) collective-permute-start(bf16[2,144,128]{2,1,0:T(8,128)(2,1)S(1)} %pad_maximum_fusion.1.refs_3_), channel_id=1, source_target_pairs={{0,64},{64,128},{128,192},{192,0},{1,65},{65,129},{129,193},{193,1... | collective-permute-start | bytes 221192 | tf_op jit(solution)/shard_map/ppermute | solution.py:420
  24.9 11.7 %collective-permute-start.6 = (bf16[1056,128]{1,0:T(8,128)(2,1)S(1)}, bf16[1056,128]{1,0:T(8,128)(2,1)S(1)}, u32[]{:S(2)}, u32[]{:S(2)}) collective-permute-start(bf16[1056,128]{1,0:T(8,128)(2,1)S(1)} %pad_maximum_fusion.refs_0_), channel_id=1, source_target_pairs={{0,6},{2,0},{4,2},{6,4},{1,7},{3,1},{5,3},{7,5},{8,14},{10,8},{12,... | collective-permute-start | bytes 811016 | tf_op jit(solution)/shard_map/ppermute | solution.py:426
  27.4 9.4 %collective-permute-start.5 = (bf16[1056,128]{1,0:T(8,128)(2,1)S(1)}, bf16[1056,128]{1,0:T(8,128)(2,1)S(1)}, u32[]{:S(2)}, u32[]{:S(2)}) collective-permute-start(bf16[1056,128]{1,0:T(8,128)(2,1)S(1)} %pad_maximum_fusion.refs_0_), channel_id=1, source_target_pairs={{0,2},{2,4},{4,6},{6,0},{1,3},{3,5},{5,7},{7,1},{8,10},{10,12},{12... | collective-permute-start | bytes 811016 | tf_op jit(solution)/shard_map/ppermute | solution.py:426
  27.4 15.7 %collective-permute-start.4 = (bf16[1056,128]{1,0:T(8,128)(2,1)S(1)}, bf16[1056,128]{1,0:T(8,128)(2,1)S(1)}, u32[]{:S(2)}, u32[]{:S(2)}) collective-permute-start(bf16[1056,128]{1,0:T(8,128)(2,1)S(1)} %pad_maximum_fusion.refs_0_), channel_id=1, source_target_pairs={{0,4},{2,6},{4,0},{6,2},{1,5},{3,7},{5,1},{7,3},{8,12},{10,14},{12... | collective-permute-start | bytes 811016 | tf_op jit(solution)/shard_map/ppermute | solution.py:426
  29.1 0.8 copy-start
  29.9 0.8 copy-start.2

commit v3 on v2

v3 whole, which is shorter than its diff:
```python
import functools

import jax
import jax.numpy as jnp
from jax import lax
from jax.experimental import pallas as pl
from jax.experimental.pallas import tpu as pltpu
from jax.sharding import Mesh
from jax.sharding import PartitionSpec as P

LOW = -1e30
LOG2E = 1.4426950408889634
LN2 = 0.6931471805599453
TILE = 256
HEAD = 128
FEAT = 256
PIECE = 128
MARK_ROW = 512
LISTED = 64
GROUPS = ((0,), (1, 3), (2,))
MARKS = 32
CHUNKS = (0, 1, 3, 2)


def nn(a, b):
    return lax.dot_general(a, b, (((1,), (0,)), ((), ())), preferred_element_type=jnp.float32)


def nt(a, b):
    return lax.dot_general(a, b, (((1,), (1,)), ((), ())), preferred_element_type=jnp.float32)


def fold(a):
    return a.reshape(a.shape[0] // 8, 8, a.shape[1])


def place():
    return tuple(lax.axis_index(name) for name in ("x", "y", "z", "c"))


def rotate_kernel(
    pos_hbm, q_hbm, k_hbm, mask_hbm, wq_hbm, wk_hbm,
    q_out, k_out, wq_out, wk_out,
    lines_ref, values_ref, mask_ref, sems,
):
    x, y, z, c = place()
    pieces = ((y * 8 + z) * 8 + x * 2 + c, (x * 2 + c) * 32 + y * 8 + z)
    copies = [
        pltpu.make_async_copy(pos_hbm.at[pieces[0] // 8], lines_ref.at[0], sems.at[0]),
        pltpu.make_async_copy(pos_hbm.at[pieces[1] // 8], lines_ref.at[1], sems.at[1]),
        pltpu.make_async_copy(q_hbm, values_ref.at[0], sems.at[2]),
        pltpu.make_async_copy(k_hbm, values_ref.at[1], sems.at[3]),
        pltpu.make_async_copy(mask_hbm, mask_ref, sems.at[4]),
        pltpu.make_async_copy(wq_hbm, wq_out, sems.at[5]),
        pltpu.make_async_copy(wk_hbm, wk_out, sems.at[6]),
    ]
    for copy in copies:
        copy.start()
    row = lax.broadcasted_iota(jnp.int32, (8, PIECE), 0)
    base = jnp.ones((8, PIECE), jnp.float32)
    for n in range(1, 8):
        base = jnp.where(row == n, jnp.float32(10000.0 ** (-n / 64)), base)
    frequency = jnp.concatenate(
        [base * jnp.float32(10000.0 ** (-8 * n / 64)) for n in range(8)], 0
    )
    for copy in copies:
        copy.wait()

    def turn(n):
        line = jnp.sum(jnp.where(row == pieces[n] % 8, lines_ref[n], 0), 0, keepdims=True)
        angles = line.astype(jnp.float32) * frequency
        both = jnp.transpose(jnp.concatenate([jnp.cos(angles), jnp.sin(angles)], 0))
        other = pltpu.roll(both, 64, 1)
        low = lax.broadcasted_iota(jnp.int32, (PIECE, HEAD), 1) < 64
        values = values_ref[n].astype(jnp.float32)
        return (
            values * jnp.where(low, both, other)
            + pltpu.roll(values, 64, 1) * jnp.where(low, -other, both)
        ).astype(jnp.bfloat16)

    own_q = turn(0)
    own_k = turn(1)
    marks = mask_ref[...].astype(jnp.float32)
    marks = jnp.concatenate([marks, jnp.zeros((4, 112), jnp.float32)], 1)
    marks = jnp.concatenate([marks, jnp.zeros((12, HEAD), jnp.float32)], 0).astype(jnp.bfloat16)
    q_out[:PIECE] = own_q
    q_out[PIECE:] = marks
    for n in range(8):
        k_out[n] = own_k


def features(weight_t, rows):
    mapped = nt(weight_t, rows)
    up = jnp.exp(mapped - jnp.max(mapped, 0, keepdims=True))
    down = jnp.exp(jnp.min(mapped, 0, keepdims=True) - mapped)
    up = up * (1.0 / jnp.sum(up, 0, keepdims=True))
    down = down * (1.0 / jnp.sum(down, 0, keepdims=True))
    return jnp.concatenate([up, down], axis=0)


def turned(a):
    return jnp.transpose(a.astype(jnp.float32)).astype(jnp.bfloat16)


def not_after():
    shape = (TILE, TILE)
    return lax.broadcasted_iota(jnp.int32, shape, 0) <= lax.broadcasted_iota(jnp.int32, shape, 1)


def listed(marks, chunks, full, corner):
    x, y, z, c = place()
    spare = len(chunks) * 16
    counts = [jnp.int32(0), jnp.int32(0)]
    for n, chunk in enumerate(chunks):
        first_tile = ((x + 4 - chunk) % 4) * 32 + c * 16 + y * 4
        for stripe in range(4):
            row_tile = stripe * 32 + z * 4 + x
            back = (y + 4 - stripe) % 4
            row = (back ^ (back // 2)) * 8 + x
            for sub in range(4):
                live = marks[n, row, y * 4 + sub] > 0
                kinds = (first_tile + sub < row_tile, first_tile + sub == row_tile)
                for which, (kind, tiles) in enumerate(zip(kinds, (full, corner))):
                    tiles[counts[which]] = (n * 4 + sub) * 4 + stripe
                    counts[which] = counts[which] + (live & kind).astype(jnp.int32)
    for count, tiles in zip(counts, (full, corner)):
        for n in range(3):
            tiles[count + n] = spare
        tiles[LISTED - 1] = count


def in_pairs(tiles, begin, finish, zero):
    count = tiles[LISTED - 1]

    def pair(n, ahead):
        here, there, after = (tiles[2 * n + step] for step in range(3))
        other = begin(there, 1)
        finish(here, 0, ahead)
        ahead = begin(after, 0)
        finish(there, 1, other)
        return ahead

    lax.fori_loop(0, (count + 1) // 2, pair, begin(tiles[0], 0))


def first_kernel(chunks, *refs):
    count = len(chunks)
    opens, closes = 0 in chunks, 2 in chunks
    spare = count * 16
    refs = list(refs)
    take = lambda number: [refs.pop(0) for _ in range(number)]
    k_refs = take(count + closes)
    (wk_ref,) = take(1)
    if opens:
        wq_ref, *q_refs = take(5)
    else:
        old_run, q_turned, qf_low = take(3)
    run, top_ref, u_ref, kfeat_ref, kft_ref, keys_ref, full, corner = take(8)
    if opens:
        q_turned, qf_low, qfeat_ref, rows_ref, dk_ref, dq_ref = take(6)
    if closes:
        (stats_ref,) = take(1)
    raw_a, raw_b, kf_ref, staged, marks, sems = refs
    scale = LOG2E * HEAD**-0.5
    x, y, z, c = place()
    fetched = []
    for n in range(count):
        staged[n] = k_refs[n][MARK_ROW : MARK_ROW + MARKS, :].astype(jnp.float32).astype(jnp.int32)
        fetched.append(pltpu.make_async_copy(staged.at[n], marks.at[n], sems.at[n]))
        fetched[-1].start()
    wk_t = turned(wk_ref[...])
    if opens:
        wq_t = turned(wq_ref[...])
        for n, q_ref in enumerate(q_refs):
            stripe = (y + 4 - CHUNKS[n]) % 4
            rows_ref[stripe, c] = q_ref[0, :PIECE]
            rows_ref[stripe, 1 - c] = q_ref[1, :PIECE]
        for stripe in range(4):
            rows = rows_ref[stripe].reshape(TILE, HEAD)
            q_turned[stripe] = turned(rows)
            feat = features(wq_t, rows)
            qfeat_ref[stripe] = feat
            qf_low[stripe] = feat.astype(jnp.bfloat16)
        run[0] = jnp.full((5, 8, TILE), LOW, jnp.float32)
        for n in (1, 2, 3):
            run[n] = jnp.zeros((5, 8, TILE), jnp.float32)
        for n in range(17):
            dk_ref[n] = jnp.zeros((FEAT, TILE), jnp.float32)
        for n in range(5):
            dq_ref[n] = jnp.zeros((FEAT, TILE), jnp.float32)
    else:
        run[...] = old_run[...]

    for n in range(count):
        for sub in range(4):
            if closes and chunks[n] == 2 and sub >= 2:
                keys = k_refs[n + 1][(sub - 2) * TILE : (sub - 1) * TILE, :]
            else:
                start = sub * TILE + (MARKS if sub >= 2 else 0)
                keys = k_refs[n][start : start + TILE, :]
            keys_ref[n * 4 + sub] = keys
            feat = features(wk_t, keys)
            kfeat_ref[n * 4 + sub] = feat
            low = feat.astype(jnp.bfloat16)
            kft_ref[n * 4 + sub] = low
            kf_ref[n * 4 + sub] = jnp.transpose(low)
    for copy in fetched:
        copy.wait()
    listed(marks, chunks, full, corner)

    def begin(tile, side, cut=False):
        raw = nn(keys_ref[tile // 4], q_turned[tile % 4])
        if cut:
            raw = jnp.where(not_after(), raw, LOW)
        (raw_b if side else raw_a)[...] = raw
        top = jnp.max(jnp.max(fold(raw), 0), 0, keepdims=True) * scale
        return jnp.broadcast_to(top, (8, TILE))

    def finish(tile, side, top, cut=False):
        student = nn(kf_ref[tile // 4], qf_low[tile % 4])
        if cut:
            norm = jnp.sum(fold(jnp.where(not_after(), student, 0.0)), 0)
            student = jnp.where(not_after(), student, 1.0)
        else:
            norm = jnp.sum(fold(student), 0)
        t = fold((raw_b if side else raw_a)[...]) * scale - top[None]
        weight = jnp.exp2(t)
        log_student = jnp.log2(fold(student))
        u_ref[tile] = (t - log_student).reshape(TILE, TILE)
        total = jnp.sum(weight, 0)
        logs = jnp.sum(weight * log_student, 0)
        top_ref[tile] = top
        stripe = jnp.where(tile == spare, 4, tile % 4)
        old = run[0, stripe]
        new = jnp.maximum(old, top)
        left = jnp.exp2(old - new)
        right = jnp.exp2(top - new)
        run[0, stripe] = new
        run[1, stripe] = run[1, stripe] * left + total * right
        run[2, stripe] = run[2, stripe] * left + logs * right
        run[3, stripe] = run[3, stripe] + norm

    in_pairs(full, begin, finish, None)

    def corner_step(n, carry):
        tile = corner[n]
        finish(tile, 0, begin(tile, 0, True), True)
        return carry

    lax.fori_loop(0, corner[LISTED - 1], corner_step, 0)

    if closes:
        lines = [run[0, stripe][:1] for stripe in range(4)] + [
            jnp.sum(run[n, stripe], 0, keepdims=True) for n in (1, 2, 3) for stripe in range(4)
        ]
        lines = jnp.concatenate(lines, 0)
        for copy in range(8):
            stats_ref[copy] = lines


def split2(a):
    high = a.astype(jnp.bfloat16)
    low = (a - high.astype(jnp.float32)).astype(jnp.bfloat16)
    return jnp.concatenate([high, low], axis=0)


def weight_grad(feat, dfeat, rows):
    up, down = feat[:HEAD], feat[HEAD:]
    d1, d2 = dfeat[:HEAD], dfeat[HEAD:]
    dmapped = up * (d1 - jnp.sum(up * d1, 0, keepdims=True)) - down * (
        d2 - jnp.sum(down * d2, 0, keepdims=True)
    )
    parts = nn(split2(dmapped), rows)
    return parts[HEAD:] + parts[:HEAD]


def second_kernel(st_ref, q_ref, qfeat_ref, qf_low, dk_in, dq_in, *refs):
    refs = list(refs)
    groups = [[refs.pop(0) for _ in range(7)] for _ in GROUPS]
    loss_ref, grad_ref, dk_ref, dq_ref, lines, losses, g_a, g_b = refs
    x, y, z, c = place()
    top = st_ref[0, 0:4]
    for n in range(1, 8):
        top = jnp.maximum(top, st_ref[n, 0:4])
    total = jnp.zeros_like(top)
    logs = jnp.zeros_like(top)
    norm = jnp.zeros_like(top)
    for n in range(8):
        factor = jnp.exp2(st_ref[n, 0:4] - top)
        total = total + st_ref[n, 4:8] * factor
        logs = logs + st_ref[n, 8:12] * factor
        norm = norm + st_ref[n, 12:16]
    loss = jnp.log(norm) - (logs / total) * LN2
    for stripe in range(4):
        for half in range(2):
            losses[half, stripe] = jnp.broadcast_to(
                loss[stripe : stripe + 1, half * 128 : half * 128 + 128], (8, 128)
            )
    loss_ref[...] = losses[c, y][:1]
    base = (1.0 / norm) * (1.0 / 32768.0)
    shift = top + jnp.log2(total) + 15.0
    for stripe in range(4):
        lines[0, stripe] = jnp.broadcast_to(base[stripe : stripe + 1], (8, TILE))
        lines[1, stripe] = jnp.broadcast_to(shift[stripe : stripe + 1], (8, TILE))

    gk = jnp.zeros((HEAD, HEAD), jnp.float32)
    offset = 0
    for chunks, group in zip(GROUPS, groups):
        top_ref, u_ref, kfeat_ref, kft_ref, keys_ref, full, corner = group
        spare = 16 * len(chunks)

        def begin(tile, side, cut=False):
            stripe = tile % 4
            less = lines[1, stripe] - top_ref[tile]
            grad = lines[0, stripe][None] - jnp.exp2(fold(u_ref[tile]) - less[None])
            grad = grad.reshape(TILE, TILE)
            if cut:
                grad = jnp.where(not_after(), grad, 0.0)
            (g_b if side else g_a)[...] = grad.astype(jnp.bfloat16)
            return 0

        def finish(tile, side, ahead):
            grad = (g_b if side else g_a)[...]
            key_tile = jnp.where(tile == spare, 16, offset + tile // 4)
            stripe = jnp.where(tile == spare, 4, tile % 4)
            dq_ref[stripe] += nn(kft_ref[tile // 4], grad)
            dk_ref[key_tile] += nt(qf_low[tile % 4], grad)

        in_pairs(full, begin, finish, None)

        def corner_step(n, carry):
            tile = corner[n]
            begin(tile, 0, True)
            finish(tile, 0, 0)
            return carry

        lax.fori_loop(0, corner[LISTED - 1], corner_step, 0)
        for key_tile in range(4 * len(chunks)):
            gk = gk + weight_grad(
                kfeat_ref[key_tile], dk_ref[offset + key_tile], keys_ref[key_tile]
            )
        offset += 4 * len(chunks)

    gq = jnp.zeros((HEAD, HEAD), jnp.float32)
    for stripe in range(4):
        gq = gq + weight_grad(
            qfeat_ref[stripe], dq_ref[stripe], q_ref[stripe].reshape(TILE, HEAD)
        )
    grad_ref[0] = jnp.transpose(gq)
    grad_ref[1] = jnp.transpose(gk)


def f32(*shape):
    return jax.ShapeDtypeStruct(shape, jnp.float32)


def b16(*shape):
    return jax.ShapeDtypeStruct(shape, jnp.bfloat16)


def params(work, limit=12):
    return dict(
        compiler_params=pltpu.CompilerParams(vmem_limit_bytes=limit << 20),
        cost_estimate=pl.CostEstimate(
            flops=int(work * 1e8), bytes_accessed=int(work * 1e5), transcendentals=int(work * 1e5)
        ),
    )


VMEM = pl.BlockSpec(memory_space=pltpu.VMEM)
SMEM = pl.BlockSpec(memory_space=pltpu.SMEM)


def first_call(chunks, loads, w_key, *others):
    count = len(chunks)
    outs = [
        f32(4, 5, 8, TILE),
        f32(16 * count + 1, 8, TILE),
        f32(16 * count + 1, TILE, TILE),
        f32(4 * count, FEAT, TILE),
        b16(4 * count + 1, FEAT, TILE),
        b16(4 * count + 1, TILE, HEAD),
        jax.ShapeDtypeStruct((LISTED,), jnp.int32),
        jax.ShapeDtypeStruct((LISTED,), jnp.int32),
    ]
    if 0 in chunks:
        outs += [
            b16(4, HEAD, TILE),
            b16(4, FEAT, TILE),
            f32(4, FEAT, TILE),
            b16(4, 2, PIECE, HEAD),
            f32(17, FEAT, TILE),
            f32(5, FEAT, TILE),
        ]
    if 2 in chunks:
        outs += [f32(8, 16, TILE)]
    return pl.pallas_call(
        functools.partial(first_kernel, chunks),
        out_shape=tuple(outs),
        in_specs=[VMEM] * (len(loads) + 1 + len(others)),
        out_specs=tuple(SMEM if n in (6, 7) else VMEM for n in range(len(outs))),
        scratch_shapes=[
            pltpu.VMEM((TILE, TILE), jnp.float32),
            pltpu.VMEM((TILE, TILE), jnp.float32),
            pltpu.VMEM((4 * count + 1, TILE, FEAT), jnp.bfloat16),
            pltpu.VMEM((count, MARKS, HEAD), jnp.int32),
            pltpu.SMEM((count, MARKS, HEAD), jnp.int32),
            pltpu.SemaphoreType.DMA((count,)),
        ],
        name="first%d" % chunks[0],
        **params(20 * count),
    )(*loads, w_key, *others)


def exchanged(copies, axes):
    return lax.all_to_all(copies, axes, split_axis=0, concat_axis=0, tiled=True)


def local(queries, keys, positions, tile_mask, w_query, w_key):
    hbm = pl.BlockSpec(memory_space=pltpu.HBM)
    vmem = pl.BlockSpec(memory_space=pltpu.VMEM)
    q_own, k_copies, w_query, w_key = pl.pallas_call(
        rotate_kernel,
        out_shape=(
            b16(PIECE + 16, HEAD), b16(8, PIECE, HEAD), b16(HEAD, HEAD), b16(HEAD, HEAD)
        ),
        in_specs=[hbm] * 6,
        out_specs=(vmem,) * 4,
        scratch_shapes=[
            pltpu.VMEM((2, 8, PIECE), jnp.int32),
            pltpu.VMEM((2, PIECE, HEAD), jnp.bfloat16),
            pltpu.VMEM((4, 16), jnp.int32),
            pltpu.SemaphoreType.DMA((7,)),
        ],
        compiler_params=pltpu.CompilerParams(vmem_limit_bytes=60 << 20),
        name="rotate",
    )(
        positions.reshape(32, 8, PIECE),
        queries.reshape(PIECE, HEAD),
        keys.reshape(PIECE, HEAD),
        tile_mask,
        w_query[0],
        w_key[0],
    )
    k_near = exchanged(k_copies, "z").reshape(4 * TILE, HEAD)
    other = lax.ppermute(q_own, "c", [(0, 1), (1, 0)])
    pair = jnp.stack([q_own, other])
    pairs = [pair] + [
        lax.ppermute(pair, "y", [(i, (i + step) % 4) for i in range(4)]) for step in (1, 3, 2)
    ]
    marks = jnp.stack([near[:, PIECE : PIECE + 4] for near in pairs]).reshape(MARKS, HEAD)
    half = 2 * TILE
    load = jnp.concatenate([k_near[:half], marks, k_near[half:]], 0)
    after = [(i, (i + 1) % 4) for i in range(4)]
    before = [(i, (i + 3) % 4) for i in range(4)]
    lower = lax.ppermute(load, "x", after)
    upper = lax.ppermute(load, "x", before)
    far = (
        lax.ppermute(lower[: half + MARKS], "x", after),
        lax.ppermute(upper[half + MARKS :], "x", before),
    )
    run, *first, q_turned, qf_low, qfeat, q_rows, dk, dq = first_call(
        (0,), [load], w_key, w_query, *pairs
    )
    run, *second = first_call((1, 3), [lower, upper], w_key, run, q_turned, qf_low)
    run, *third, stats = first_call((2,), far, w_key, run, q_turned, qf_low)
    stats = exchanged(stats, ("y", "c"))
    loss, grads, _, _ = pl.pallas_call(
        second_kernel,
        out_shape=(f32(1, PIECE), f32(2, HEAD, HEAD), f32(17, FEAT, TILE), f32(5, FEAT, TILE)),
        in_specs=[VMEM] * 6 + ([VMEM] * 5 + [SMEM] * 2) * 3,
        out_specs=(VMEM,) * 4,
        scratch_shapes=[
            pltpu.VMEM((2, 4, 8, TILE), jnp.float32),
            pltpu.VMEM((2, 4, 8, 128), jnp.float32),
            pltpu.VMEM((TILE, TILE), jnp.bfloat16),
            pltpu.VMEM((TILE, TILE), jnp.bfloat16),
        ],
        input_output_aliases={4: 2, 5: 3},
        name="second",
        **params(100),
    )(stats, q_rows, qfeat, qf_low, dk, dq, *first, *second, *third)
    wide = ("y", "x", "c")
    part = exchanged(grads.reshape(32, 8, HEAD), wide).sum(0)
    part = exchanged(jnp.broadcast_to(part, (8, 8, HEAD)), "z").sum(0)
    whole = exchanged(jnp.broadcast_to(part, (32, 8, HEAD)), wide).reshape(2, 1, HEAD, HEAD)
    return loss.reshape(1, 1, PIECE), whole[0], whole[1]


def solution(mesh):
    finer = Mesh(mesh.devices.reshape(4, 8, 4, 2), ("y", "z", "x", "c"))
    qb, kb = ("y", "z"), ("x", "c")
    placed = (P(qb, kb, None, None), P(kb, qb, None, None), P(), P(qb, kb), P(), P())
    return jax.shard_map(
        local, mesh=finer, in_specs=placed, out_specs=(P(qb, kb, None), P(), P()), check_vma=False
    )
```

time: 119 us -> 103 us (0.87)
  Pallas kernels: 31.7 us -> 20.8 us
  blocking collectives: 57.5 us -> 50.2 us
    pallas_call x4, Pallas kernels: 29.7 us -> 18.8 us  [the longest x3 12.5 us: first_call(): pl.pallas_call(functools.partial(first_kernel, chunks), out_shape=tuple(o...]
    all_to_all x4, blocking collectives: 57.5 us -> 50.2 us  [exchanged(): return lax.all_to_all(copies, axes, split_axis=0, concat_axis=0, tiled=True)]
    ppermute x3 -> x4, starting transfers between devices: 4.29 us -> 5.08 us  [the longest x1 2.56 us: local(): upper = lax.ppermute(load, 'x', before)]
  transfers between devices with their start and end apart: 8 -> 9, of which waited for: 4 -> 4; matrix products, arithmetic and copies ran while one was open for 1% -> 1% of each run, Pallas kernels for 10% -> 9%
where the time goes in v3:
time: 103 us; the launch traced here: 102 us
  blocking collectives  50.2 us (49%)
  Pallas kernels  20.8 us (20%)
  starting transfers between devices  19.2 us (19%)
  waiting for transfers between devices  7.29 us (7%)
  local copies, waits for them, and re-layouts  2.25 us (2%)
  other arithmetic  1.55 us (2%)
    all_to_all x4, blocking collectives, exchanged(): return lax.all_to_all(copies, axes, split_axis=0, concat_axis=0, tiled=True)  50.2 us
    pallas_call x3, Pallas kernels, first_call(): pl.pallas_call(functools.partial(first_kernel, chunks), out_shape=tuple(o...  12.5 us
    all_to_all x1, starting transfers between devices, exchanged(): return lax.all_to_all(copies, axes, split_axis=0, concat_axis=0, tiled=True)  6.48 us
    pallas_call x1, Pallas kernels, local(): pl.pallas_call(second_kernel, out_shape=(f32(1, PIECE), f32(2, HEAD, HEAD...  6.25 us
    ppermute x3, starting transfers between devices, local(): lax.ppermute(pair, 'y', [(i, (i + step) % 4) for i in range(4)])  4.38 us
    all_to_all x1, waiting for transfers between devices, exchanged(): return lax.all_to_all(copies, axes, split_axis=0, concat_axis=0, tiled=True)  3.39 us
    ppermute x1, starting transfers between devices, local(): other = lax.ppermute(q_own, 'c', [(0, 1), (1, 0)])  3.29 us
    ppermute x3, waiting for transfers between devices, local(): lax.ppermute(pair, 'y', [(i, (i + step) % 4) for i in range(4)])  3.08 us
  transfers between devices with their start and end apart: 9, of which 4 were waited for; matrix products, arithmetic and copies ran while one was open for 1% of the time, Pallas kernels for 9%

profile of v3, /device:TPU:1, one launch (start us, length us, event | category | flops | bytes accessed | tf_op | source)
XLA Modules:
  0.0 102.1 jit_solution(859507105405537122)
XLA Ops:
  0.6 2.1 %rotate.1 = (bf16[144,128]{1,0:T(8,128)(2,1)}, bf16[8,128,128]{2,1,0:T(8,128)(2,1)}, bf16[128,128]{1,0:T(8,128)(2,1)}, bf16[128,128]{1,0:T(8,128)(2,1)}) custom-call(s32[32,8,128]{2,1,0:T(8,128)} %bitcast.31, bf16[128,128]{1,0:T(8,128)(2,1)} %bitcast.33, bf16[128,128]{1,0:T(8,128)(2,1)} %bitcast.34, s32[4,16]{1,0:T(4,128)} %mask_hbm.1, ...), custom_call_target="tpu_custom_call" | custom-call | tf_op jit(solution)/shard_map/rotate/pallas_call | solution.py:422
  2.7 3.3 %collective-permute-start = (bf16[144,128]{1,0:T(8,128)(2,1)}, bf16[144,128]{1,0:T(8,128)(2,1)S(1)}, u32[]{:S(2)}, u32[]{:S(2)}) collective-permute-start(bf16[144,128]{1,0:T(8,128)(2,1)} %get-tuple-element.40), channel_id=1, source_target_pairs={{0,1},{1,0},{2,3},{3,2},{4,5},{5,4},{6,7},{7,6},{8,9},{9,8},{10,11... | collective-permute-start | bytes 110600 | tf_op jit(solution)/shard_map/ppermute | solution.py:446
  6.0 6.5 %all-to-all-start = ((bf16[8,128,128]{2,1,0:T(8,128)(2,1)}), bf16[8,128,128]{2,1,0:T(8,128)(2,1)S(1)}, u32[]{:S(2)}, u32[]{:S(2)}) async-start(bf16[8,128,128]{2,1,0:T(8,128)(2,1)} %get-tuple-element.39), calls=%async_computation | async-start | bytes 524288 | tf_op jit(solution)/shard_map/all_to_all | solution.py:416
  12.5 0.0 collective-permute-done
  12.5 0.8 pad_maximum_fusion.1.refs_3_
  13.3 2.9 %collective-permute-start.3 = (bf16[2,144,128]{2,1,0:T(8,128)(2,1)S(1)}, bf16[2,144,128]{2,1,0:T(8,128)(2,1)S(1)}, u32[]{:S(2)}, u32[]{:S(2)}) collective-permute-start(bf16[2,144,128]{2,1,0:T(8,128)(2,1)S(1)} %pad_maximum_fusion.1.refs_3_), channel_id=1, source_target_pairs={{0,128},{64,192},{128,0},{192,64},{1,129},{65,193},{129,1},{193,65... | collective-permute-start | bytes 221192 | tf_op jit(solution)/shard_map/ppermute | solution.py:449
  16.2 0.8 collective-permute-start.2
  16.9 0.7 collective-permute-start.1
  17.6 0.7 fusion.1
  18.3 0.0 collective-permute-done.3.refs_6_
  18.3 2.1 %collective-permute-done.2.refs_5_ = bf16[2,144,128]{2,1,0:T(8,128)(2,1)S(1)} collective-permute-done((bf16[2,144,128]{2,1,0:T(8,128)(2,1)S(1)}, bf16[2,144,128]{2,1,0:T(8,128)(2,1)S(1)}, u32[]{:S(2)}, u32[]{:S(2)}) %collective-permute-start.2) | collective-permute-done | bytes 73760 | tf_op jit(solution)/shard_map/ppermute | solution.py:449
  20.4 1.0 collective-permute-done.1.refs_4_
  21.4 3.4 %all-to-all-done = bf16[8,128,128]{2,1,0:T(8,128)(2,1)S(1)} async-done(((bf16[8,128,128]{2,1,0:T(8,128)(2,1)}), bf16[8,128,128]{2,1,0:T(8,128)(2,1)S(1)}, u32[]{:S(2)}, u32[]{:S(2)}) %all-to-all-start) | async-done | bytes 262176 | tf_op jit(solution)/shard_map/all_to_all | solution.py:416
  24.9 2.6 %collective-permute-start.6 = (bf16[1056,128]{1,0:T(8,128)(2,1)S(1)}, bf16[1056,128]{1,0:T(8,128)(2,1)S(1)}, u32[]{:S(2)}, u32[]{:S(2)}) collective-permute-start(bf16[1056,128]{1,0:T(8,128)(2,1)S(1)} %pad_maximum_fusion.refs_0_), channel_id=1, source_target_pairs={{0,6},{2,0},{4,2},{6,4},{1,7},{3,1},{5,3},{7,5},{8,14},{10,8},{12,... | collective-permute-start | bytes 811016 | tf_op jit(solution)/shard_map/ppermute | solution.py:457
  27.4 0.0 collective-permute-start.4
  27.4 0.8 copy-done
  28.2 0.8 copy-done.2
  29.0 4.9 %first0.1 = (f32[4,5,8,256]{3,2,1,0:T(8,128)S(1)}, f32[17,8,256]{2,1,0:T(8,128)S(1)}, f32[17,256,256]{2,1,0:T(8,128)S(1)}, f32[4,256,256]{2,1,0:T(8,128)S(1)}, b...) custom-call(bf16[1056,128]{1,0:T(8,128)(2,1)S(1)} %pad_maximum_fusio, ...), custom_call_target="tpu_custom_call" | custom-call | flops 2000000000 | bytes 2000000 | tf_op jit(solution)/shard_map/first0/pallas_call | solution.py:397
  33.8 0.0 collective-permute-done.6.refs_1_
  33.9 2.4 %collective-permute-start.7 = (bf16[512,128]{1,0:T(8,128)(2,1)S(1)}, bf16[512,128]{1,0:T(8,128)(2,1)S(1)}, u32[]{:S(2)}, u32[]{:S(2)}) collective-permute-start(bf16[512,128]{1,0:T(8,128)(2,1)S(1)} %slice.58), channel_id=1, source_target_pairs={{0,6},{2,0},{4,2},{6,4},{1,7},{3,1},{5,3},{7,5},{8,14},{10,8},{12,... | collective-permute-start | bytes 393224 | tf_op jit(solution)/shard_map/ppermute | solution.py:460
  36.3 0.0 collective-permute-done.4.refs_0_
  36.3 0.1 collective-permute-start.5
  36.4 4.3 %first1.1 = (f32[4,5,8,256]{3,2,1,0:T(8,128)S(1)}, f32[33,8,256]{2,1,0:T(8,128)S(1)}, f32[33,256,256]{2,1,0:T(8,128)S(1)}, f32[8,256,256]{2,1,0:T(8,128)S(1)}, b...) custom-call(bf16[1056,128]{1,0:T(8,128)(2,1)S(1)} %collective-permute-done.4., ...), custom_call_target="tpu_custom_call" | custom-call | flops 4000000000 | bytes 4000000 | tf_op jit(solution)/shard_map/first1/pallas_call | solution.py:397
  40.7 0.0 collective-permute-done.7.refs_1_
  40.7 0.8 collective-permute-done.5.refs_0_
  41.5 3.4 %first2.1 = (f32[4,5,8,256]{3,2,1,0:T(8,128)}, f32[17,8,256]{2,1,0:T(8,128)S(1)}, f32[17,256,256]{2,1,0:T(8,128)S(1)}, f32[4,256,256]{2,1,0:T(8,128)S(1)}, bf16[...) custom-call(bf16[544,128]{1,0:T(8,128)(2,1)S(1)} %collective-permute, ...), custom_call_target="tpu_custom_call" | custom-call | flops 2000000000 | bytes 2000000 | tf_op jit(solution)/shard_map/first2/pallas_call | solution.py:397
  44.9 12.1 %all_to_all.25.st_ref = f32[8,16,256]{2,1,0:T(8,128)S(1)} all-to-all(f32[8,16,256]{2,1,0:T(8,128)S(1)} %get-tuple-element.47), channel_id=1, replica_groups=mesh['y'=4,'z'=8,'x'=4,'c'=2] {'y','c'}, dimensions={0} | all-to-all | bytes 262144 | tf_op jit(solution)/shard_map/all_to_all | solution.py:416
  57.0 6.2 %second.1 = (f32[1,128]{1,0:T(1,128)}, f32[2,128,128]{2,1,0:T(8,128)S(1)}, f32[17,256,256]{2,1,0:T(8,128)S(1)}, f32[5,256,256]{2,1,0:T(8,128)S(1)}) custom-call(f32[8,16,256]{2,1,0:T(8,128)S(1)} %all_to_all.25.st_ref, bf16[4,2,128,128]{3,2,1,0:T(8,128)(2,1)S(1)} %get-tuple-element.48.q_ref, ...), custom_call_target="tpu_custom_call", output_to_operand_aliasing={{2}: (4, {}), {3}: (5, {})} | custom-call | flops 10000000000 | bytes 10000000 | tf_op jit(solution)/shard_map/second/pallas_call | solution.py:468
  63.2 15.2 %all_to_all.26 = f32[32,8,128]{2,1,0:T(8,128)S(1)} all-to-all(f32[32,8,128]{2,1,0:T(8,128)S(1)} %bitcast.24), channel_id=1, replica_groups=mesh['y'=4,'z'=8,'x'=4,'c'=2] {'y','x','c'}, dimensions={0} | all-to-all | bytes 262144 | tf_op jit(solution)/shard_map/all_to_all | solution.py:416
  78.5 10.3 %all_to_all.27 = f32[8,8,128]{2,1,0:T(8,128)S(1)} all-to-all(f32[8,8,128]{2,1,0:T(8,128)S(1)} %broadcast_in_dim.6), channel_id=1, replica_groups=mesh['y'=4,'z'=8,'x'=4,'c'=2] {'z'}, dimensions={0} | all-to-all | bytes 65536 | tf_op jit(solution)/shard_map/all_to_all | solution.py:416
  88.8 12.6 %all_to_all.28 = f32[32,8,128]{2,1,0:T(8,128)S(1)} all-to-all(f32[32,8,128]{2,1,0:T(8,128)S(1)} %broadcast_in_dim.7), channel_id=1, replica_groups=mesh['y'=4,'z'=8,'x'=4,'c'=2] {'y','x','c'}, dimensions={0} | all-to-all | bytes 262144 | tf_op jit(solution)/shard_map/all_to_all | solution.py:416
  101.4 0.7 slice_bitcast_fusion
  (16 shorter events, 0.2 us)
Async XLA Ops:
  2.7 9.8 %collective-permute-start = (bf16[144,128]{1,0:T(8,128)(2,1)}, bf16[144,128]{1,0:T(8,128)(2,1)S(1)}, u32[]{:S(2)}, u32[]{:S(2)}) collective-permute-start(bf16[144,128]{1,0:T(8,128)(2,1)} %get-tuple-element.40), channel_id=1, source_target_pairs={{0,1},{1,0},{2,3},{3,2},{4,5},{5,4},{6,7},{7,6},{8,9},{9,8},{10,11... | collective-permute-start | bytes 110600 | tf_op jit(solution)/shard_map/ppermute | solution.py:446
  6.0 18.8 %all-to-all-start = ((bf16[8,128,128]{2,1,0:T(8,128)(2,1)}), bf16[8,128,128]{2,1,0:T(8,128)(2,1)S(1)}, u32[]{:S(2)}, u32[]{:S(2)}) async-start(bf16[8,128,128]{2,1,0:T(8,128)(2,1)} %get-tuple-element.39), calls=%async_computation | async-start | bytes 524288 | tf_op jit(solution)/shard_map/all_to_all | solution.py:416
  13.3 5.1 %collective-permute-start.3 = (bf16[2,144,128]{2,1,0:T(8,128)(2,1)S(1)}, bf16[2,144,128]{2,1,0:T(8,128)(2,1)S(1)}, u32[]{:S(2)}, u32[]{:S(2)}) collective-permute-start(bf16[2,144,128]{2,1,0:T(8,128)(2,1)S(1)} %pad_maximum_fusion.1.refs_3_), channel_id=1, source_target_pairs={{0,128},{64,192},{128,0},{192,64},{1,129},{65,193},{129,1},{193,65... | collective-permute-start | bytes 221192 | tf_op jit(solution)/shard_map/ppermute | solution.py:449
  16.2 4.3 %collective-permute-start.2 = (bf16[2,144,128]{2,1,0:T(8,128)(2,1)S(1)}, bf16[2,144,128]{2,1,0:T(8,128)(2,1)S(1)}, u32[]{:S(2)}, u32[]{:S(2)}) collective-permute-start(bf16[2,144,128]{2,1,0:T(8,128)(2,1)S(1)} %pad_maximum_fusion.1.refs_3_), channel_id=1, source_target_pairs={{0,192},{64,0},{128,64},{192,128},{1,193},{65,1},{129,65},{193,129... | collective-permute-start | bytes 221192 | tf_op jit(solution)/shard_map/ppermute | solution.py:449
  16.9 4.5 %collective-permute-start.1 = (bf16[2,144,128]{2,1,0:T(8,128)(2,1)S(1)}, bf16[2,144,128]{2,1,0:T(8,128)(2,1)S(1)}, u32[]{:S(2)}, u32[]{:S(2)}) collective-permute-start(bf16[2,144,128]{2,1,0:T(8,128)(2,1)S(1)} %pad_maximum_fusion.1.refs_3_), channel_id=1, source_target_pairs={{0,64},{64,128},{128,192},{192,0},{1,65},{65,129},{129,193},{193,1... | collective-permute-start | bytes 221192 | tf_op jit(solution)/shard_map/ppermute | solution.py:449
  21.4 15.0 %copy-start.1 = (bf16[128,128]{1,0:T(8,128)(2,1)S(1)}, bf16[128,128]{1,0:T(8,128)(2,1)}, u32[]{:S(2)}) copy-start(bf16[128,128]{1,0:T(8,128)(2,1)} %get-tuple-element.41.refs_1_.refs_2_) | copy-start | bytes 98308
  24.9 9.0 %collective-permute-start.6 = (bf16[1056,128]{1,0:T(8,128)(2,1)S(1)}, bf16[1056,128]{1,0:T(8,128)(2,1)S(1)}, u32[]{:S(2)}, u32[]{:S(2)}) collective-permute-start(bf16[1056,128]{1,0:T(8,128)(2,1)S(1)} %pad_maximum_fusion.refs_0_), channel_id=1, source_target_pairs={{0,6},{2,0},{4,2},{6,4},{1,7},{3,1},{5,3},{7,5},{8,14},{10,8},{12,... | collective-permute-start | bytes 811016 | tf_op jit(solution)/shard_map/ppermute | solution.py:457
  27.4 8.9 %collective-permute-start.4 = (bf16[1056,128]{1,0:T(8,128)(2,1)S(1)}, bf16[1056,128]{1,0:T(8,128)(2,1)S(1)}, u32[]{:S(2)}, u32[]{:S(2)}) collective-permute-start(bf16[1056,128]{1,0:T(8,128)(2,1)S(1)} %pad_maximum_fusion.refs_0_), channel_id=1, source_target_pairs={{0,2},{2,4},{4,6},{6,0},{1,3},{3,5},{5,7},{7,1},{8,10},{10,12},{12... | collective-permute-start | bytes 811016 | tf_op jit(solution)/shard_map/ppermute | solution.py:456
  27.4 0.8 copy-start
  28.2 0.8 copy-start.2
  33.9 6.8 %collective-permute-start.7 = (bf16[512,128]{1,0:T(8,128)(2,1)S(1)}, bf16[512,128]{1,0:T(8,128)(2,1)S(1)}, u32[]{:S(2)}, u32[]{:S(2)}) collective-permute-start(bf16[512,128]{1,0:T(8,128)(2,1)S(1)} %slice.58), channel_id=1, source_target_pairs={{0,6},{2,0},{4,2},{6,4},{1,7},{3,1},{5,3},{7,5},{8,14},{10,8},{12,... | collective-permute-start | bytes 393224 | tf_op jit(solution)/shard_map/ppermute | solution.py:460
  36.3 5.2 %collective-permute-start.5 = (bf16[544,128]{1,0:T(8,128)(2,1)S(1)}, bf16[544,128]{1,0:T(8,128)(2,1)S(1)}, u32[]{:S(2)}, u32[]{:S(2)}) collective-permute-start(bf16[544,128]{1,0:T(8,128)(2,1)S(1)} %slice.57), channel_id=1, source_target_pairs={{0,2},{2,4},{4,6},{6,0},{1,3},{3,5},{5,7},{7,1},{8,10},{10,12},{12... | collective-permute-start | bytes 417800 | tf_op jit(solution)/shard_map/ppermute | solution.py:459

commit v4 on v3

--- a/solution.py
+++ b/solution.py
@@ -16,7 +16,9 @@
 FEAT = 256
 PIECE = 128
 MARK_ROW = 512
-LISTED = 64
+LISTED = 96
+SPARE = 64
+WIDTH = 4
 GROUPS = ((0,), (1, 3), (2,))
 MARKS = 32
 CHUNKS = (0, 1, 3, 2)
@@ -39,8 +41,8 @@
 
 
 def rotate_kernel(
-    pos_hbm, q_hbm, k_hbm, mask_hbm, wq_hbm, wk_hbm,
-    q_out, k_out, wq_out, wk_out,
+    pos_hbm, q_hbm, k_hbm, mask_hbm,
+    q_out, k_out,
     lines_ref, values_ref, mask_ref, sems,
 ):
     x, y, z, c = place()
@@ -51,8 +53,6 @@
         pltpu.make_async_copy(q_hbm, values_ref.at[0], sems.at[2]),
         pltpu.make_async_copy(k_hbm, values_ref.at[1], sems.at[3]),
         pltpu.make_async_copy(mask_hbm, mask_ref, sems.at[4]),
-        pltpu.make_async_copy(wq_hbm, wq_out, sems.at[5]),
-        pltpu.make_async_copy(wk_hbm, wk_out, sems.at[6]),
     ]
     for copy in copies:
         copy.start()
@@ -89,6 +89,11 @@
         k_out[n] = own_k
 
 
+def early_kernel(after, wq_ref, wk_ref, wq_out, wk_out):
+    wq_out[...] = turned(wq_ref[...])
+    wk_out[...] = turned(wk_ref[...])
+
+
 def features(weight_t, rows):
     mapped = nt(weight_t, rows)
     up = jnp.exp(mapped - jnp.max(mapped, 0, keepdims=True))
@@ -107,9 +112,8 @@
     return lax.broadcasted_iota(jnp.int32, shape, 0) <= lax.broadcasted_iota(jnp.int32, shape, 1)
 
 
-def listed(marks, chunks, full, corner):
+def listed(marks, chunks, offset, full, corner):
     x, y, z, c = place()
-    spare = len(chunks) * 16
     counts = [jnp.int32(0), jnp.int32(0)]
     for n, chunk in enumerate(chunks):
         first_tile = ((x + 4 - chunk) % 4) * 32 + c * 16 + y * 4
@@ -121,32 +125,31 @@
                 live = marks[n, row, y * 4 + sub] > 0
                 kinds = (first_tile + sub < row_tile, first_tile + sub == row_tile)
                 for which, (kind, tiles) in enumerate(zip(kinds, (full, corner))):
-                    tiles[counts[which]] = (n * 4 + sub) * 4 + stripe
+                    tiles[counts[which]] = (offset + n * 4 + sub) * 4 + stripe
                     counts[which] = counts[which] + (live & kind).astype(jnp.int32)
     for count, tiles in zip(counts, (full, corner)):
         for n in range(3):
-            tiles[count + n] = spare
+            tiles[count + n] = SPARE
         tiles[LISTED - 1] = count
 
 
-def in_pairs(tiles, begin, finish, zero):
+def in_groups(tiles, width, begin, finish):
+    def group(n, ahead):
+        here = [tiles[width * n + step] for step in range(width + 1)]
+        for step in range(width):
+            later = begin(here[step + 1], (step + 1) % width)
+            finish(here[step], step, ahead)
+            ahead = later
+        return ahead
+
     count = tiles[LISTED - 1]
-
-    def pair(n, ahead):
-        here, there, after = (tiles[2 * n + step] for step in range(3))
-        other = begin(there, 1)
-        finish(here, 0, ahead)
-        ahead = begin(after, 0)
-        finish(there, 1, other)
-        return ahead
-
-    lax.fori_loop(0, (count + 1) // 2, pair, begin(tiles[0], 0))
+    lax.fori_loop(0, (count + width - 1) // width, group, begin(tiles[0], 0))
 
 
 def first_kernel(chunks, *refs):
     count = len(chunks)
     opens, closes = 0 in chunks, 2 in chunks
-    spare = count * 16
+    offset = 4 * CHUNKS.index(chunks[0])
     refs = list(refs)
     take = lambda number: [refs.pop(0) for _ in range(number)]
     k_refs = take(count + closes)
@@ -155,7 +158,8 @@
         wq_ref, *q_refs = take(5)
     else:
         old_run, q_turned, qf_low = take(3)
-    run, top_ref, u_ref, kfeat_ref, kft_ref, keys_ref, full, corner = take(8)
+        take(4)
+    run, u_ref, kfeat_ref, kft_ref, keys_ref, full, corner = take(7)
     if opens:
         q_turned, qf_low, qfeat_ref, rows_ref, dk_ref, dq_ref = take(6)
     if closes:
@@ -168,9 +172,9 @@
         staged[n] = k_refs[n][MARK_ROW : MARK_ROW + MARKS, :].astype(jnp.float32).astype(jnp.int32)
         fetched.append(pltpu.make_async_copy(staged.at[n], marks.at[n], sems.at[n]))
         fetched[-1].start()
-    wk_t = turned(wk_ref[...])
+    wk_t = wk_ref[...]
     if opens:
-        wq_t = turned(wq_ref[...])
+        wq_t = wq_ref[...]
         for n, q_ref in enumerate(q_refs):
             stripe = (y + 4 - CHUNKS[n]) % 4
             rows_ref[stripe, c] = q_ref[0, :PIECE]
@@ -181,13 +185,11 @@
             feat = features(wq_t, rows)
             qfeat_ref[stripe] = feat
             qf_low[stripe] = feat.astype(jnp.bfloat16)
+        dk_ref[...] = jnp.zeros_like(dk_ref)
+        dq_ref[...] = jnp.zeros_like(dq_ref)
         run[0] = jnp.full((5, 8, TILE), LOW, jnp.float32)
         for n in (1, 2, 3):
             run[n] = jnp.zeros((5, 8, TILE), jnp.float32)
-        for n in range(17):
-            dk_ref[n] = jnp.zeros((FEAT, TILE), jnp.float32)
-        for n in range(5):
-            dq_ref[n] = jnp.zeros((FEAT, TILE), jnp.float32)
     else:
         run[...] = old_run[...]
 
@@ -198,15 +200,16 @@
             else:
                 start = sub * TILE + (MARKS if sub >= 2 else 0)
                 keys = k_refs[n][start : start + TILE, :]
-            keys_ref[n * 4 + sub] = keys
+            spot = offset + n * 4 + sub
+            keys_ref[spot] = keys
             feat = features(wk_t, keys)
-            kfeat_ref[n * 4 + sub] = feat
+            kfeat_ref[spot] = feat
             low = feat.astype(jnp.bfloat16)
-            kft_ref[n * 4 + sub] = low
-            kf_ref[n * 4 + sub] = jnp.transpose(low)
+            kft_ref[spot] = low
+            kf_ref[spot] = jnp.transpose(low)
     for copy in fetched:
         copy.wait()
-    listed(marks, chunks, full, corner)
+    listed(marks, chunks, offset, full, corner)
 
     def begin(tile, side, cut=False):
         raw = nn(keys_ref[tile // 4], q_turned[tile % 4])
@@ -223,14 +226,14 @@
             student = jnp.where(not_after(), student, 1.0)
         else:
             norm = jnp.sum(fold(student), 0)
-        t = fold((raw_b if side else raw_a)[...]) * scale - top[None]
+        score = fold((raw_b if side else raw_a)[...]) * scale
+        t = score - top[None]
         weight = jnp.exp2(t)
         log_student = jnp.log2(fold(student))
-        u_ref[tile] = (t - log_student).reshape(TILE, TILE)
+        u_ref[tile] = (score - log_student).reshape(TILE, TILE)
         total = jnp.sum(weight, 0)
         logs = jnp.sum(weight * log_student, 0)
-        top_ref[tile] = top
-        stripe = jnp.where(tile == spare, 4, tile % 4)
+        stripe = jnp.where(tile == SPARE, 4, tile % 4)
         old = run[0, stripe]
         new = jnp.maximum(old, top)
         left = jnp.exp2(old - new)
@@ -240,7 +243,7 @@
         run[2, stripe] = run[2, stripe] * left + logs * right
         run[3, stripe] = run[3, stripe] + norm
 
-    in_pairs(full, begin, finish, None)
+    in_groups(full, 2, begin, finish)
 
     def corner_step(n, carry):
         tile = corner[n]
@@ -276,8 +279,17 @@
 
 def second_kernel(st_ref, q_ref, qfeat_ref, qf_low, dk_in, dq_in, *refs):
     refs = list(refs)
-    groups = [[refs.pop(0) for _ in range(7)] for _ in GROUPS]
-    loss_ref, grad_ref, dk_ref, dq_ref, lines, losses, g_a, g_b = refs
+    u_ref, kfeat_ref, kft_ref, keys_ref = (refs.pop(0) for _ in range(4))
+    lists = [[refs.pop(0) for _ in range(2)] for _ in GROUPS]
+    loss_ref, grad_ref, dk_ref, dq_ref, lines, losses, g_ref, merged = refs
+    count = jnp.int32(0)
+    for chunks, (full, _) in zip(GROUPS, lists):
+        for n in range(16 * len(chunks)):
+            merged[count + n] = full[n]
+        count = count + full[LISTED - 1]
+    for n in range(WIDTH + 1):
+        merged[count + n] = SPARE
+    merged[LISTED - 1] = count
     x, y, z, c = place()
     top = st_ref[0, 0:4]
     for n in range(1, 8):
@@ -303,44 +315,34 @@
         lines[0, stripe] = jnp.broadcast_to(base[stripe : stripe + 1], (8, TILE))
         lines[1, stripe] = jnp.broadcast_to(shift[stripe : stripe + 1], (8, TILE))
 
+    def begin(tile, side, cut=False):
+        stripe = tile % 4
+        grad = lines[0, stripe][None] - jnp.exp2(fold(u_ref[tile]) - lines[1, stripe][None])
+        grad = grad.reshape(TILE, TILE)
+        if cut:
+            grad = jnp.where(not_after(), grad, 0.0)
+        g_ref[side] = grad.astype(jnp.bfloat16)
+        return 0
+
+    def finish(tile, side, ahead):
+        grad = g_ref[side]
+        stripe = jnp.where(tile == SPARE, 4, tile % 4)
+        dq_ref[stripe] += nn(kft_ref[tile // 4], grad)
+        dk_ref[tile // 4] += nt(qf_low[tile % 4], grad)
+
+    in_groups(merged, WIDTH, begin, finish)
+
+    def corner_step(corner, n, carry):
+        tile = corner[n]
+        begin(tile, 0, True)
+        finish(tile, 0, 0)
+        return carry
+
+    for _, corner in lists:
+        lax.fori_loop(0, corner[LISTED - 1], functools.partial(corner_step, corner), 0)
     gk = jnp.zeros((HEAD, HEAD), jnp.float32)
-    offset = 0
-    for chunks, group in zip(GROUPS, groups):
-        top_ref, u_ref, kfeat_ref, kft_ref, keys_ref, full, corner = group
-        spare = 16 * len(chunks)
-
-        def begin(tile, side, cut=False):
-            stripe = tile % 4
-            less = lines[1, stripe] - top_ref[tile]
-            grad = lines[0, stripe][None] - jnp.exp2(fold(u_ref[tile]) - less[None])
-            grad = grad.reshape(TILE, TILE)
-            if cut:
-                grad = jnp.where(not_after(), grad, 0.0)
-            (g_b if side else g_a)[...] = grad.astype(jnp.bfloat16)
-            return 0
-
-        def finish(tile, side, ahead):
-            grad = (g_b if side else g_a)[...]
-            key_tile = jnp.where(tile == spare, 16, offset + tile // 4)
-            stripe = jnp.where(tile == spare, 4, tile % 4)
-            dq_ref[stripe] += nn(kft_ref[tile // 4], grad)
-            dk_ref[key_tile] += nt(qf_low[tile % 4], grad)
-
-        in_pairs(full, begin, finish, None)
-
-        def corner_step(n, carry):
-            tile = corner[n]
-            begin(tile, 0, True)
-            finish(tile, 0, 0)
-            return carry
-
-        lax.fori_loop(0, corner[LISTED - 1], corner_step, 0)
-        for key_tile in range(4 * len(chunks)):
-            gk = gk + weight_grad(
-                kfeat_ref[key_tile], dk_ref[offset + key_tile], keys_ref[key_tile]
-            )
-        offset += 4 * len(chunks)
-
+    for key_tile in range(16):
+        gk = gk + weight_grad(kfeat_ref[key_tile], dk_ref[key_tile], keys_ref[key_tile])
     gq = jnp.zeros((HEAD, HEAD), jnp.float32)
     for stripe in range(4):
         gq = gq + weight_grad(
@@ -375,11 +377,10 @@
     count = len(chunks)
     outs = [
         f32(4, 5, 8, TILE),
-        f32(16 * count + 1, 8, TILE),
-        f32(16 * count + 1, TILE, TILE),
-        f32(4 * count, FEAT, TILE),
-        b16(4 * count + 1, FEAT, TILE),
-        b16(4 * count + 1, TILE, HEAD),
+        f32(SPARE + 1, TILE, TILE),
+        f32(16, FEAT, TILE),
+        b16(17, FEAT, TILE),
+        b16(17, TILE, HEAD),
         jax.ShapeDtypeStruct((LISTED,), jnp.int32),
         jax.ShapeDtypeStruct((LISTED,), jnp.int32),
     ]
@@ -398,15 +399,16 @@
         functools.partial(first_kernel, chunks),
         out_shape=tuple(outs),
         in_specs=[VMEM] * (len(loads) + 1 + len(others)),
-        out_specs=tuple(SMEM if n in (6, 7) else VMEM for n in range(len(outs))),
+        out_specs=tuple(SMEM if n in (5, 6) else VMEM for n in range(len(outs))),
         scratch_shapes=[
             pltpu.VMEM((TILE, TILE), jnp.float32),
             pltpu.VMEM((TILE, TILE), jnp.float32),
-            pltpu.VMEM((4 * count + 1, TILE, FEAT), jnp.bfloat16),
+            pltpu.VMEM((17, TILE, FEAT), jnp.bfloat16),
             pltpu.VMEM((count, MARKS, HEAD), jnp.int32),
             pltpu.SMEM((count, MARKS, HEAD), jnp.int32),
             pltpu.SemaphoreType.DMA((count,)),
         ],
+        input_output_aliases={} if 0 in chunks else {len(loads) + 4 + n: 1 + n for n in range(4)},
         name="first%d" % chunks[0],
         **params(20 * count),
     )(*loads, w_key, *others)
@@ -419,18 +421,16 @@
 def local(queries, keys, positions, tile_mask, w_query, w_key):
     hbm = pl.BlockSpec(memory_space=pltpu.HBM)
     vmem = pl.BlockSpec(memory_space=pltpu.VMEM)
-    q_own, k_copies, w_query, w_key = pl.pallas_call(
+    q_own, k_copies = pl.pallas_call(
         rotate_kernel,
-        out_shape=(
-            b16(PIECE + 16, HEAD), b16(8, PIECE, HEAD), b16(HEAD, HEAD), b16(HEAD, HEAD)
-        ),
-        in_specs=[hbm] * 6,
-        out_specs=(vmem,) * 4,
+        out_shape=(b16(PIECE + 16, HEAD), b16(8, PIECE, HEAD)),
+        in_specs=[hbm] * 4,
+        out_specs=(vmem,) * 2,
         scratch_shapes=[
             pltpu.VMEM((2, 8, PIECE), jnp.int32),
             pltpu.VMEM((2, PIECE, HEAD), jnp.bfloat16),
             pltpu.VMEM((4, 16), jnp.int32),
-            pltpu.SemaphoreType.DMA((7,)),
+            pltpu.SemaphoreType.DMA((5,)),
         ],
         compiler_params=pltpu.CompilerParams(vmem_limit_bytes=60 << 20),
         name="rotate",
@@ -439,16 +439,23 @@
         queries.reshape(PIECE, HEAD),
         keys.reshape(PIECE, HEAD),
         tile_mask,
-        w_query[0],
-        w_key[0],
     )
     k_near = exchanged(k_copies, "z").reshape(4 * TILE, HEAD)
     other = lax.ppermute(q_own, "c", [(0, 1), (1, 0)])
+    w_query, w_key = pl.pallas_call(
+        early_kernel,
+        out_shape=(b16(HEAD, HEAD), b16(HEAD, HEAD)),
+        in_specs=[VMEM] * 3,
+        out_specs=(VMEM,) * 2,
+        name="early",
+        **params(10),
+    )(other, w_query[0], w_key[0])
     pair = jnp.stack([q_own, other])
     pairs = [pair] + [
         lax.ppermute(pair, "y", [(i, (i + step) % 4) for i in range(4)]) for step in (1, 3, 2)
     ]
     marks = jnp.stack([near[:, PIECE : PIECE + 4] for near in pairs]).reshape(MARKS, HEAD)
+    marks, w_query, w_key = lax.optimization_barrier((marks, w_query, w_key))
     half = 2 * TILE
     load = jnp.concatenate([k_near[:half], marks, k_near[half:]], 0)
     after = [(i, (i + 1) % 4) for i in range(4)]
@@ -459,27 +466,31 @@
         lax.ppermute(lower[: half + MARKS], "x", after),
         lax.ppermute(upper[half + MARKS :], "x", before),
     )
-    run, *first, q_turned, qf_low, qfeat, q_rows, dk, dq = first_call(
+    run, *kept, full0, corner0, q_turned, qf_low, qfeat, q_rows, dk, dq = first_call(
         (0,), [load], w_key, w_query, *pairs
     )
-    run, *second = first_call((1, 3), [lower, upper], w_key, run, q_turned, qf_low)
-    run, *third, stats = first_call((2,), far, w_key, run, q_turned, qf_low)
+    run, *kept, full1, corner1 = first_call(
+        (1, 3), [lower, upper], w_key, run, q_turned, qf_low, *kept
+    )
+    run, *kept, full2, corner2, stats = first_call(
+        (2,), far, w_key, run, q_turned, qf_low, *kept
+    )
     stats = exchanged(stats, ("y", "c"))
     loss, grads, _, _ = pl.pallas_call(
         second_kernel,
         out_shape=(f32(1, PIECE), f32(2, HEAD, HEAD), f32(17, FEAT, TILE), f32(5, FEAT, TILE)),
-        in_specs=[VMEM] * 6 + ([VMEM] * 5 + [SMEM] * 2) * 3,
+        in_specs=[VMEM] * 10 + [SMEM] * 6,
         out_specs=(VMEM,) * 4,
         scratch_shapes=[
             pltpu.VMEM((2, 4, 8, TILE), jnp.float32),
             pltpu.VMEM((2, 4, 8, 128), jnp.float32),
-            pltpu.VMEM((TILE, TILE), jnp.bfloat16),
-            pltpu.VMEM((TILE, TILE), jnp.bfloat16),
+            pltpu.VMEM((WIDTH, TILE, TILE), jnp.bfloat16),
+            pltpu.SMEM((LISTED,), jnp.int32),
         ],
         input_output_aliases={4: 2, 5: 3},
         name="second",
         **params(100),
-    )(stats, q_rows, qfeat, qf_low, dk, dq, *first, *second, *third)
+    )(stats, q_rows, qfeat, qf_low, dk, dq, *kept, full0, corner0, full1, corner1, full2, corner2)
     wide = ("y", "x", "c")
     part = exchanged(grads.reshape(32, 8, HEAD), wide).sum(0)
     part = exchanged(jnp.broadcast_to(part, (8, 8, HEAD)), "z").sum(0)

time: 103 us -> 99.9 us (0.970)
  Pallas kernels: 20.8 us -> 19.3 us
    ppermute x3, waiting for transfers between devices: 3.08 us -> 1.44 us  [local(): lax.ppermute(pair, 'y', [(i, (i + step) % 4) for i in range(4)])]
    ppermute x1, waiting for transfers between devices: 0.01 us -> 1.43 us  [local(): lower = lax.ppermute(load, 'x', after)]
    pallas_call x1, Pallas kernels: 6.25 us -> 4.88 us  [local(): pl.pallas_call(second_kernel, out_shape=(f32(1, PIECE), f32(2, HEAD, HEAD...]
    ppermute x1, starting transfers between devices: 0.01 us -> 1.29 us  [local(): lower = lax.ppermute(load, 'x', after)]
    ppermute x1, starting transfers between devices: 2.56 us -> 1.47 us  [local(): upper = lax.ppermute(load, 'x', before)]
  transfers between devices with their start and end apart: 9 -> 9, of which waited for: 4 -> 4; matrix products, arithmetic and copies ran while one was open for 1% -> 2% of each run, Pallas kernels for 9% -> 9%
where the time goes in v4:
time: 99.9 us; the launch traced here: 99.1 us
  blocking collectives  49.2 us (49%)
  starting transfers between devices  19.7 us (20%)
  Pallas kernels  19.3 us (19%)
  waiting for transfers between devices  6.29 us (6%)
  local copies, waits for them, and re-layouts  2.24 us (2%)
  other arithmetic  1.55 us (2%)
    all_to_all x4, blocking collectives, exchanged(): return lax.all_to_all(copies, axes, split_axis=0, concat_axis=0, tiled=True)  49.2 us
    pallas_call x3, Pallas kernels, first_call(): pl.pallas_call(functools.partial(first_kernel, chunks), out_shape=tuple(o...  12.4 us
    all_to_all x1, starting transfers between devices, exchanged(): return lax.all_to_all(copies, axes, split_axis=0, concat_axis=0, tiled=True)  6.48 us
    pallas_call x1, Pallas kernels, local(): pl.pallas_call(second_kernel, out_shape=(f32(1, PIECE), f32(2, HEAD, HEAD...  4.88 us
    ppermute x3, starting transfers between devices, local(): lax.ppermute(pair, 'y', [(i, (i + step) % 4) for i in range(4)])  4.38 us
    all_to_all x1, waiting for transfers between devices, exchanged(): return lax.all_to_all(copies, axes, split_axis=0, concat_axis=0, tiled=True)  3.4 us
    ppermute x1, starting transfers between devices, local(): other = lax.ppermute(q_own, 'c', [(0, 1), (1, 0)])  3.29 us
    ppermute x1, starting transfers between devices, local(): lax.ppermute(upper[half + MARKS:], 'x', before)  2.73 us
  transfers between devices with their start and end apart: 9, of which 4 were waited for; matrix products, arithmetic and copies ran while one was open for 2% of the time, Pallas kernels for 9%

profile of v4, /device:TPU:1, one launch (start us, length us, event | category | flops | bytes accessed | tf_op | source)
XLA Modules:
  0.0 99.1 jit_solution(9896499049450757019)
XLA Ops:
  0.6 2.0 %rotate.1 = (bf16[144,128]{1,0:T(8,128)(2,1)}, bf16[8,128,128]{2,1,0:T(8,128)(2,1)}) custom-call(s32[32,8,128]{2,1,0:T(8,128)} %bitcast.33, bf16[128,128]{1,0:T(8,128)(2,1)} %bitcast.35, bf16[128,128]{1,0:T(8,128)(2,1)} %bitcast.36, s32[4,16]{1,0:T(4,128)} %mask_hbm.1), custom_call_target="tpu_custom_call" | custom-call | tf_op jit(solution)/shard_map/rotate/pallas_call | solution.py:424
  2.6 3.3 %collective-permute-start = (bf16[144,128]{1,0:T(8,128)(2,1)}, bf16[144,128]{1,0:T(8,128)(2,1)S(1)}, u32[]{:S(2)}, u32[]{:S(2)}) collective-permute-start(bf16[144,128]{1,0:T(8,128)(2,1)} %get-tuple-element.40), channel_id=1, source_target_pairs={{0,1},{1,0},{2,3},{3,2},{4,5},{5,4},{6,7},{7,6},{8,9},{9,8},{10,11... | collective-permute-start | bytes 110600 | tf_op jit(solution)/shard_map/ppermute | solution.py:444
  5.9 6.5 %all-to-all-start = ((bf16[8,128,128]{2,1,0:T(8,128)(2,1)}), bf16[8,128,128]{2,1,0:T(8,128)(2,1)S(1)}, u32[]{:S(2)}, u32[]{:S(2)}) async-start(bf16[8,128,128]{2,1,0:T(8,128)(2,1)} %get-tuple-element.39), calls=%async_computation | async-start | bytes 524288 | tf_op jit(solution)/shard_map/all_to_all | solution.py:418
  12.4 0.0 collective-permute-done.after
  12.4 0.8 pad_maximum_fusion.1.refs_3_
  13.2 2.9 %collective-permute-start.3 = (bf16[2,144,128]{2,1,0:T(8,128)(2,1)S(1)}, bf16[2,144,128]{2,1,0:T(8,128)(2,1)S(1)}, u32[]{:S(2)}, u32[]{:S(2)}) collective-permute-start(bf16[2,144,128]{2,1,0:T(8,128)(2,1)S(1)} %pad_maximum_fusion.1.refs_3_), channel_id=1, source_target_pairs={{0,128},{64,192},{128,0},{192,64},{1,129},{65,193},{129,1},{193,65... | collective-permute-start | bytes 221192 | tf_op jit(solution)/shard_map/ppermute | solution.py:455
  16.1 0.8 collective-permute-start.2
  16.9 0.7 collective-permute-start.1
  17.6 0.7 fusion.1
  18.3 0.8 copy-done
  19.0 0.8 copy-done.1
  19.8 0.1 early.1
  19.9 0.0 collective-permute-done.3.refs_6_
  19.9 0.5 collective-permute-done.2.refs_5_
  20.4 1.0 collective-permute-done.1.refs_4_
  21.4 3.4 %all-to-all-done = bf16[8,128,128]{2,1,0:T(8,128)(2,1)S(1)} async-done(((bf16[8,128,128]{2,1,0:T(8,128)(2,1)}), bf16[8,128,128]{2,1,0:T(8,128)(2,1)S(1)}, u32[]{:S(2)}, u32[]{:S(2)}) %all-to-all-start) | async-done | bytes 262176 | tf_op jit(solution)/shard_map/all_to_all | solution.py:418
  24.8 1.3 %collective-permute-start.4 = (bf16[1056,128]{1,0:T(8,128)(2,1)S(1)}, bf16[1056,128]{1,0:T(8,128)(2,1)S(1)}, u32[]{:S(2)}, u32[]{:S(2)}) collective-permute-start(bf16[1056,128]{1,0:T(8,128)(2,1)S(1)} %pad_maximum_fusion.refs_0_), channel_id=1, source_target_pairs={{0,2},{2,4},{4,6},{6,0},{1,3},{3,5},{5,7},{7,1},{8,10},{10,12},{12... | collective-permute-start | bytes 811016 | tf_op jit(solution)/shard_map/ppermute | solution.py:463
  26.1 1.5 %collective-permute-start.6 = (bf16[1056,128]{1,0:T(8,128)(2,1)S(1)}, bf16[1056,128]{1,0:T(8,128)(2,1)S(1)}, u32[]{:S(2)}, u32[]{:S(2)}) collective-permute-start(bf16[1056,128]{1,0:T(8,128)(2,1)S(1)} %pad_maximum_fusion.refs_0_), channel_id=1, source_target_pairs={{0,6},{2,0},{4,2},{6,4},{1,7},{3,1},{5,3},{7,5},{8,14},{10,8},{12,... | collective-permute-start | bytes 811016 | tf_op jit(solution)/shard_map/ppermute | solution.py:464
  27.6 4.7 %first0.1 = (f32[4,5,8,256]{3,2,1,0:T(8,128)S(1)}, f32[65,256,256]{2,1,0:T(8,128)S(1)}, f32[16,256,256]{2,1,0:T(8,128)S(1)}, bf16[17,256,256]{2,1,0:T(8,128)(2,1...) custom-call(bf16[1056,128]{1,0:T(8,128)(2,1)S(1)} %pad_maximum_fusio, ...), custom_call_target="tpu_custom_call" | custom-call | flops 2000000000 | bytes 2000000 | tf_op jit(solution)/shard_map/first0/pallas_call | solution.py:398
  32.2 1.4 %collective-permute-done.4.refs_0_ = bf16[1056,128]{1,0:T(8,128)(2,1)S(1)} collective-permute-done((bf16[1056,128]{1,0:T(8,128)(2,1)S(1)}, bf16[1056,128]{1,0:T(8,128)(2,1)S(1)}, u32[]{:S(2)}, u32[]{:S(2)}) %collective-permute-start.4) | collective-permute-done | bytes 270368 | tf_op jit(solution)/shard_map/ppermute | solution.py:463
  33.7 0.1 collective-permute-start.5
  33.8 0.0 collective-permute-done.6.refs_1_
  33.8 2.7 %collective-permute-start.7 = (bf16[512,128]{1,0:T(8,128)(2,1)S(1)}, bf16[512,128]{1,0:T(8,128)(2,1)S(1)}, u32[]{:S(2)}, u32[]{:S(2)}) collective-permute-start(bf16[512,128]{1,0:T(8,128)(2,1)S(1)} %slice.58), channel_id=1, source_target_pairs={{0,6},{2,0},{4,2},{6,4},{1,7},{3,1},{5,3},{7,5},{8,14},{10,8},{12,... | collective-permute-start | bytes 393224 | tf_op jit(solution)/shard_map/ppermute | solution.py:467
  36.5 4.3 %first1.1 = (f32[4,5,8,256]{3,2,1,0:T(8,128)S(1)}, f32[65,256,256]{2,1,0:T(8,128)S(1)}, f32[16,256,256]{2,1,0:T(8,128)S(1)}, bf16[17,256,256]{2,1,0:T(8,128)(2,1...) custom-call(bf16[1056,128]{1,0:T(8,128)(2,1)S(1)} %collective-permut, ...), custom_call_target="tpu_custom_call", output_to_operand_aliasing={{1}: (6, {}), {2}: (7, {}), {3}: (8, {}), {4}: (9, {})} | custom-call | flops 4000000000 | bytes 4000000 | tf_op jit(solution)/shard_map/first1/pallas_call | solution.py:398
  40.8 0.0 collective-permute-done.7.refs_1_
  40.9 3.4 %first2.1 = (f32[4,5,8,256]{3,2,1,0:T(8,128)}, f32[65,256,256]{2,1,0:T(8,128)S(1)}, f32[16,256,256]{2,1,0:T(8,128)S(1)}, bf16[17,256,256]{2,1,0:T(8,128)(2,1)S(1...) custom-call(bf16[544,128]{1,0:T(8,128)(2,1)S(1)} %collective-permute, ...), custom_call_target="tpu_custom_call", output_to_operand_aliasing={{1}: (6, {}), {2}: (7, {}), {3}: (8, {}), {4}: (9, {})} | custom-call | flops 2000000000 | bytes 2000000 | tf_op jit(solution)/shard_map/first2/pallas_call | solution.py:398
  44.3 11.2 %all_to_all.25.st_ref = f32[8,16,256]{2,1,0:T(8,128)S(1)} all-to-all(f32[8,16,256]{2,1,0:T(8,128)S(1)} %get-tuple-element.58), channel_id=1, replica_groups=mesh['y'=4,'z'=8,'x'=4,'c'=2] {'y','c'}, dimensions={0} | all-to-all | bytes 262144 | tf_op jit(solution)/shard_map/all_to_all | solution.py:418
  55.5 4.9 %second.1 = (f32[1,128]{1,0:T(1,128)}, f32[2,128,128]{2,1,0:T(8,128)S(1)}, f32[17,256,256]{2,1,0:T(8,128)S(1)}, f32[5,256,256]{2,1,0:T(8,128)S(1)}) custom-call(f32[8,16,256]{2,1,0:T(8,128)S(1)} %all_to_all.25.st_ref, bf16[4,2,128,128]{3,2,1,0:T(8,128)(2,1)S(1)} %get-tuple-element.59.q_ref, ...), custom_call_target="tpu_custom_call", output_to_operand_aliasing={{2}: (4, {}), {3}: (5, {})} | custom-call | flops 10000000000 | bytes 10000000 | tf_op jit(solution)/shard_map/second/pallas_call | solution.py:479
  60.4 16.2 %all_to_all.26 = f32[32,8,128]{2,1,0:T(8,128)S(1)} all-to-all(f32[32,8,128]{2,1,0:T(8,128)S(1)} %bitcast.26), channel_id=1, replica_groups=mesh['y'=4,'z'=8,'x'=4,'c'=2] {'y','x','c'}, dimensions={0} | all-to-all | bytes 262144 | tf_op jit(solution)/shard_map/all_to_all | solution.py:418
  76.6 9.3 %all_to_all.27 = f32[8,8,128]{2,1,0:T(8,128)S(1)} all-to-all(f32[8,8,128]{2,1,0:T(8,128)S(1)} %broadcast_in_dim.6), channel_id=1, replica_groups=mesh['y'=4,'z'=8,'x'=4,'c'=2] {'z'}, dimensions={0} | all-to-all | bytes 65536 | tf_op jit(solution)/shard_map/all_to_all | solution.py:418
  85.9 12.5 %all_to_all.28 = f32[32,8,128]{2,1,0:T(8,128)S(1)} all-to-all(f32[32,8,128]{2,1,0:T(8,128)S(1)} %broadcast_in_dim.7), channel_id=1, replica_groups=mesh['y'=4,'z'=8,'x'=4,'c'=2] {'y','x','c'}, dimensions={0} | all-to-all | bytes 262144 | tf_op jit(solution)/shard_map/all_to_all | solution.py:418
  98.4 0.7 slice_bitcast_fusion
  (15 shorter events, 0.2 us)
Async XLA Ops:
  2.6 9.8 %collective-permute-start = (bf16[144,128]{1,0:T(8,128)(2,1)}, bf16[144,128]{1,0:T(8,128)(2,1)S(1)}, u32[]{:S(2)}, u32[]{:S(2)}) collective-permute-start(bf16[144,128]{1,0:T(8,128)(2,1)} %get-tuple-element.40), channel_id=1, source_target_pairs={{0,1},{1,0},{2,3},{3,2},{4,5},{5,4},{6,7},{7,6},{8,9},{9,8},{10,11... | collective-permute-start | bytes 110600 | tf_op jit(solution)/shard_map/ppermute | solution.py:444
  5.9 18.8 %all-to-all-start = ((bf16[8,128,128]{2,1,0:T(8,128)(2,1)}), bf16[8,128,128]{2,1,0:T(8,128)(2,1)S(1)}, u32[]{:S(2)}, u32[]{:S(2)}) async-start(bf16[8,128,128]{2,1,0:T(8,128)(2,1)} %get-tuple-element.39), calls=%async_computation | async-start | bytes 524288 | tf_op jit(solution)/shard_map/all_to_all | solution.py:418
  13.2 6.7 %collective-permute-start.3 = (bf16[2,144,128]{2,1,0:T(8,128)(2,1)S(1)}, bf16[2,144,128]{2,1,0:T(8,128)(2,1)S(1)}, u32[]{:S(2)}, u32[]{:S(2)}) collective-permute-start(bf16[2,144,128]{2,1,0:T(8,128)(2,1)S(1)} %pad_maximum_fusion.1.refs_3_), channel_id=1, source_target_pairs={{0,128},{64,192},{128,0},{192,64},{1,129},{65,193},{129,1},{193,65... | collective-permute-start | bytes 221192 | tf_op jit(solution)/shard_map/ppermute | solution.py:455
  16.1 4.3 %collective-permute-start.2 = (bf16[2,144,128]{2,1,0:T(8,128)(2,1)S(1)}, bf16[2,144,128]{2,1,0:T(8,128)(2,1)S(1)}, u32[]{:S(2)}, u32[]{:S(2)}) collective-permute-start(bf16[2,144,128]{2,1,0:T(8,128)(2,1)S(1)} %pad_maximum_fusion.1.refs_3_), channel_id=1, source_target_pairs={{0,192},{64,0},{128,64},{192,128},{1,193},{65,1},{129,65},{193,129... | collective-permute-start | bytes 221192 | tf_op jit(solution)/shard_map/ppermute | solution.py:455
  16.9 4.5 %collective-permute-start.1 = (bf16[2,144,128]{2,1,0:T(8,128)(2,1)S(1)}, bf16[2,144,128]{2,1,0:T(8,128)(2,1)S(1)}, u32[]{:S(2)}, u32[]{:S(2)}) collective-permute-start(bf16[2,144,128]{2,1,0:T(8,128)(2,1)S(1)} %pad_maximum_fusion.1.refs_3_), channel_id=1, source_target_pairs={{0,64},{64,128},{128,192},{192,0},{1,65},{65,129},{129,193},{193,1... | collective-permute-start | bytes 221192 | tf_op jit(solution)/shard_map/ppermute | solution.py:455
  18.3 0.8 copy-start
  19.0 0.8 copy-start.1
  24.8 8.9 %collective-permute-start.4 = (bf16[1056,128]{1,0:T(8,128)(2,1)S(1)}, bf16[1056,128]{1,0:T(8,128)(2,1)S(1)}, u32[]{:S(2)}, u32[]{:S(2)}) collective-permute-start(bf16[1056,128]{1,0:T(8,128)(2,1)S(1)} %pad_maximum_fusion.refs_0_), channel_id=1, source_target_pairs={{0,2},{2,4},{4,6},{6,0},{1,3},{3,5},{5,7},{7,1},{8,10},{10,12},{12... | collective-permute-start | bytes 811016 | tf_op jit(solution)/shard_map/ppermute | solution.py:463
  26.1 7.7 %collective-permute-start.6 = (bf16[1056,128]{1,0:T(8,128)(2,1)S(1)}, bf16[1056,128]{1,0:T(8,128)(2,1)S(1)}, u32[]{:S(2)}, u32[]{:S(2)}) collective-permute-start(bf16[1056,128]{1,0:T(8,128)(2,1)S(1)} %pad_maximum_fusion.refs_0_), channel_id=1, source_target_pairs={{0,6},{2,0},{4,2},{6,4},{1,7},{3,1},{5,3},{7,5},{8,14},{10,8},{12,... | collective-permute-start | bytes 811016 | tf_op jit(solution)/shard_map/ppermute | solution.py:464
  33.7 7.2 %collective-permute-start.5 = (bf16[544,128]{1,0:T(8,128)(2,1)S(1)}, bf16[544,128]{1,0:T(8,128)(2,1)S(1)}, u32[]{:S(2)}, u32[]{:S(2)}) collective-permute-start(bf16[544,128]{1,0:T(8,128)(2,1)S(1)} %slice.57), channel_id=1, source_target_pairs={{0,2},{2,4},{4,6},{6,0},{1,3},{3,5},{5,7},{7,1},{8,10},{10,12},{12... | collective-permute-start | bytes 417800 | tf_op jit(solution)/shard_map/ppermute | solution.py:466
  33.8 7.0 %collective-permute-start.7 = (bf16[512,128]{1,0:T(8,128)(2,1)S(1)}, bf16[512,128]{1,0:T(8,128)(2,1)S(1)}, u32[]{:S(2)}, u32[]{:S(2)}) collective-permute-start(bf16[512,128]{1,0:T(8,128)(2,1)S(1)} %slice.58), channel_id=1, source_target_pairs={{0,6},{2,0},{4,2},{6,4},{1,7},{3,1},{5,3},{7,5},{8,14},{10,8},{12,... | collective-permute-start | bytes 393224 | tf_op jit(solution)/shard_map/ppermute | solution.py:467

commit v5 on v4

--- a/solution.py
+++ b/solution.py
@@ -38,6 +38,27 @@
 
 def place():
     return tuple(lax.axis_index(name) for name in ("x", "y", "z", "c"))
+
+
+def cosine_and_sine(angles):
+    turns = jnp.floor(angles * 0.6366197723675814 + 0.5)
+    rest = angles
+    for part in (1.5703125, 0.0004825592041015625, 1.2665987014770508e-06, 9.920935184482005e-10):
+        rest = rest - turns * jnp.float32(part)
+    quarter = turns.astype(jnp.int32)
+    z = rest * rest
+    sine = rest + rest * z * (
+        -1.6666654611e-1 + z * (8.3321608736e-3 + z * -1.9515295891e-4)
+    )
+    cosine = (1.0 - 0.5 * z) + z * z * (
+        4.166664568298827e-2 + z * (-1.388731625493765e-3 + z * 2.443315711809948e-5)
+    )
+    odd = (quarter & 1) == 1
+    first, second = jnp.where(odd, sine, cosine), jnp.where(odd, cosine, sine)
+    return (
+        jnp.where(((quarter + 1) & 2) == 2, -first, first),
+        jnp.where((quarter & 2) == 2, -second, second),
+    )
 
 
 def rotate_kernel(
@@ -69,7 +90,7 @@
     def turn(n):
         line = jnp.sum(jnp.where(row == pieces[n] % 8, lines_ref[n], 0), 0, keepdims=True)
         angles = line.astype(jnp.float32) * frequency
-        both = jnp.transpose(jnp.concatenate([jnp.cos(angles), jnp.sin(angles)], 0))
+        both = jnp.transpose(jnp.concatenate(cosine_and_sine(angles), 0))
         other = pltpu.roll(both, 64, 1)
         low = lax.broadcasted_iota(jnp.int32, (PIECE, HEAD), 1) < 64
         values = values_ref[n].astype(jnp.float32)
@@ -158,8 +179,8 @@
         wq_ref, *q_refs = take(5)
     else:
         old_run, q_turned, qf_low = take(3)
-        take(4)
-    run, u_ref, kfeat_ref, kft_ref, keys_ref, full, corner = take(7)
+        take(5)
+    run, u_ref, kfeat_ref, kft_ref, keys_ref, top_ref, full, corner = take(8)
     if opens:
         q_turned, qf_low, qfeat_ref, rows_ref, dk_ref, dq_ref = take(6)
     if closes:
@@ -226,11 +247,11 @@
             student = jnp.where(not_after(), student, 1.0)
         else:
             norm = jnp.sum(fold(student), 0)
-        score = fold((raw_b if side else raw_a)[...]) * scale
-        t = score - top[None]
+        t = fold((raw_b if side else raw_a)[...]) * scale - top[None]
         weight = jnp.exp2(t)
         log_student = jnp.log2(fold(student))
-        u_ref[tile] = (score - log_student).reshape(TILE, TILE)
+        u_ref[tile] = (t - log_student).reshape(TILE, TILE)
+        top_ref[tile] = top
         total = jnp.sum(weight, 0)
         logs = jnp.sum(weight * log_student, 0)
         stripe = jnp.where(tile == SPARE, 4, tile % 4)
@@ -279,7 +300,7 @@
 
 def second_kernel(st_ref, q_ref, qfeat_ref, qf_low, dk_in, dq_in, *refs):
     refs = list(refs)
-    u_ref, kfeat_ref, kft_ref, keys_ref = (refs.pop(0) for _ in range(4))
+    u_ref, kfeat_ref, kft_ref, keys_ref, top_ref = (refs.pop(0) for _ in range(5))
     lists = [[refs.pop(0) for _ in range(2)] for _ in GROUPS]
     loss_ref, grad_ref, dk_ref, dq_ref, lines, losses, g_ref, merged = refs
     count = jnp.int32(0)
@@ -317,7 +338,8 @@
 
     def begin(tile, side, cut=False):
         stripe = tile % 4
-        grad = lines[0, stripe][None] - jnp.exp2(fold(u_ref[tile]) - lines[1, stripe][None])
+        less = lines[1, stripe] - top_ref[tile]
+        grad = lines[0, stripe][None] - jnp.exp2(fold(u_ref[tile]) - less[None])
         grad = grad.reshape(TILE, TILE)
         if cut:
             grad = jnp.where(not_after(), grad, 0.0)
@@ -381,6 +403,7 @@
         f32(16, FEAT, TILE),
         b16(17, FEAT, TILE),
         b16(17, TILE, HEAD),
+        f32(SPARE + 1, 8, TILE),
         jax.ShapeDtypeStruct((LISTED,), jnp.int32),
         jax.ShapeDtypeStruct((LISTED,), jnp.int32),
     ]
@@ -399,7 +422,7 @@
         functools.partial(first_kernel, chunks),
         out_shape=tuple(outs),
         in_specs=[VMEM] * (len(loads) + 1 + len(others)),
-        out_specs=tuple(SMEM if n in (5, 6) else VMEM for n in range(len(outs))),
+        out_specs=tuple(SMEM if n in (6, 7) else VMEM for n in range(len(outs))),
         scratch_shapes=[
             pltpu.VMEM((TILE, TILE), jnp.float32),
             pltpu.VMEM((TILE, TILE), jnp.float32),
@@ -408,7 +431,7 @@
             pltpu.SMEM((count, MARKS, HEAD), jnp.int32),
             pltpu.SemaphoreType.DMA((count,)),
         ],
-        input_output_aliases={} if 0 in chunks else {len(loads) + 4 + n: 1 + n for n in range(4)},
+        input_output_aliases={} if 0 in chunks else {len(loads) + 4 + n: 1 + n for n in range(5)},
         name="first%d" % chunks[0],
         **params(20 * count),
     )(*loads, w_key, *others)
@@ -479,7 +502,7 @@
     loss, grads, _, _ = pl.pallas_call(
         second_kernel,
         out_shape=(f32(1, PIECE), f32(2, HEAD, HEAD), f32(17, FEAT, TILE), f32(5, FEAT, TILE)),
-        in_specs=[VMEM] * 10 + [SMEM] * 6,
+        in_specs=[VMEM] * 11 + [SMEM] * 6,
         out_specs=(VMEM,) * 4,
         scratch_shapes=[
             pltpu.VMEM((2, 4, 8, TILE), jnp.float32),

time: 99.9 us -> 98.7 us (0.988)
  no operation moved by 1% of the time
where the time goes in v5:
time: 98.7 us; the launch traced here: 98.3 us
  blocking collectives  48.8 us (49%)
  starting transfers between devices  19.7 us (20%)
  Pallas kernels  18.8 us (19%)
  waiting for transfers between devices  6.41 us (6%)
  local copies, waits for them, and re-layouts  2.24 us (2%)
  other arithmetic  1.55 us (2%)
    all_to_all x4, blocking collectives, exchanged(): return lax.all_to_all(copies, axes, split_axis=0, concat_axis=0, tiled=True)  48.8 us
    pallas_call x3, Pallas kernels, first_call(): pl.pallas_call(functools.partial(first_kernel, chunks), out_shape=tuple(o...  11.9 us
    all_to_all x1, starting transfers between devices, exchanged(): return lax.all_to_all(copies, axes, split_axis=0, concat_axis=0, tiled=True)  6.48 us
    pallas_call x1, Pallas kernels, local(): pl.pallas_call(second_kernel, out_shape=(f32(1, PIECE), f32(2, HEAD, HEAD...  4.96 us
    ppermute x3, starting transfers between devices, local(): lax.ppermute(pair, 'y', [(i, (i + step) % 4) for i in range(4)])  4.38 us
    all_to_all x1, waiting for transfers between devices, exchanged(): return lax.all_to_all(copies, axes, split_axis=0, concat_axis=0, tiled=True)  3.4 us
    ppermute x1, starting transfers between devices, local(): other = lax.ppermute(q_own, 'c', [(0, 1), (1, 0)])  3.29 us
    ppermute x1, starting transfers between devices, local(): lax.ppermute(upper[half + MARKS:], 'x', before)  2.73 us
  transfers between devices with their start and end apart: 9, of which 4 were waited for; matrix products, arithmetic and copies ran while one was open for 2% of the time, Pallas kernels for 9%

profile of v5, /device:TPU:1, one launch (start us, length us, event | category | flops | bytes accessed | tf_op | source)
XLA Modules:
  0.0 98.3 jit_solution(5495951250442346908)
XLA Ops:
  0.6 1.9 %rotate.1 = (bf16[144,128]{1,0:T(8,128)(2,1)}, bf16[8,128,128]{2,1,0:T(8,128)(2,1)}) custom-call(s32[32,8,128]{2,1,0:T(8,128)} %bitcast.33, bf16[128,128]{1,0:T(8,128)(2,1)} %bitcast.35, bf16[128,128]{1,0:T(8,128)(2,1)} %bitcast.36, s32[4,16]{1,0:T(4,128)} %mask_hbm.1), custom_call_target="tpu_custom_call" | custom-call | tf_op jit(solution)/shard_map/rotate/pallas_call | solution.py:447
  2.5 3.3 %collective-permute-start = (bf16[144,128]{1,0:T(8,128)(2,1)}, bf16[144,128]{1,0:T(8,128)(2,1)S(1)}, u32[]{:S(2)}, u32[]{:S(2)}) collective-permute-start(bf16[144,128]{1,0:T(8,128)(2,1)} %get-tuple-element.43), channel_id=1, source_target_pairs={{0,1},{1,0},{2,3},{3,2},{4,5},{5,4},{6,7},{7,6},{8,9},{9,8},{10,11... | collective-permute-start | bytes 110600 | tf_op jit(solution)/shard_map/ppermute | solution.py:467
  5.8 6.5 %all-to-all-start = ((bf16[8,128,128]{2,1,0:T(8,128)(2,1)}), bf16[8,128,128]{2,1,0:T(8,128)(2,1)S(1)}, u32[]{:S(2)}, u32[]{:S(2)}) async-start(bf16[8,128,128]{2,1,0:T(8,128)(2,1)} %get-tuple-element.42), calls=%async_computation | async-start | bytes 524288 | tf_op jit(solution)/shard_map/all_to_all | solution.py:441
  12.3 0.0 collective-permute-done.after
  12.3 0.8 pad_maximum_fusion.1.refs_3_
  13.0 2.9 %collective-permute-start.3 = (bf16[2,144,128]{2,1,0:T(8,128)(2,1)S(1)}, bf16[2,144,128]{2,1,0:T(8,128)(2,1)S(1)}, u32[]{:S(2)}, u32[]{:S(2)}) collective-permute-start(bf16[2,144,128]{2,1,0:T(8,128)(2,1)S(1)} %pad_maximum_fusion.1.refs_3_), channel_id=1, source_target_pairs={{0,128},{64,192},{128,0},{192,64},{1,129},{65,193},{129,1},{193,65... | collective-permute-start | bytes 221192 | tf_op jit(solution)/shard_map/ppermute | solution.py:478
  16.0 0.8 collective-permute-start.2
  16.7 0.7 collective-permute-start.1
  17.4 0.7 fusion.1
  18.1 0.8 copy-done
  18.9 0.8 copy-done.1
  19.6 0.1 early.1
  19.8 0.5 collective-permute-done.2.refs_5_
  20.2 1.0 collective-permute-done.1.refs_4_
  21.2 3.4 %all-to-all-done = bf16[8,128,128]{2,1,0:T(8,128)(2,1)S(1)} async-done(((bf16[8,128,128]{2,1,0:T(8,128)(2,1)}), bf16[8,128,128]{2,1,0:T(8,128)(2,1)S(1)}, u32[]{:S(2)}, u32[]{:S(2)}) %all-to-all-start) | async-done | bytes 262176 | tf_op jit(solution)/shard_map/all_to_all | solution.py:441
  24.7 1.3 %collective-permute-start.4 = (bf16[1056,128]{1,0:T(8,128)(2,1)S(1)}, bf16[1056,128]{1,0:T(8,128)(2,1)S(1)}, u32[]{:S(2)}, u32[]{:S(2)}) collective-permute-start(bf16[1056,128]{1,0:T(8,128)(2,1)S(1)} %pad_maximum_fusion.refs_0_), channel_id=1, source_target_pairs={{0,2},{2,4},{4,6},{6,0},{1,3},{3,5},{5,7},{7,1},{8,10},{10,12},{12... | collective-permute-start | bytes 811016 | tf_op jit(solution)/shard_map/ppermute | solution.py:486
  26.0 1.5 %collective-permute-start.6 = (bf16[1056,128]{1,0:T(8,128)(2,1)S(1)}, bf16[1056,128]{1,0:T(8,128)(2,1)S(1)}, u32[]{:S(2)}, u32[]{:S(2)}) collective-permute-start(bf16[1056,128]{1,0:T(8,128)(2,1)S(1)} %pad_maximum_fusion.refs_0_), channel_id=1, source_target_pairs={{0,6},{2,0},{4,2},{6,4},{1,7},{3,1},{5,3},{7,5},{8,14},{10,8},{12,... | collective-permute-start | bytes 811016 | tf_op jit(solution)/shard_map/ppermute | solution.py:487
  27.4 4.5 %first0.1 = (f32[4,5,8,256]{3,2,1,0:T(8,128)S(1)}, f32[65,256,256]{2,1,0:T(8,128)S(1)}, f32[16,256,256]{2,1,0:T(8,128)S(1)}, bf16[17,256,256]{2,1,0:T(8,128)(2,1...) custom-call(bf16[1056,128]{1,0:T(8,128)(2,1)S(1)} %pad_maximum_fusio, ...), custom_call_target="tpu_custom_call" | custom-call | flops 2000000000 | bytes 2000000 | tf_op jit(solution)/shard_map/first0/pallas_call | solution.py:421
  32.0 1.6 %collective-permute-done.4.refs_0_ = bf16[1056,128]{1,0:T(8,128)(2,1)S(1)} collective-permute-done((bf16[1056,128]{1,0:T(8,128)(2,1)S(1)}, bf16[1056,128]{1,0:T(8,128)(2,1)S(1)}, u32[]{:S(2)}, u32[]{:S(2)}) %collective-permute-start.4) | collective-permute-done | bytes 270368 | tf_op jit(solution)/shard_map/ppermute | solution.py:486
  33.6 0.1 collective-permute-start.5
  33.6 0.0 collective-permute-done.6.refs_1_
  33.7 2.7 %collective-permute-start.7 = (bf16[512,128]{1,0:T(8,128)(2,1)S(1)}, bf16[512,128]{1,0:T(8,128)(2,1)S(1)}, u32[]{:S(2)}, u32[]{:S(2)}) collective-permute-start(bf16[512,128]{1,0:T(8,128)(2,1)S(1)} %slice.58), channel_id=1, source_target_pairs={{0,6},{2,0},{4,2},{6,4},{1,7},{3,1},{5,3},{7,5},{8,14},{10,8},{12,... | collective-permute-start | bytes 393224 | tf_op jit(solution)/shard_map/ppermute | solution.py:490
  36.4 4.2 %first1.1 = (f32[4,5,8,256]{3,2,1,0:T(8,128)S(1)}, f32[65,256,256]{2,1,0:T(8,128)S(1)}, f32[16,256,256]{2,1,0:T(8,128)S(1)}, bf16[17,256,256]{2,1,0:T(8,128)(2,1...) custom-call(bf16[1056,128]{1,0:T(8,128)(2,1)S(1)} %collective-permut, ...), custom_call_target="tpu_custom_call", output_to_operand_aliasing={{1}: (6, {}), {2}: (7, {}), {3}: (8, {}), {4}: (9, {}), {5}... | custom-call | flops 4000000000 | bytes 4000000 | tf_op jit(solution)/shard_map/first1/pallas_call | solution.py:421
  40.6 0.0 collective-permute-done.7.refs_1_
  40.6 0.0 collective-permute-done.5.refs_0_
  40.6 3.2 %first2.1 = (f32[4,5,8,256]{3,2,1,0:T(8,128)}, f32[65,256,256]{2,1,0:T(8,128)S(1)}, f32[16,256,256]{2,1,0:T(8,128)S(1)}, bf16[17,256,256]{2,1,0:T(8,128)(2,1)S(1...) custom-call(bf16[544,128]{1,0:T(8,128)(2,1)S(1)} %collective-permute, ...), custom_call_target="tpu_custom_call", output_to_operand_aliasing={{1}: (6, {}), {2}: (7, {}), {3}: (8, {}), {4}: (9, {}), {5}... | custom-call | flops 2000000000 | bytes 2000000 | tf_op jit(solution)/shard_map/first2/pallas_call | solution.py:421
  43.8 11.2 %all_to_all.25.st_ref = f32[8,16,256]{2,1,0:T(8,128)S(1)} all-to-all(f32[8,16,256]{2,1,0:T(8,128)S(1)} %get-tuple-element.63), channel_id=1, replica_groups=mesh['y'=4,'z'=8,'x'=4,'c'=2] {'y','c'}, dimensions={0} | all-to-all | bytes 262144 | tf_op jit(solution)/shard_map/all_to_all | solution.py:441
  55.0 5.0 %second.1 = (f32[1,128]{1,0:T(1,128)}, f32[2,128,128]{2,1,0:T(8,128)S(1)}, f32[17,256,256]{2,1,0:T(8,128)S(1)}, f32[5,256,256]{2,1,0:T(8,128)S(1)}) custom-call(f32[8,16,256]{2,1,0:T(8,128)S(1)} %all_to_all.25.st_ref, bf16[4,2,128,128]{3,2,1,0:T(8,128)(2,1)S(1)} %get-tuple-element.64.q_ref, ...), custom_call_target="tpu_custom_call", output_to_operand_aliasing={{2}: (4, {}), {3}: (5, {})} | custom-call | flops 10000000000 | bytes 10000000 | tf_op jit(solution)/shard_map/second/pallas_call | solution.py:502
  60.0 14.3 %all_to_all.26 = f32[32,8,128]{2,1,0:T(8,128)S(1)} all-to-all(f32[32,8,128]{2,1,0:T(8,128)S(1)} %bitcast.26), channel_id=1, replica_groups=mesh['y'=4,'z'=8,'x'=4,'c'=2] {'y','x','c'}, dimensions={0} | all-to-all | bytes 262144 | tf_op jit(solution)/shard_map/all_to_all | solution.py:441
  74.3 10.7 %all_to_all.27 = f32[8,8,128]{2,1,0:T(8,128)S(1)} all-to-all(f32[8,8,128]{2,1,0:T(8,128)S(1)} %broadcast_in_dim.6), channel_id=1, replica_groups=mesh['y'=4,'z'=8,'x'=4,'c'=2] {'z'}, dimensions={0} | all-to-all | bytes 65536 | tf_op jit(solution)/shard_map/all_to_all | solution.py:441
  85.1 12.6 %all_to_all.28 = f32[32,8,128]{2,1,0:T(8,128)S(1)} all-to-all(f32[32,8,128]{2,1,0:T(8,128)S(1)} %broadcast_in_dim.7), channel_id=1, replica_groups=mesh['y'=4,'z'=8,'x'=4,'c'=2] {'y','x','c'}, dimensions={0} | all-to-all | bytes 262144 | tf_op jit(solution)/shard_map/all_to_all | solution.py:441
  97.7 0.7 slice_bitcast_fusion
  (15 shorter events, 0.2 us)
Async XLA Ops:
  2.5 9.8 %collective-permute-start = (bf16[144,128]{1,0:T(8,128)(2,1)}, bf16[144,128]{1,0:T(8,128)(2,1)S(1)}, u32[]{:S(2)}, u32[]{:S(2)}) collective-permute-start(bf16[144,128]{1,0:T(8,128)(2,1)} %get-tuple-element.43), channel_id=1, source_target_pairs={{0,1},{1,0},{2,3},{3,2},{4,5},{5,4},{6,7},{7,6},{8,9},{9,8},{10,11... | collective-permute-start | bytes 110600 | tf_op jit(solution)/shard_map/ppermute | solution.py:467
  5.8 18.8 %all-to-all-start = ((bf16[8,128,128]{2,1,0:T(8,128)(2,1)}), bf16[8,128,128]{2,1,0:T(8,128)(2,1)S(1)}, u32[]{:S(2)}, u32[]{:S(2)}) async-start(bf16[8,128,128]{2,1,0:T(8,128)(2,1)} %get-tuple-element.42), calls=%async_computation | async-start | bytes 524288 | tf_op jit(solution)/shard_map/all_to_all | solution.py:441
  13.0 6.7 %collective-permute-start.3 = (bf16[2,144,128]{2,1,0:T(8,128)(2,1)S(1)}, bf16[2,144,128]{2,1,0:T(8,128)(2,1)S(1)}, u32[]{:S(2)}, u32[]{:S(2)}) collective-permute-start(bf16[2,144,128]{2,1,0:T(8,128)(2,1)S(1)} %pad_maximum_fusion.1.refs_3_), channel_id=1, source_target_pairs={{0,128},{64,192},{128,0},{192,64},{1,129},{65,193},{129,1},{193,65... | collective-permute-start | bytes 221192 | tf_op jit(solution)/shard_map/ppermute | solution.py:478
  16.0 4.3 %collective-permute-start.2 = (bf16[2,144,128]{2,1,0:T(8,128)(2,1)S(1)}, bf16[2,144,128]{2,1,0:T(8,128)(2,1)S(1)}, u32[]{:S(2)}, u32[]{:S(2)}) collective-permute-start(bf16[2,144,128]{2,1,0:T(8,128)(2,1)S(1)} %pad_maximum_fusion.1.refs_3_), channel_id=1, source_target_pairs={{0,192},{64,0},{128,64},{192,128},{1,193},{65,1},{129,65},{193,129... | collective-permute-start | bytes 221192 | tf_op jit(solution)/shard_map/ppermute | solution.py:478
  16.7 4.5 %collective-permute-start.1 = (bf16[2,144,128]{2,1,0:T(8,128)(2,1)S(1)}, bf16[2,144,128]{2,1,0:T(8,128)(2,1)S(1)}, u32[]{:S(2)}, u32[]{:S(2)}) collective-permute-start(bf16[2,144,128]{2,1,0:T(8,128)(2,1)S(1)} %pad_maximum_fusion.1.refs_3_), channel_id=1, source_target_pairs={{0,64},{64,128},{128,192},{192,0},{1,65},{65,129},{129,193},{193,1... | collective-permute-start | bytes 221192 | tf_op jit(solution)/shard_map/ppermute | solution.py:478
  18.1 0.8 copy-start
  18.9 0.8 copy-start.1
  24.7 8.9 %collective-permute-start.4 = (bf16[1056,128]{1,0:T(8,128)(2,1)S(1)}, bf16[1056,128]{1,0:T(8,128)(2,1)S(1)}, u32[]{:S(2)}, u32[]{:S(2)}) collective-permute-start(bf16[1056,128]{1,0:T(8,128)(2,1)S(1)} %pad_maximum_fusion.refs_0_), channel_id=1, source_target_pairs={{0,2},{2,4},{4,6},{6,0},{1,3},{3,5},{5,7},{7,1},{8,10},{10,12},{12... | collective-permute-start | bytes 811016 | tf_op jit(solution)/shard_map/ppermute | solution.py:486
  26.0 7.7 %collective-permute-start.6 = (bf16[1056,128]{1,0:T(8,128)(2,1)S(1)}, bf16[1056,128]{1,0:T(8,128)(2,1)S(1)}, u32[]{:S(2)}, u32[]{:S(2)}) collective-permute-start(bf16[1056,128]{1,0:T(8,128)(2,1)S(1)} %pad_maximum_fusion.refs_0_), channel_id=1, source_target_pairs={{0,6},{2,0},{4,2},{6,4},{1,7},{3,1},{5,3},{7,5},{8,14},{10,8},{12,... | collective-permute-start | bytes 811016 | tf_op jit(solution)/shard_map/ppermute | solution.py:487
  33.6 7.1 %collective-permute-start.5 = (bf16[544,128]{1,0:T(8,128)(2,1)S(1)}, bf16[544,128]{1,0:T(8,128)(2,1)S(1)}, u32[]{:S(2)}, u32[]{:S(2)}) collective-permute-start(bf16[544,128]{1,0:T(8,128)(2,1)S(1)} %slice.57), channel_id=1, source_target_pairs={{0,2},{2,4},{4,6},{6,0},{1,3},{3,5},{5,7},{7,1},{8,10},{10,12},{12... | collective-permute-start | bytes 417800 | tf_op jit(solution)/shard_map/ppermute | solution.py:489
  33.7 7.0 %collective-permute-start.7 = (bf16[512,128]{1,0:T(8,128)(2,1)S(1)}, bf16[512,128]{1,0:T(8,128)(2,1)S(1)}, u32[]{:S(2)}, u32[]{:S(2)}) collective-permute-start(bf16[512,128]{1,0:T(8,128)(2,1)S(1)} %slice.58), channel_id=1, source_target_pairs={{0,6},{2,0},{4,2},{6,4},{1,7},{3,1},{5,3},{7,5},{8,14},{10,8},{12,... | collective-permute-start | bytes 393224 | tf_op jit(solution)/shard_map/ppermute | solution.py:490
